TPU v7x, 32 devices: a whole 2x2x4 slice. The times are simulated.
32 devices in a mesh: row: 8 (over z, x), col: 4 (over y, core).
Axes of the slice: x: 2, y: 2, z: 4, core: 2. Of those that a mesh axis runs over, the one named last changes fastest.
Arguments:
- krylov_block: bfloat16 [64, 16384], P(None, ('row', 'col')), may hold values from -54 to 54
- degree: int32 [16384], P(('row', 'col')), may hold values from 16 to 64
- tile_values: bfloat16 [256, 4, 64, 512], P('row', 'col'), may hold values from -6 to 6
- tile_column: int32 [256, 4, 8], P('row', 'col'), may hold values from 0 to 63
- tile_live: int32 [256, 4, 8], P('row', 'col'), may hold values 0 or 1
Outputs:
- orthonormal: float32 [64, 16384], P(None, ('row', 'col'))
- quotient: float32 [64, 64], replicated
All inputs are finite; a program needn't handle non-finite values. No bound on the sum of `tile_live` on one device may be relied on, other than what follows from the above.
Results may differ from a plain program's by a relative error of at most 0.0032.
Values may be sent and summed in bfloat16 or wider, within the bound.
No kernel may reach another device: no remote copies, remote signals or barrier semaphores. Data moves between devices by JAX's collectives and lax.ppermute only.
A program may use at most 128 MiB of HBM per device.

v0:
```python
import math

import jax
import jax.numpy as jnp
from jax import lax
from jax.sharding import PartitionSpec as P


def gram_of(left, right):
    return lax.dot_general(
        left,
        right,
        (((1,), (1,)), ((), ())),
        precision=lax.Precision.HIGHEST,
        preferred_element_type=jnp.float32,
    )


def on_device(krylov_block, degree, tile_values, tile_column, tile_live):
    vectors = krylov_block.shape[0]
    owned_rows = krylov_block.shape[1]
    block_rows = tile_values.shape[0]
    height = tile_values.shape[2]
    slot_width = tile_values.shape[3]
    sources = lax.axis_size("row")
    groups = lax.axis_size("col")
    per_piece = owned_rows // height
    inv_root = lax.rsqrt(degree.astype(jnp.float32))
    basis_wide = krylov_block.astype(jnp.float32)
    scaled = (basis_wide * inv_root[None, :]).astype(jnp.bfloat16)
    gathered = lax.all_gather(scaled, "row", axis=1, tiled=True)
    blocks = gathered.reshape(vectors, sources * per_piece, height)
    pick_index = tile_column[:, 0, :].reshape(-1)
    chosen = jnp.take(blocks, pick_index, axis=1)
    chosen = chosen * tile_live[:, 0, :].reshape(1, -1, 1).astype(jnp.bfloat16)
    chosen = chosen.reshape(vectors, block_rows, slot_width)
    panel = tile_values[:, 0]
    whole_rows = jnp.einsum("klc,luc->klu", chosen, panel, preferred_element_type=jnp.float32)
    whole_rows = whole_rows.reshape(vectors, block_rows * height)
    spread = lax.psum_scatter(whole_rows, "col", scatter_dimension=1, tiled=True)
    applied = basis_wide - inv_root[None, :] * spread
    quotient, energy = lax.psum(
        (gram_of(basis_wide, applied), gram_of(applied, applied)), ("row", "col")
    )
    factor = jnp.linalg.cholesky(energy)
    identity = jnp.eye(vectors, dtype=jnp.float32)
    inverse = lax.linalg.triangular_solve(factor, identity, left_side=True, lower=True)
    total_rows = sources * groups * owned_rows
    orthonormal = jnp.dot(inverse, applied, precision=lax.Precision.HIGHEST) * math.sqrt(total_rows)
    return (orthonormal, quotient / total_rows)


def solution(mesh):
    return jax.shard_map(
        on_device,
        mesh=mesh,
        in_specs=(
            P(None, ("row", "col")),
            P(("row", "col")),
            P("row", "col", None, None),
            P("row", "col", None),
            P("row", "col", None),
        ),
        out_specs=(P(None, ("row", "col")), P()),
        check_vma=False,
    )
```

profile of v0, /device:TPU:0, one launch (start us, length us, event | category | flops | bytes accessed | tf_op | source)
XLA Modules:
  0.0 156.6 jit_solution(8631686106743871151)
XLA Ops:
  7.2 0.0 copy-start
  7.2 0.0 reduce-scatter.2.cloned.1.call-start
  7.2 0.9 copy.22
  8.1 0.7 compare_and_fusion
  8.8 0.7 convert_rsqrt_fusion
  9.5 0.9 fusion.8
  10.4 33.0 %all_gather.3 = bf16[64,4096]{1,0:T(8,128)(2,1)S(1)} all-gather(bf16[64,512]{1,0:T(8,128)(2,1)S(1)} %fusion.8), channel_id=1, replica_groups=mesh['row'=8,'col'=4] {'row'}, dimensions={1}, use_global_device_ids=true | all-gather | bytes 589824 | tf_op jit(solution)/shard_map/all_gather | solution.py:31
  43.4 2.1 %reshape.72 = bf16[64,64,64]{2,1,0:T(8,128)(2,1)} reshape(bf16[64,4096]{1,0:T(8,128)(2,1)S(1)} %all_gather.3) | data formatting | bytes 1048576 | tf_op jit(solution)/shard_map/reshape | solution.py:32
  45.5 1.9 %copy.23 = bf16[64,64,64]{2,0,1:T(8,128)(2,1)S(1)} copy(bf16[64,64,64]{2,1,0:T(8,128)(2,1)} %reshape.72) | data formatting | bytes 1048576 | tf_op jit(solution)/shard_map/reshape | solution.py:32
  47.4 0.1 reshape_squeeze.7
  47.5 3.1 %gather_fusion = bf16[256,64,64]{2,1,0:T(8,128)(2,1)} fusion(bf16[64,64,64]{2,0,1:T(8,128)(2,1)S(1)} %copy.23, s32[1024]{0:T(1024)S(1)} %pad_clamp_fusion), kind=kCustom, calls=%fused_computation | custom fusion | bytes 4195328 | tf_op jit(solution)/shard_map/jit(_take)/gather | solution.py:34
  50.6 6.8 %copy.24 = bf16[64,256,64]{2,1,0:T(8,128)(2,1)} copy(bf16[64,256,64]{2,0,1:T(8,128)(2,1)} %bitcast.30) | data formatting | bytes 4194304 | tf_op jit(solution)/shard_map/jit(_take)/gather | solution.py:34
  57.4 0.0 copy-start.2
  57.4 6.5 %gather.7 = bf16[64,32,512]{2,1,0:T(8,128)(2,1)} reshape(bf16[64,256,64]{2,1,0:T(8,128)(2,1)} %copy.24) | data formatting | bytes 4194304 | tf_op jit(solution)/shard_map/jit(_take)/gather | solution.py:34
  63.9 0.0 copy-done.2
  63.9 0.1 copy.25
  64.0 0.1 mul.35
  64.1 0.1 mul.36
  64.2 0.1 copy.21
  64.3 0.1 broadcast_in_dim.18
  64.4 0.1 broadcast_in_dim.19
  64.5 1.8 %select_multiply_fusion = bf16[64,32,512]{2,1,0:T(8,128)(2,1)S(1)} fusion(bf16[64,32,512]{2,1,0:T(8,128)(2,1)} %gather.7, pred[32,512]{1,0:T(8,128)(4,1)S(1)} %broadcast_in_dim.19, bf16[32,512]{1,0:T(8,128)(2,1)S(1)} %mul.36), kind=kLoop, calls=%fused_computation.4 | loop fusion | flops 2097152 | bytes 4243456 | tf_op jit(solution)/shard_map/mul | solution.py:35
  66.3 0.0 copy-done
  66.3 1.4 fusion.3
  67.7 0.0 copy-start.1
  67.7 0.6 copy.27
  68.4 1.1 reshape.73
  69.5 0.0 reduce-scatter.2.cloned.1.call-update
  69.5 22.9 %reduce-scatter.2.cloned.1.call-done = f32[64,512]{1,0:T(8,128)} async-done(((f32[64,2048]{1,0:T(8,128)}), f32[64,512]{1,0:T(8,128)}) %reduce-scatter.2.cloned.1.call-update) | async-done | bytes 131088 | tf_op jit(solution)/shard_map/reduce_scatter | solution.py:40
  92.5 0.0 copy-done.1
  92.5 1.1 convolution_bitcast_fusion
  93.6 1.3 fusion.9
  94.8 40.0 %all-reduce = (f32[64,64]{0,1:T(8,128)S(1)}, f32[64,64]{0,1:T(8,128)S(1)}) all-reduce(f32[64,64]{0,1:T(8,128)S(1)} %fusion.9, f32[64,64]{0,1:T(8,128)S(1)} %convolution_bitcast_fusion), channel_id=1, replica_groups=mesh['row'=8,'col'=4] {'row','col'}, use_global_device_ids=true, to_apply=%region_1.2 | all-reduce | flops 8192 | bytes 65536 | tf_op jit(solution)/shard_map/psum | solution.py:42
  134.8 0.1 copy.29
  134.9 5.8 %cholesky.17 = f32[64,64]{1,0:T(8,128)S(1)} custom-call(f32[64,64]{1,0:T(8,128)S(1)} %fusion.16), custom_call_target="Cholesky" | custom-call | tf_op jit(solution)/shard_map/jit(cholesky)/cholesky | solution.py:45
  140.8 0.6 compare_reduce_fusion
  141.4 0.7 fusion.13
  142.1 4.9 %custom-call.6 = f32[1,64,64]{1,2,0:T(8,128)S(1)} custom-call(f32[1,64,64]{2,1,0:T(8,128)S(1)} %fusion.13), custom_call_target="InvertDiagBlocksLowerTriangular" | custom-call | tf_op jit(solution)/shard_map/triangular_solve | solution.py:47
  147.0 0.2 fusion.14
  147.3 0.7 copy.30
  148.0 1.8 %convolution_multiply_fusion = f32[64,512]{1,0:T(8,128)} fusion(f32[64,64]{1,0:T(8,128)S(1)} %fusion.14, bf16[64,512]{1,0:T(8,128)(2,1)S(1)} %copy-done.1, f32[64,512]{1,0:T(8,128)} %reduce-scatter.2.cloned.1.call-done, f32[512]{0:T(512)S(1)} %convert_rsqrt_fusion), kind=kOutput, calls=%fused_computation.6 | convolution fusion | flops 25296896 | bytes 346112 | tf_op jit(solution)/shard_map/dot_general | solution.py:49
  (6 shorter events, 0.1 us)
Async XLA Ops:
  7.2 59.1 %copy-start = (bf16[32,1,64,512]{3,2,1,0:T(8,128)(2,1)S(1)}, bf16[32,1,64,512]{3,2,1,0:T(8,128)(2,1)}, u32[]{:S(2)}) copy-start(bf16[32,1,64,512]{3,2,1,0:T(8,128)(2,1)} %param.7) | copy-start | bytes 6291460
  7.2 85.3 %reduce-scatter.2.cloned.1.call-start = ((), (), s32[]{:S(2)}) async-start(), calls=%async_computation.1 | async-start | bytes 655360 | tf_op jit(solution)/shard_map/reduce_scatter | solution.py:40
  57.4 6.5 %copy-start.2 = (s32[32,1,8]{0,2,1:T(8,128)S(1)}, s32[32,1,8]{0,2,1:T(8,128)}, u32[]{:S(2)}) copy-start(s32[32,1,8]{0,2,1:T(8,128)} %param.9) | copy-start | bytes 3076
  67.7 24.7 %copy-start.1 = (bf16[64,512]{1,0:T(8,128)(2,1)S(1)}, bf16[64,512]{1,0:T(8,128)(2,1)}, u32[]{:S(2)}) copy-start(bf16[64,512]{1,0:T(8,128)(2,1)} %param.5) | copy-start | bytes 196612
Sparse Core Ops, SparseCore 0:
  69.7 22.7 reduce-scatter.1
where the time goes:
time: 157 us
  blocking collectives  73 us (46%)
  local copies, waits for them, and re-layouts  24.5 us (16%)
  waiting for transfers between devices  22.9 us (15%)
  other arithmetic  16.1 us (10%)
  between operations  14.1 us (9%)
  matrix products  5.85 us (4%)
    psum x1, blocking collectives, on_device(): lax.psum((gram_of(basis_wide, applied), gram_of(applied, applied)), ('row...  40 us
    all_gather x1, blocking collectives, on_device(): gathered = lax.all_gather(scaled, 'row', axis=1, tiled=True)  33 us
    reduce_scatter x1, waiting for transfers between devices, on_device(): lax.psum_scatter(whole_rows, 'col', scatter_dimension=1, tiled=True)  22.9 us
    gather x3, local copies, waits for them, and re-layouts, on_device(): chosen = jnp.take(blocks, pick_index, axis=1)  16.3 us
    another operation x3, other arithmetic, on_device(): factor = jnp.linalg.cholesky(energy)  6.52 us
    another operation x2, other arithmetic, on_device(): lax.linalg.triangular_solve(factor, identity, left_side=True, lower=True)  5.55 us
    reshape x2, local copies, waits for them, and re-layouts, on_device(): blocks = gathered.reshape(vectors, sources * per_piece, height)  4.01 us
  transfers between devices with their start and end apart: 1, of which 1 were waited for; matrix products, arithmetic and copies ran while one was open for 0% of the time, Pallas kernels for 0%

commit v1 on v0

v1 whole, which is shorter than its diff:
```python
import math

import jax
import jax.numpy as jnp
from jax import lax
from jax.experimental import pallas as pl
from jax.experimental.pallas import tpu as pltpu
from jax.sharding import PartitionSpec as P

F32 = jnp.float32
BF16 = jnp.bfloat16


def vmem():
    return pl.BlockSpec(memory_space=pltpu.VMEM)


def smem():
    return pl.BlockSpec(memory_space=pltpu.SMEM)


def swap(value, axis, size, mask):
    return lax.ppermute(value, axis, [(i, i ^ mask) for i in range(size)])


def bits(size):
    out = []
    mask = 1
    while mask < size:
        out.append(mask)
        mask *= 2
    return out


def split3(value):
    high = value.astype(BF16)
    rest = value - high.astype(F32)
    mid = rest.astype(BF16)
    low = (rest - mid.astype(F32)).astype(BF16)
    return high, mid, low


def scale_kernel(basis_ref, degree_ref, left_ref, right_ref):
    half = left_ref.shape[1]
    inv_root = lax.rsqrt(degree_ref[...].astype(F32))
    scaled = (basis_ref[...].astype(F32) * inv_root).astype(BF16)
    left_ref[...] = scaled[:, :half]
    right_ref[...] = scaled[:, half:]


def tile_kernel(sources, groups, per_piece, left_order, right_order, column_ref, live_ref, left_ref, right_ref,
                panel_ref, keep_ref, send_ref, table_ref, lhs_ref):
    vectors = left_ref.shape[1]
    half = left_ref.shape[2]
    height = panel_ref.shape[1]
    slots = column_ref.shape[1]
    wide = 2 * height
    pairs = half // wide
    my_row = lax.axis_index("row")
    my_col = lax.axis_index("col")
    zero_at = sources * per_piece
    for side, order, ref in ((0, left_order, left_ref), (1, right_order, right_ref)):
        for at in range(sources):
            for pair in range(pairs):
                tile = ref[at, :, pair * wide:(pair + 1) * wide]
                block = order[at] * per_piece + 2 * (side * pairs + pair)
                table_ref[block] = tile
                table_ref[block + 1] = jnp.concatenate([tile[:, height:], tile[:, :height]], axis=1)
    table_ref[zero_at] = jnp.zeros((vectors, wide), BF16)
    lane = lax.broadcasted_iota(jnp.int32, (vectors, wide), 1)
    is_low = lane < height
    turn = my_row * per_piece
    pack = 4
    chunks = per_piece // pack

    def group(piece_at, chunk, slot_of):
        row0 = (piece_at ^ my_col) * per_piece + chunk * pack
        for inner in range(pack):
            row = row0 + inner
            for pair in range(slots // 2):
                first = column_ref[row, 2 * pair] ^ turn
                second = column_ref[row, 2 * pair + 1] ^ turn ^ 1
                first = jnp.where(live_ref[row, 2 * pair] == 1, first, zero_at)
                second = jnp.where(live_ref[row, 2 * pair + 1] == 1, second, zero_at)
                lhs_ref[slot_of, inner * vectors:(inner + 1) * vectors, pair * wide:(pair + 1) * wide] = jnp.where(
                    is_low, table_ref[first], table_ref[second])
        rhs = panel_ref[pl.ds(row0, pack)].reshape(pack * height, slots * height)
        prod = lax.dot_general(lhs_ref[slot_of], rhs, (((1,), (1,)), ((), ())), preferred_element_type=F32)
        out = []
        for pair in range(pack // 2):
            lanes = slice(pair * wide, (pair + 1) * wide)
            top = prod[2 * pair * vectors:(2 * pair + 1) * vectors, lanes]
            low = prod[(2 * pair + 1) * vectors:(2 * pair + 2) * vectors, lanes]
            out.append(jnp.where(is_low, top, low))
        return jnp.concatenate(out, axis=1)

    span = pack * height
    if groups <= 4:
        at = 0
        for piece in [s for s in range(groups) if s % 2] + [s for s in range(groups) if s % 2 == 0]:
            for chunk in range(chunks):
                value = group(piece, chunk, at % 2)
                at += 1
                lanes = slice(chunk * span, (chunk + 1) * span)
                if piece % 2:
                    send_ref[piece // 2, :, lanes] = value.astype(BF16)
                else:
                    keep_ref[piece // 2, :, lanes] = value
    else:
        def body(step, carry):
            for chunk in range(chunks):
                lanes = slice(chunk * span, (chunk + 1) * span)
                send_ref[step, :, lanes] = group(2 * step + 1, chunk, 0).astype(BF16)
                keep_ref[step, :, lanes] = group(2 * step, chunk, 1)
            return carry

        lax.fori_loop(0, groups // 2, body, 0)


def gram_kernel(received, basis_ref, degree_ref, keep_ref, *refs):
    parts = refs[:received]
    split_ref, gram_ref, stack_ref = refs[received:]
    vectors = basis_ref.shape[0]
    spread = keep_ref[0]
    for ref in parts:
        spread = spread + ref[0].astype(F32)
    basis = basis_ref[...]
    inv_root = lax.rsqrt(degree_ref[...].astype(F32))
    applied = basis.astype(F32) - inv_root * spread
    for at, piece in enumerate(split3(applied)):
        split_ref[at * vectors:(at + 1) * vectors, :] = piece
        stack_ref[at * vectors:(at + 1) * vectors, :] = piece
    stack_ref[3 * vectors:4 * vectors, :] = basis
    stack = stack_ref[...]
    prod = lax.dot_general(stack, stack, (((1,), (1,)), ((), ())), preferred_element_type=F32)
    wide = 2 * vectors
    near = prod[:, :wide]
    far = prod[:, wide:]

    def rows(value, at):
        return value[at * vectors:(at + 1) * vectors]

    energy_low = rows(near, 0) + (rows(near, 1) + (rows(near, 2) + rows(far, 0)))
    energy_high = rows(near, 0) + rows(near, 1)
    quotient_low = rows(near, 3) + rows(far, 3)
    quotient_high = rows(near, 3)
    lane = lax.broadcasted_iota(jnp.int32, (vectors, wide), 1)
    gram_ref[...] = jnp.where(
        lane < vectors,
        energy_low + pltpu.roll(energy_high, vectors, 1),
        quotient_high + pltpu.roll(quotient_low, vectors, 1),
    )


def finish_kernel(total_rows, gram_ref, split_ref, out_ref, quotient_ref):
    vectors = gram_ref.shape[0]
    wide = 2 * vectors
    gram = gram_ref[...]
    quotient_ref[...] = (gram / total_rows)[:, vectors:]
    row = lax.broadcasted_iota(jnp.int32, (vectors, wide), 0)
    lane = lax.broadcasted_iota(jnp.int32, (vectors, wide), 1)
    work = jnp.where(lane < vectors, gram, jnp.where(lane == row + vectors, 1.0, 0.0))
    height = 8
    tiles = [work[at * height:(at + 1) * height] for at in range(vectors // height)]
    row8 = lax.broadcasted_iota(jnp.int32, (height, wide), 0)
    for step in range(vectors):
        home = step // height
        own = tiles[home][step % height:step % height + 1]
        scaled = own / own[:, step:step + 1]
        for at in range(home, vectors // height):
            column = tiles[at][:, step:step + 1]
            change = column * scaled
            if at == home:
                change = jnp.where(row8 > step % height, change, 0.0)
            tiles[at] = tiles[at] - change
    done = jnp.concatenate(tiles, axis=0)
    pivot = jnp.sum(jnp.where(lane == row, done, 0.0), axis=1, keepdims=True)
    inverse = done * (lax.rsqrt(pivot) * math.sqrt(total_rows))
    inverse = inverse[:, vectors:]
    w_high, w_mid, w_low = split3(inverse)
    left = jnp.concatenate([w_high, w_high, w_high, w_mid, w_mid, w_low], axis=1)
    pieces = split_ref[...]
    right = jnp.concatenate([pieces, pieces[:2 * vectors], pieces[:vectors]], axis=0)
    out_ref[...] = jnp.dot(left, right, preferred_element_type=F32)


def on_device(krylov_block, degree, tile_values, tile_column, tile_live):
    vectors, owned = krylov_block.shape
    block_rows, _, height, slot_width = tile_values.shape
    sources = lax.axis_size("row")
    groups = lax.axis_size("col")
    per_piece = owned // height
    half = owned // 2
    degree_row = degree.reshape(1, owned)
    left, right = pl.pallas_call(
        scale_kernel,
        out_shape=[jax.ShapeDtypeStruct((vectors, half), BF16)] * 2,
        in_specs=[vmem(), vmem()],
        out_specs=[vmem(), vmem()],
        name="scale",
    )(krylov_block, degree_row)
    row_bits = bits(sources)
    left_bits = row_bits[:0:-1] + row_bits[:1]
    right_bits = row_bits[:1] + row_bits[:0:-1]
    left, right = left[None], right[None]
    left_order, right_order = [0], [0]
    for left_bit, right_bit in zip(left_bits, right_bits):
        new_left = swap(left, "row", sources, left_bit)
        new_right = swap(right, "row", sources, right_bit)
        left = jnp.concatenate([left, new_left], axis=0)
        right = jnp.concatenate([right, new_right], axis=0)
        left_order = left_order + [at ^ left_bit for at in left_order]
        right_order = right_order + [at ^ right_bit for at in right_order]
    many = groups // 2
    keep, send = pl.pallas_call(
        lambda *refs: tile_kernel(sources, groups, per_piece, left_order, right_order, *refs),
        out_shape=[
            jax.ShapeDtypeStruct((many, vectors, owned), F32),
            jax.ShapeDtypeStruct((many, vectors, owned), BF16),
        ],
        in_specs=[smem(), smem(), vmem(), vmem(), vmem()],
        out_specs=[vmem(), vmem()],
        scratch_shapes=[
            pltpu.VMEM((sources * per_piece + 1, vectors, 2 * height), BF16),
            pltpu.VMEM((2, 4 * vectors, slot_width), BF16),
        ],
        compiler_params=pltpu.CompilerParams(vmem_limit_bytes=48 << 20),
        name="tiles",
    )(tile_column[:, 0], tile_live[:, 0], left, right, tile_values[:, 0])
    running = keep
    received = []
    for bit in bits(groups):
        got = swap(send, "col", groups, bit)
        received.append(got)
        if running.shape[0] > 1:
            summed = running + got.astype(F32)
            pairs = summed.reshape((-1, 2) + summed.shape[1:])
            running, send = pairs[:, 0], pairs[:, 1].astype(BF16)
    pieces, gram = pl.pallas_call(
        lambda *refs: gram_kernel(len(received), *refs),
        out_shape=[
            jax.ShapeDtypeStruct((3 * vectors, owned), BF16),
            jax.ShapeDtypeStruct((vectors, 2 * vectors), F32),
        ],
        in_specs=[vmem()] * (3 + len(received)),
        out_specs=[vmem(), vmem()],
        scratch_shapes=[pltpu.VMEM((4 * vectors, owned), BF16)],
        name="gram",
    )(krylov_block, degree_row, keep, *received)
    for axis, size in (("col", groups), ("row", sources)):
        for bit in bits(size):
            gram = gram + swap(gram, axis, size, bit)
    total_rows = sources * groups * owned
    orthonormal, quotient = pl.pallas_call(
        lambda *refs: finish_kernel(total_rows, *refs),
        out_shape=[
            jax.ShapeDtypeStruct((vectors, owned), F32),
            jax.ShapeDtypeStruct((vectors, vectors), F32),
        ],
        in_specs=[vmem(), vmem()],
        out_specs=[vmem(), vmem()],
        name="finish",
    )(gram, pieces)
    return (orthonormal, quotient)


def solution(mesh):
    return jax.shard_map(
        on_device,
        mesh=mesh,
        in_specs=(
            P(None, ("row", "col")),
            P(("row", "col")),
            P("row", "col", None, None),
            P("row", "col", None),
            P("row", "col", None),
        ),
        out_specs=(P(None, ("row", "col")), P()),
        check_vma=False,
    )
```

time: 157 us -> 63.3 us (0.40)
  blocking collectives: 73 us -> 0 us
  starting transfers between devices: 0.04 us -> 22.1 us
  local copies, waits for them, and re-layouts: 24.5 us -> 3.74 us
  between operations: 14.1 us -> 0.71 us
  Pallas kernels: 0 us -> 13.2 us
  other arithmetic: 16.1 us -> 6.07 us
  waiting for transfers between devices: 22.9 us -> 16.7 us
  matrix products: 5.85 us -> 0 us
    psum x1 -> x0, blocking collectives: 40 us -> none  [on_device(): lax.psum((gram_of(basis_wide, applied), gram_of(applied, applied)), ('row...]
    all_gather x1 -> x0, blocking collectives: 33 us -> none  [on_device(): gathered = lax.all_gather(scaled, 'row', axis=1, tiled=True)]
    reduce_scatter x1 -> x0, waiting for transfers between devices: 22.9 us -> none  [on_device(): lax.psum_scatter(whole_rows, 'col', scatter_dimension=1, tiled=True)]
    ppermute x0 -> x13, starting transfers between devices: none -> 22.1 us  [swap(): return lax.ppermute(value, axis, [(i, i ^ mask) for i in range(size)])]
    ppermute x0 -> x13, waiting for transfers between devices: none -> 16.7 us  [swap(): return lax.ppermute(value, axis, [(i, i ^ mask) for i in range(size)])]
    gather x3 -> x0, local copies, waits for them, and re-layouts: 16.3 us -> none  [on_device(): chosen = jnp.take(blocks, pick_index, axis=1)]
    pallas_call x0 -> x4, Pallas kernels: none -> 13.2 us  [the longest x1 7.17 us: on_device(): pl.pallas_call(lambda *refs: finish_kernel(total_rows, *refs), out_shape=...]
    another operation x5 -> x0, other arithmetic: 12.1 us -> none  [the longest x3 6.52 us: on_device(): factor = jnp.linalg.cholesky(energy)]
  transfers between devices with their start and end apart: 1 -> 13, of which waited for: 1 -> 9; matrix products, arithmetic and copies ran while one was open for 0% -> 9% of each run, Pallas kernels for 0% -> 0%
where the time goes in v1:
time: 63.3 us; the launch traced here: 62.5 us
  starting transfers between devices  22.1 us (35%)
  waiting for transfers between devices  16.7 us (26%)
  Pallas kernels  13.2 us (21%)
  other arithmetic  6.07 us (10%)
  local copies, waits for them, and re-layouts  3.74 us (6%)
  between operations  0.71 us (1%)
    ppermute x13, starting transfers between devices, swap(): return lax.ppermute(value, axis, [(i, i ^ mask) for i in range(size)])  22.1 us
    ppermute x13, waiting for transfers between devices, swap(): return lax.ppermute(value, axis, [(i, i ^ mask) for i in range(size)])  16.7 us
    pallas_call x1, Pallas kernels, on_device(): pl.pallas_call(lambda *refs: finish_kernel(total_rows, *refs), out_shape=...  7.17 us
    unnamed x10, local copies, waits for them, and re-layouts  3.73 us
    pallas_call x1, Pallas kernels, on_device(): pl.pallas_call(lambda *refs: tile_kernel(sources, groups, per_piece, left...  2.51 us
    concatenate x3, other arithmetic, on_device(): right = jnp.concatenate([right, new_right], axis=0)  2.32 us
    concatenate x3, other arithmetic, on_device(): left = jnp.concatenate([left, new_left], axis=0)  2.32 us
    pallas_call x1, Pallas kernels, on_device(): pl.pallas_call(lambda *refs: gram_kernel(len(received), *refs), out_shape...  2.04 us
  transfers between devices with their start and end apart: 13, of which 9 were waited for; matrix products, arithmetic and copies ran while one was open for 9% of the time, Pallas kernels for 0%

profile of v1, /device:TPU:0, one launch (start us, length us, event | category | flops | bytes accessed | tf_op | source)
XLA Modules:
  0.0 62.5 jit_solution(8241747399978252301)
XLA Ops:
  0.6 1.5 %scale.1 = (bf16[64,256]{1,0:T(8,128)(2,1)}, bf16[64,256]{1,0:T(8,128)(2,1)}) custom-call(bf16[64,512]{1,0:T(8,128)(2,1)} %refs_0_.1, s32[1,512]{1,0:T(1,128)} %bitcast.21), custom_call_target="tpu_custom_call" | custom-call | tf_op jit(solution)/shard_map/scale/pallas_call | solution.py:195
  2.1 2.9 %collective-permute-start.3 = (bf16[1,64,256]{2,1,0:T(8,128)(2,1)}, bf16[1,64,256]{2,1,0:T(8,128)(2,1)S(1)}, u32[]{:S(2)}, u32[]{:S(2)}) collective-permute-start(bf16[1,64,256]{2,1,0:T(8,128)(2,1)} %bitcast.17), channel_id=1, source_target_pairs={{0,4},{4,0},{8,12},{12,8},{16,20},{20,16},{24,28},{28,24},{1,5},{5... | collective-permute-start | bytes 98312 | tf_op jit(solution)/shard_map/ppermute | solution.py:23
  5.1 2.6 %collective-permute-start = (bf16[1,64,256]{2,1,0:T(8,128)(2,1)}, bf16[1,64,256]{2,1,0:T(8,128)(2,1)S(1)}, u32[]{:S(2)}, u32[]{:S(2)}) collective-permute-start(bf16[1,64,256]{2,1,0:T(8,128)(2,1)} %bitcast.13), channel_id=1, source_target_pairs={{0,16},{4,20},{8,24},{12,28},{16,0},{20,4},{24,8},{28,12},{1,17},{... | collective-permute-start | bytes 98312 | tf_op jit(solution)/shard_map/ppermute | solution.py:23
  7.6 0.0 collective-permute-done.3
  7.6 0.8 %pad_maximum_fusion.5 = bf16[2,64,256]{2,1,0:T(8,128)(2,1)S(1)} fusion(bf16[1,64,256]{2,1,0:T(8,128)(2,1)S(1)} %collective-permute-done.3, bf16[1,64,256]{2,1,0:T(8,128)(2,1)} %bitcast.18), kind=kLoop, calls=%fused_computation.8 | loop fusion | flops 32768 | bytes 131072 | tf_op jit(solution)/shard_map/concatenate | solution.py:211
  8.4 2.6 %collective-permute-start.4 = (bf16[2,64,256]{2,1,0:T(8,128)(2,1)S(1)}, bf16[2,64,256]{2,1,0:T(8,128)(2,1)S(1)}, u32[]{:S(2)}, u32[]{:S(2)}) collective-permute-start(bf16[2,64,256]{2,1,0:T(8,128)(2,1)S(1)} %pad_maximum_fusion.5), channel_id=1, source_target_pairs={{0,16},{4,20},{8,24},{12,28},{16,0},{20,4},{24,8},{28,12},{1,17},{... | collective-permute-start | bytes 196616 | tf_op jit(solution)/shard_map/ppermute | solution.py:23
  11.0 0.0 collective-permute-done
  11.0 0.8 %pad_maximum_fusion.4 = bf16[2,64,256]{2,1,0:T(8,128)(2,1)S(1)} fusion(bf16[1,64,256]{2,1,0:T(8,128)(2,1)S(1)} %collective-permute-done, bf16[1,64,256]{2,1,0:T(8,128)(2,1)} %bitcast.14), kind=kLoop, calls=%fused_computation.7 | loop fusion | flops 32768 | bytes 131072 | tf_op jit(solution)/shard_map/concatenate | solution.py:210
  11.8 1.6 %collective-permute-start.1 = (bf16[2,64,256]{2,1,0:T(8,128)(2,1)S(1)}, bf16[2,64,256]{2,1,0:T(8,128)(2,1)S(1)}, u32[]{:S(2)}, u32[]{:S(2)}) collective-permute-start(bf16[2,64,256]{2,1,0:T(8,128)(2,1)S(1)} %pad_maximum_fusion.4), channel_id=1, source_target_pairs={{0,8},{4,12},{8,0},{12,4},{16,24},{20,28},{24,16},{28,20},{1,9},{5... | collective-permute-start | bytes 196616 | tf_op jit(solution)/shard_map/ppermute | solution.py:23
  13.4 0.3 collective-permute-done.4
  13.7 0.8 %pad_maximum_fusion.3 = bf16[4,64,256]{2,1,0:T(8,128)(2,1)S(1)} fusion(bf16[2,64,256]{2,1,0:T(8,128)(2,1)S(1)} %collective-permute-done.4, bf16[1,64,256]{2,1,0:T(8,128)(2,1)S(1)} %collective-permute-done.3, bf16[1,64,256]{2,1,0:T(8,128)(2,1)} %bitcast.19), kind=kLoop, calls=%fused_computation.5 | loop fusion | flops 131072 | bytes 262144 | tf_op jit(solution)/shard_map/concatenate | solution.py:211
  14.5 2.2 %collective-permute-start.5 = (bf16[4,64,256]{2,1,0:T(8,128)(2,1)S(1)}, bf16[4,64,256]{2,1,0:T(8,128)(2,1)S(1)}, u32[]{:S(2)}, u32[]{:S(2)}) collective-permute-start(bf16[4,64,256]{2,1,0:T(8,128)(2,1)S(1)} %pad_maximum_fusion.3), channel_id=1, source_target_pairs={{0,8},{4,12},{8,0},{12,4},{16,24},{20,28},{24,16},{28,20},{1,9},{5... | collective-permute-start | bytes 393224 | tf_op jit(solution)/shard_map/ppermute | solution.py:23
  16.7 0.1 collective-permute-done.1
  16.8 0.8 %pad_maximum_fusion.2 = bf16[4,64,256]{2,1,0:T(8,128)(2,1)S(1)} fusion(bf16[2,64,256]{2,1,0:T(8,128)(2,1)S(1)} %collective-permute-done.1, bf16[1,64,256]{2,1,0:T(8,128)(2,1)S(1)} %collective-permute-done, bf16[1,64,256]{2,1,0:T(8,128)(2,1)} %bitcast.15), kind=kLoop, calls=%fused_computation.4 | loop fusion | flops 131072 | bytes 262144 | tf_op jit(solution)/shard_map/concatenate | solution.py:210
  17.5 1.5 %collective-permute-start.2 = (bf16[4,64,256]{2,1,0:T(8,128)(2,1)S(1)}, bf16[4,64,256]{2,1,0:T(8,128)(2,1)S(1)}, u32[]{:S(2)}, u32[]{:S(2)}) collective-permute-start(bf16[4,64,256]{2,1,0:T(8,128)(2,1)S(1)} %pad_maximum_fusion.2), channel_id=1, source_target_pairs={{0,4},{4,0},{8,12},{12,8},{16,20},{20,16},{24,28},{28,24},{1,5},{5... | collective-permute-start | bytes 393224 | tf_op jit(solution)/shard_map/ppermute | solution.py:23
  19.0 0.8 %copy.7 = s32[32,1,8]{2,0,1:T(8,128)S(1)} copy(s32[32,1,8]{0,2,1:T(8,128)} %param.8) | data formatting | bytes 2048 | tf_op args[3]
  19.8 0.8 %copy.8 = s32[32,1,8]{2,0,1:T(8,128)S(1)} copy(s32[32,1,8]{0,2,1:T(8,128)} %param.9) | data formatting | bytes 2048 | tf_op args[4]
  20.5 0.0 collective-permute-done.5
  20.6 0.8 %pad_maximum_fusion.1.refs_3_ = bf16[8,64,256]{2,1,0:T(8,128)(2,1)S(1)} fusion(bf16[4,64,256]{2,1,0:T(8,128)(2,1)S(1)} %collective-permute-done.5, bf16[2,64,256]{2,1,0:T(8,128)(2,1)S(1)} %collective-permute-done.4, bf16[1,64,256]{2,1,0:T(8,128)(2,1)S(1)} %collective-permute-done.3, bf16[1,64,256]{2,1,0:T(8,128)(2,1)} %bitcast.20), kind=kLoop, calls=%fused_computation.1 | loop fusion | flops 393216 | bytes 524288 | tf_op jit(solution)/shard_map/concatenate | solution.py:211
  21.3 1.2 %collective-permute-done.2 = bf16[4,64,256]{2,1,0:T(8,128)(2,1)S(1)} collective-permute-done((bf16[4,64,256]{2,1,0:T(8,128)(2,1)S(1)}, bf16[4,64,256]{2,1,0:T(8,128)(2,1)S(1)}, u32[]{:S(2)}, u32[]{:S(2)}) %collective-permute-start.2) | collective-permute-done | bytes 131104 | tf_op jit(solution)/shard_map/ppermute | solution.py:23
  22.6 0.8 %pad_maximum_fusion.refs_2_ = bf16[8,64,256]{2,1,0:T(8,128)(2,1)S(1)} fusion(bf16[4,64,256]{2,1,0:T(8,128)(2,1)S(1)} %collective-permute-done.2, bf16[2,64,256]{2,1,0:T(8,128)(2,1)S(1)} %collective-permute-done.1, bf16[1,64,256]{2,1,0:T(8,128)(2,1)S(1)} %collective-permute-done, bf16[1,64,256]{2,1,0:T(8,128)(2,1)} %bitcast.16), kind=kLoop, calls=%fused_computation | loop fusion | flops 393216 | bytes 524288 | tf_op jit(solution)/shard_map/concatenate | solution.py:210
  23.4 0.0 copy-start
  23.4 1.6 %copy-done = bf16[32,1,64,512]{3,2,1,0:T(8,128)(2,1)S(1)} copy-done((bf16[32,1,64,512]{3,2,1,0:T(8,128)(2,1)S(1)}, bf16[32,1,64,512]{3,2,1,0:T(8,128)(2,1)}, u32[]{:S(2)}) %copy-start) | copy-done | bytes 2097176
  25.0 2.5 %tiles.1 = (f32[2,64,512]{2,1,0:T(8,128)S(1)}, bf16[2,64,512]{2,1,0:T(8,128)(2,1)S(1)}) custom-call(s32[32,8]{1,0:T(8,128)S(1)} %bitcast.11, s32[32,8]{1,0:T(8,128)S(1)} %bitcast.12, bf16[8,64,256]{2,1,0:T(8,128)(2,1)S(1)} %pad_maximum_fusion.refs_2_, bf16[8,64,256]{2,1,0:T(8,128)(2,1)S(1)} %pad_maximum_fusion.1.refs_3_, bf16[32,64,512]{2,1,0:T(8,128)(2,1)S(1)} %bitcast.10), custom_call_target="tpu_custom_call" | custom-call | tf_op jit(solution)/shard_map/tiles/pallas_call | solution.py:215
  27.5 0.0 copy-start.1
  27.5 0.1 collective-permute-start.6
  27.6 1.3 %collective-permute-done.6.refs_3_ = bf16[2,64,512]{2,1,0:T(8,128)(2,1)S(1)} collective-permute-done((bf16[2,64,512]{2,1,0:T(8,128)(2,1)S(1)}, bf16[2,64,512]{2,1,0:T(8,128)(2,1)S(1)}, u32[]{:S(2)}, u32[]{:S(2)}) %collective-permute-start.6) | collective-permute-done | bytes 131104 | tf_op jit(solution)/shard_map/ppermute | solution.py:23
  28.9 0.0 copy-start.2
  29.0 1.6 %collective-permute-start.7 = (bf16[1,64,512]{2,1,0:T(8,128)(2,1)S(1)}, bf16[1,64,512]{2,1,0:T(8,128)(2,1)S(1)}, u32[]{:S(2)}, u32[]{:S(2)}) collective-permute-start(bf16[1,64,512]{2,1,0:T(8,128)(2,1)S(1)} %slice_bitcast_fusion), channel_id=1, source_target_pairs={{0,2},{1,3},{2,0},{3,1},{4,6},{5,7},{6,4},{7,5},{8,10},{9,11},{10,... | collective-permute-start | bytes 196616 | tf_op jit(solution)/shard_map/ppermute | solution.py:23
  30.5 2.7 %collective-permute-done.7.refs_4_ = bf16[1,64,512]{2,1,0:T(8,128)(2,1)S(1)} collective-permute-done((bf16[1,64,512]{2,1,0:T(8,128)(2,1)S(1)}, bf16[1,64,512]{2,1,0:T(8,128)(2,1)S(1)}, u32[]{:S(2)}, u32[]{:S(2)}) %collective-permute-start.7) | collective-permute-done | bytes 65568 | tf_op jit(solution)/shard_map/ppermute | solution.py:23
  33.3 0.0 copy-done.1
  33.3 0.0 copy-done.2
  33.3 0.0 copy-start.3
  33.3 0.6 copy-done.3
  33.9 2.0 %gram.1 = (bf16[192,512]{1,0:T(8,128)(2,1)}, f32[64,128]{1,0:T(8,128)}) custom-call(bf16[64,512]{1,0:T(8,128)(2,1)} %refs_0_.1, s32[1,512]{1,0:T(1,128)} %bitcast.22, f32[2,64,512]{2,1,0:T(8,128)} %copy-done.1, bf16[2,64,512]{2,1,0:T(8,128)(2,1)} %copy-done.2, bf16[1,64,512]{2,1,0:T(8,128)(2,1)} %copy-done.3), custom_call_target="tpu_custom_call" | custom-call | tf_op jit(solution)/shard_map/gram/pallas_call | solution.py:239
  36.0 0.0 collective-permute-start.8
  36.0 1.4 %collective-permute-done.8 = f32[64,128]{1,0:T(8,128)S(1)} collective-permute-done((f32[64,128]{1,0:T(8,128)}, f32[64,128]{1,0:T(8,128)S(1)}, u32[]{:S(2)}, u32[]{:S(2)}) %collective-permute-start.8) | collective-permute-done | bytes 32800 | tf_op jit(solution)/shard_map/ppermute | solution.py:23
  37.4 0.8 %add.19 = f32[64,128]{1,0:T(8,128)S(1)} add(f32[64,128]{1,0:T(8,128)} %get-tuple-element.12, f32[64,128]{1,0:T(8,128)S(1)} %collective-permute-done.8) | non-fusion elementwise | flops 8192 | bytes 98304 | tf_op jit(solution)/shard_map/add | solution.py:252
  38.1 1.5 %collective-permute-start.9 = (f32[64,128]{1,0:T(8,128)S(1)}, f32[64,128]{1,0:T(8,128)S(1)}, u32[]{:S(2)}, u32[]{:S(2)}) collective-permute-start(f32[64,128]{1,0:T(8,128)S(1)} %add.19), channel_id=1, source_target_pairs={{0,2},{1,3},{2,0},{3,1},{4,6},{5,7},{6,4},{7,5},{8,10},{9,11},{10,... | collective-permute-start | bytes 98312 | tf_op jit(solution)/shard_map/ppermute | solution.py:23
  39.7 2.4 %collective-permute-done.9 = f32[64,128]{1,0:T(8,128)S(1)} collective-permute-done((f32[64,128]{1,0:T(8,128)S(1)}, f32[64,128]{1,0:T(8,128)S(1)}, u32[]{:S(2)}, u32[]{:S(2)}) %collective-permute-start.9) | collective-permute-done | bytes 32800 | tf_op jit(solution)/shard_map/ppermute | solution.py:23
  42.1 1.4 %collective-permute-start.10 = (f32[64,128]{1,0:T(8,128)S(1)}, f32[64,128]{1,0:T(8,128)S(1)}, u32[]{:S(2)}, u32[]{:S(2)}) collective-permute-start(f32[64,128]{1,0:T(8,128)S(1)} %add.20), channel_id=1, source_target_pairs={{0,4},{4,0},{8,12},{12,8},{16,20},{20,16},{24,28},{28,24},{1,5},{5... | collective-permute-start | bytes 98312 | tf_op jit(solution)/shard_map/ppermute | solution.py:23
  43.5 2.5 %collective-permute-done.10 = f32[64,128]{1,0:T(8,128)S(1)} collective-permute-done((f32[64,128]{1,0:T(8,128)S(1)}, f32[64,128]{1,0:T(8,128)S(1)}, u32[]{:S(2)}, u32[]{:S(2)}) %collective-permute-start.10) | collective-permute-done | bytes 32800 | tf_op jit(solution)/shard_map/ppermute | solution.py:23
  46.0 1.6 %collective-permute-start.11 = (f32[64,128]{1,0:T(8,128)S(1)}, f32[64,128]{1,0:T(8,128)S(1)}, u32[]{:S(2)}, u32[]{:S(2)}) collective-permute-start(f32[64,128]{1,0:T(8,128)S(1)} %add.21), channel_id=1, source_target_pairs={{0,8},{4,12},{8,0},{12,4},{16,24},{20,28},{24,16},{28,20},{1,9},{5... | collective-permute-start | bytes 98312 | tf_op jit(solution)/shard_map/ppermute | solution.py:23
  47.6 2.3 %collective-permute-done.11 = f32[64,128]{1,0:T(8,128)S(1)} collective-permute-done((f32[64,128]{1,0:T(8,128)S(1)}, f32[64,128]{1,0:T(8,128)S(1)}, u32[]{:S(2)}, u32[]{:S(2)}) %collective-permute-start.11) | collective-permute-done | bytes 32800 | tf_op jit(solution)/shard_map/ppermute | solution.py:23
  49.9 2.5 %collective-permute-start.12 = (f32[64,128]{1,0:T(8,128)S(1)}, f32[64,128]{1,0:T(8,128)S(1)}, u32[]{:S(2)}, u32[]{:S(2)}) collective-permute-start(f32[64,128]{1,0:T(8,128)S(1)} %add.22), channel_id=1, source_target_pairs={{0,16},{4,20},{8,24},{12,28},{16,0},{20,4},{24,8},{28,12},{1,17},{... | collective-permute-start | bytes 98312 | tf_op jit(solution)/shard_map/ppermute | solution.py:23
  52.4 2.3 %collective-permute-done.12 = f32[64,128]{1,0:T(8,128)S(1)} collective-permute-done((f32[64,128]{1,0:T(8,128)S(1)}, f32[64,128]{1,0:T(8,128)S(1)}, u32[]{:S(2)}, u32[]{:S(2)}) %collective-permute-start.12) | collective-permute-done | bytes 32800 | tf_op jit(solution)/shard_map/ppermute | solution.py:23
  54.7 0.6 add.23.refs_0_
  55.3 7.2 %finish.1 = (f32[64,512]{1,0:T(8,128)}, f32[64,64]{1,0:T(8,128)}) custom-call(f32[64,128]{1,0:T(8,128)} %add.23.refs_0_, bf16[192,512]{1,0:T(8,128)(2,1)} %get-tuple-element.13.refs_1_), custom_call_target="tpu_custom_call" | custom-call | tf_op jit(solution)/shard_map/finish/pallas_call | solution.py:254
  (5 shorter events, 0.0 us)
Async XLA Ops:
  2.1 5.5 %collective-permute-start.3 = (bf16[1,64,256]{2,1,0:T(8,128)(2,1)}, bf16[1,64,256]{2,1,0:T(8,128)(2,1)S(1)}, u32[]{:S(2)}, u32[]{:S(2)}) collective-permute-start(bf16[1,64,256]{2,1,0:T(8,128)(2,1)} %bitcast.17), channel_id=1, source_target_pairs={{0,4},{4,0},{8,12},{12,8},{16,20},{20,16},{24,28},{28,24},{1,5},{5... | collective-permute-start | bytes 98312 | tf_op jit(solution)/shard_map/ppermute | solution.py:23
  5.1 6.0 %collective-permute-start = (bf16[1,64,256]{2,1,0:T(8,128)(2,1)}, bf16[1,64,256]{2,1,0:T(8,128)(2,1)S(1)}, u32[]{:S(2)}, u32[]{:S(2)}) collective-permute-start(bf16[1,64,256]{2,1,0:T(8,128)(2,1)} %bitcast.13), channel_id=1, source_target_pairs={{0,16},{4,20},{8,24},{12,28},{16,0},{20,4},{24,8},{28,12},{1,17},{... | collective-permute-start | bytes 98312 | tf_op jit(solution)/shard_map/ppermute | solution.py:23
  8.4 5.3 %collective-permute-start.4 = (bf16[2,64,256]{2,1,0:T(8,128)(2,1)S(1)}, bf16[2,64,256]{2,1,0:T(8,128)(2,1)S(1)}, u32[]{:S(2)}, u32[]{:S(2)}) collective-permute-start(bf16[2,64,256]{2,1,0:T(8,128)(2,1)S(1)} %pad_maximum_fusion.5), channel_id=1, source_target_pairs={{0,16},{4,20},{8,24},{12,28},{16,0},{20,4},{24,8},{28,12},{1,17},{... | collective-permute-start | bytes 196616 | tf_op jit(solution)/shard_map/ppermute | solution.py:23
  11.8 5.0 %collective-permute-start.1 = (bf16[2,64,256]{2,1,0:T(8,128)(2,1)S(1)}, bf16[2,64,256]{2,1,0:T(8,128)(2,1)S(1)}, u32[]{:S(2)}, u32[]{:S(2)}) collective-permute-start(bf16[2,64,256]{2,1,0:T(8,128)(2,1)S(1)} %pad_maximum_fusion.4), channel_id=1, source_target_pairs={{0,8},{4,12},{8,0},{12,4},{16,24},{20,28},{24,16},{28,20},{1,9},{5... | collective-permute-start | bytes 196616 | tf_op jit(solution)/shard_map/ppermute | solution.py:23
  14.5 6.1 %collective-permute-start.5 = (bf16[4,64,256]{2,1,0:T(8,128)(2,1)S(1)}, bf16[4,64,256]{2,1,0:T(8,128)(2,1)S(1)}, u32[]{:S(2)}, u32[]{:S(2)}) collective-permute-start(bf16[4,64,256]{2,1,0:T(8,128)(2,1)S(1)} %pad_maximum_fusion.3), channel_id=1, source_target_pairs={{0,8},{4,12},{8,0},{12,4},{16,24},{20,28},{24,16},{28,20},{1,9},{5... | collective-permute-start | bytes 393224 | tf_op jit(solution)/shard_map/ppermute | solution.py:23
  17.5 5.0 %collective-permute-start.2 = (bf16[4,64,256]{2,1,0:T(8,128)(2,1)S(1)}, bf16[4,64,256]{2,1,0:T(8,128)(2,1)S(1)}, u32[]{:S(2)}, u32[]{:S(2)}) collective-permute-start(bf16[4,64,256]{2,1,0:T(8,128)(2,1)S(1)} %pad_maximum_fusion.2), channel_id=1, source_target_pairs={{0,4},{4,0},{8,12},{12,8},{16,20},{20,16},{24,28},{28,24},{1,5},{5... | collective-permute-start | bytes 393224 | tf_op jit(solution)/shard_map/ppermute | solution.py:23
  23.4 1.6 %copy-start = (bf16[32,1,64,512]{3,2,1,0:T(8,128)(2,1)S(1)}, bf16[32,1,64,512]{3,2,1,0:T(8,128)(2,1)}, u32[]{:S(2)}) copy-start(bf16[32,1,64,512]{3,2,1,0:T(8,128)(2,1)} %param.7) | copy-start | bytes 6291460
  27.5 5.8 %copy-start.1 = (f32[2,64,512]{2,1,0:T(8,128)}, f32[2,64,512]{2,1,0:T(8,128)S(1)}, u32[]{:S(2)}) copy-start(f32[2,64,512]{2,1,0:T(8,128)S(1)} %get-tuple-element.10.refs_2_) | copy-start | bytes 786436
  27.5 1.4 %collective-permute-start.6 = (bf16[2,64,512]{2,1,0:T(8,128)(2,1)S(1)}, bf16[2,64,512]{2,1,0:T(8,128)(2,1)S(1)}, u32[]{:S(2)}, u32[]{:S(2)}) collective-permute-start(bf16[2,64,512]{2,1,0:T(8,128)(2,1)S(1)} %get-tuple-element.11), channel_id=1, source_target_pairs={{0,1},{1,0},{2,3},{3,2},{4,5},{5,4},{6,7},{7,6},{8,9},{9,8},{10,11... | collective-permute-start | bytes 393224 | tf_op jit(solution)/shard_map/ppermute | solution.py:23
  28.9 4.4 %copy-start.2 = (bf16[2,64,512]{2,1,0:T(8,128)(2,1)}, bf16[2,64,512]{2,1,0:T(8,128)(2,1)S(1)}, u32[]{:S(2)}) copy-start(bf16[2,64,512]{2,1,0:T(8,128)(2,1)S(1)} %collective-permute-done.6.refs_3_) | copy-start | bytes 393220
  29.0 4.3 %collective-permute-start.7 = (bf16[1,64,512]{2,1,0:T(8,128)(2,1)S(1)}, bf16[1,64,512]{2,1,0:T(8,128)(2,1)S(1)}, u32[]{:S(2)}, u32[]{:S(2)}) collective-permute-start(bf16[1,64,512]{2,1,0:T(8,128)(2,1)S(1)} %slice_bitcast_fusion), channel_id=1, source_target_pairs={{0,2},{1,3},{2,0},{3,1},{4,6},{5,7},{6,4},{7,5},{8,10},{9,11},{10,... | collective-permute-start | bytes 196616 | tf_op jit(solution)/shard_map/ppermute | solution.py:23
  33.3 0.6 copy-start.3
  36.0 1.4 %collective-permute-start.8 = (f32[64,128]{1,0:T(8,128)}, f32[64,128]{1,0:T(8,128)S(1)}, u32[]{:S(2)}, u32[]{:S(2)}) collective-permute-start(f32[64,128]{1,0:T(8,128)} %get-tuple-element.12), channel_id=1, source_target_pairs={{0,1},{1,0},{2,3},{3,2},{4,5},{5,4},{6,7},{7,6},{8,9},{9,8},{10,11... | collective-permute-start | bytes 98312 | tf_op jit(solution)/shard_map/ppermute | solution.py:23
  38.1 3.9 %collective-permute-start.9 = (f32[64,128]{1,0:T(8,128)S(1)}, f32[64,128]{1,0:T(8,128)S(1)}, u32[]{:S(2)}, u32[]{:S(2)}) collective-permute-start(f32[64,128]{1,0:T(8,128)S(1)} %add.19), channel_id=1, source_target_pairs={{0,2},{1,3},{2,0},{3,1},{4,6},{5,7},{6,4},{7,5},{8,10},{9,11},{10,... | collective-permute-start | bytes 98312 | tf_op jit(solution)/shard_map/ppermute | solution.py:23
  42.1 3.9 %collective-permute-start.10 = (f32[64,128]{1,0:T(8,128)S(1)}, f32[64,128]{1,0:T(8,128)S(1)}, u32[]{:S(2)}, u32[]{:S(2)}) collective-permute-start(f32[64,128]{1,0:T(8,128)S(1)} %add.20), channel_id=1, source_target_pairs={{0,4},{4,0},{8,12},{12,8},{16,20},{20,16},{24,28},{28,24},{1,5},{5... | collective-permute-start | bytes 98312 | tf_op jit(solution)/shard_map/ppermute | solution.py:23
  46.0 3.9 %collective-permute-start.11 = (f32[64,128]{1,0:T(8,128)S(1)}, f32[64,128]{1,0:T(8,128)S(1)}, u32[]{:S(2)}, u32[]{:S(2)}) collective-permute-start(f32[64,128]{1,0:T(8,128)S(1)} %add.21), channel_id=1, source_target_pairs={{0,8},{4,12},{8,0},{12,4},{16,24},{20,28},{24,16},{28,20},{1,9},{5... | collective-permute-start | bytes 98312 | tf_op jit(solution)/shard_map/ppermute | solution.py:23
  49.9 4.8 %collective-permute-start.12 = (f32[64,128]{1,0:T(8,128)S(1)}, f32[64,128]{1,0:T(8,128)S(1)}, u32[]{:S(2)}, u32[]{:S(2)}) collective-permute-start(f32[64,128]{1,0:T(8,128)S(1)} %add.22), channel_id=1, source_target_pairs={{0,16},{4,20},{8,24},{12,28},{16,0},{20,4},{24,8},{28,12},{1,17},{... | collective-permute-start | bytes 98312 | tf_op jit(solution)/shard_map/ppermute | solution.py:23

commit v2 on v1

--- a/solution.py
+++ b/solution.py
@@ -9,6 +9,10 @@
 
 F32 = jnp.float32
 BF16 = jnp.bfloat16
+
+
+def limit(mib):
+    return pltpu.CompilerParams(vmem_limit_bytes=mib << 20)
 
 
 def vmem():
@@ -53,7 +57,7 @@
     vectors = left_ref.shape[1]
     half = left_ref.shape[2]
     height = panel_ref.shape[1]
-    slots = column_ref.shape[1]
+    slots = column_ref.shape[0]
     wide = 2 * height
     pairs = half // wide
     my_row = lax.axis_index("row")
@@ -78,10 +82,10 @@
         for inner in range(pack):
             row = row0 + inner
             for pair in range(slots // 2):
-                first = column_ref[row, 2 * pair] ^ turn
-                second = column_ref[row, 2 * pair + 1] ^ turn ^ 1
-                first = jnp.where(live_ref[row, 2 * pair] == 1, first, zero_at)
-                second = jnp.where(live_ref[row, 2 * pair + 1] == 1, second, zero_at)
+                first = column_ref[2 * pair, row] ^ turn
+                second = column_ref[2 * pair + 1, row] ^ turn ^ 1
+                first = jnp.where(live_ref[2 * pair, row] == 1, first, zero_at)
+                second = jnp.where(live_ref[2 * pair + 1, row] == 1, second, zero_at)
                 lhs_ref[slot_of, inner * vectors:(inner + 1) * vectors, pair * wide:(pair + 1) * wide] = jnp.where(
                     is_low, table_ref[first], table_ref[second])
         rhs = panel_ref[pl.ds(row0, pack)].reshape(pack * height, slots * height)
@@ -197,6 +201,7 @@
         out_shape=[jax.ShapeDtypeStruct((vectors, half), BF16)] * 2,
         in_specs=[vmem(), vmem()],
         out_specs=[vmem(), vmem()],
+        compiler_params=limit(2),
         name="scale",
     )(krylov_block, degree_row)
     row_bits = bits(sources)
@@ -224,9 +229,9 @@
             pltpu.VMEM((sources * per_piece + 1, vectors, 2 * height), BF16),
             pltpu.VMEM((2, 4 * vectors, slot_width), BF16),
         ],
-        compiler_params=pltpu.CompilerParams(vmem_limit_bytes=48 << 20),
+        compiler_params=limit(12),
         name="tiles",
-    )(tile_column[:, 0], tile_live[:, 0], left, right, tile_values[:, 0])
+    )(tile_column[:, 0].T, tile_live[:, 0].T, left, right, tile_values[:, 0])
     running = keep
     received = []
     for bit in bits(groups):
@@ -245,6 +250,7 @@
         in_specs=[vmem()] * (3 + len(received)),
         out_specs=[vmem(), vmem()],
         scratch_shapes=[pltpu.VMEM((4 * vectors, owned), BF16)],
+        compiler_params=limit(4),
         name="gram",
     )(krylov_block, degree_row, keep, *received)
     for axis, size in (("col", groups), ("row", sources)):
@@ -259,6 +265,7 @@
         ],
         in_specs=[vmem(), vmem()],
         out_specs=[vmem(), vmem()],
+        compiler_params=limit(4),
         name="finish",
     )(gram, pieces)
     return (orthonormal, quotient)

time: 63.3 us -> 56.7 us (0.90)
  other arithmetic: 6.07 us -> 0.16 us
  Pallas kernels: 13.2 us -> 8.94 us
  waiting for transfers between devices: 16.7 us -> 18.7 us
  starting transfers between devices: 22.1 us -> 23.5 us
  local copies, waits for them, and re-layouts: 3.74 us -> 4.49 us
    concatenate x3, other arithmetic: 2.32 us -> 0.05 us  [on_device(): right = jnp.concatenate([right, new_right], axis=0)]
    concatenate x3, other arithmetic: 2.32 us -> 0.05 us  [on_device(): left = jnp.concatenate([left, new_left], axis=0)]
    ppermute x13, waiting for transfers between devices: 16.7 us -> 18.7 us  [swap(): return lax.ppermute(value, axis, [(i, i ^ mask) for i in range(size)])]
    pallas_call x1, Pallas kernels: 2.04 us -> 0.36 us  [on_device(): pl.pallas_call(lambda *refs: gram_kernel(len(received), *refs), out_shape...]
    pallas_call x1, Pallas kernels: 1.48 us -> 0.02 us  [on_device(): pl.pallas_call(scale_kernel, out_shape=[jax.ShapeDtypeStruct((vectors, ha...]
    add x5, other arithmetic: 1.4 us -> 0.03 us  [on_device(): gram = gram + swap(gram, axis, size, bit)]
    ppermute x13, starting transfers between devices: 22.1 us -> 23.5 us  [swap(): return lax.ppermute(value, axis, [(i, i ^ mask) for i in range(size)])]
    pallas_call x1, Pallas kernels: 7.17 us -> 6.22 us  [on_device(): pl.pallas_call(lambda *refs: finish_kernel(total_rows, *refs), out_shape=...]
  transfers between devices with their start and end apart: 13 -> 13, of which waited for: 9 -> 10; matrix products, arithmetic and copies ran while one was open for 9% -> 0% of each run, Pallas kernels for 0% -> 0%
where the time goes in v2:
time: 56.7 us; the launch traced here: 56.5 us
  starting transfers between devices  23.5 us (41%)
  waiting for transfers between devices  18.7 us (33%)
  Pallas kernels  8.94 us (16%)
  local copies, waits for them, and re-layouts  4.49 us (8%)
  between operations  0.75 us (1%)
    ppermute x13, starting transfers between devices, swap(): return lax.ppermute(value, axis, [(i, i ^ mask) for i in range(size)])  23.5 us
    ppermute x13, waiting for transfers between devices, swap(): return lax.ppermute(value, axis, [(i, i ^ mask) for i in range(size)])  18.7 us
    pallas_call x1, Pallas kernels, on_device(): pl.pallas_call(lambda *refs: finish_kernel(total_rows, *refs), out_shape=...  6.22 us
    unnamed x14, local copies, waits for them, and re-layouts  4.49 us
    pallas_call x1, Pallas kernels, on_device(): pl.pallas_call(lambda *refs: tile_kernel(sources, groups, per_piece, left...  2.34 us
  transfers between devices with their start and end apart: 13, of which 10 were waited for; matrix products, arithmetic and copies ran while one was open for 0% of the time, Pallas kernels for 0%

profile of v2, /device:TPU:0, one launch (start us, length us, event | category | flops | bytes accessed | tf_op | source)
XLA Modules:
  0.0 56.5 jit_solution(10754844139104429421)
XLA Ops:
  0.6 0.0 copy-start.1
  0.6 0.8 %copy-done.1 = bf16[64,512]{1,0:T(8,128)(2,1)S(1)} copy-done((bf16[64,512]{1,0:T(8,128)(2,1)S(1)}, bf16[64,512]{1,0:T(8,128)(2,1)}, u32[]{:S(2)}) %copy-start.1) | copy-done | bytes 65560
  1.5 0.0 copy-start.3
  1.5 0.7 %copy-done.3 = s32[512]{0:T(512)S(1)} copy-done((s32[512]{0:T(512)S(1)}, s32[512]{0:T(512)}, u32[]{:S(2)}) %copy-start.3) | copy-done | bytes 2072
  2.2 3.0 %collective-permute-start.3 = (bf16[1,64,256]{2,1,0:T(8,128)(2,1)S(1)}, bf16[1,64,256]{2,1,0:T(8,128)(2,1)S(1)}, u32[]{:S(2)}, u32[]{:S(2)}) collective-permute-start(bf16[1,64,256]{2,1,0:T(8,128)(2,1)S(1)} %bitcast.19), channel_id=1, source_target_pairs={{0,4},{4,0},{8,12},{12,8},{16,20},{20,16},{24,28},{28,24},{1,5},{5... | collective-permute-start | bytes 98312 | tf_op jit(solution)/shard_map/ppermute | solution.py:27
  5.2 2.6 %collective-permute-start = (bf16[1,64,256]{2,1,0:T(8,128)(2,1)S(1)}, bf16[1,64,256]{2,1,0:T(8,128)(2,1)S(1)}, u32[]{:S(2)}, u32[]{:S(2)}) collective-permute-start(bf16[1,64,256]{2,1,0:T(8,128)(2,1)S(1)} %bitcast.15), channel_id=1, source_target_pairs={{0,16},{4,20},{8,24},{12,28},{16,0},{20,4},{24,8},{28,12},{1,17},{... | collective-permute-start | bytes 98312 | tf_op jit(solution)/shard_map/ppermute | solution.py:27
  7.8 0.0 collective-permute-done.3
  7.8 2.5 %collective-permute-start.4 = (bf16[2,64,256]{2,1,0:T(8,128)(2,1)S(1)}, bf16[2,64,256]{2,1,0:T(8,128)(2,1)S(1)}, u32[]{:S(2)}, u32[]{:S(2)}) collective-permute-start(bf16[2,64,256]{2,1,0:T(8,128)(2,1)S(1)} %pad_maximum_fusion.5), channel_id=1, source_target_pairs={{0,16},{4,20},{8,24},{12,28},{16,0},{20,4},{24,8},{28,12},{1,17},{... | collective-permute-start | bytes 196616 | tf_op jit(solution)/shard_map/ppermute | solution.py:27
  10.3 0.0 collective-permute-done
  10.3 1.7 %collective-permute-start.1 = (bf16[2,64,256]{2,1,0:T(8,128)(2,1)S(1)}, bf16[2,64,256]{2,1,0:T(8,128)(2,1)S(1)}, u32[]{:S(2)}, u32[]{:S(2)}) collective-permute-start(bf16[2,64,256]{2,1,0:T(8,128)(2,1)S(1)} %pad_maximum_fusion.4), channel_id=1, source_target_pairs={{0,8},{4,12},{8,0},{12,4},{16,24},{20,28},{24,16},{28,20},{1,9},{5... | collective-permute-start | bytes 196616 | tf_op jit(solution)/shard_map/ppermute | solution.py:27
  12.0 1.1 %collective-permute-done.4 = bf16[2,64,256]{2,1,0:T(8,128)(2,1)S(1)} collective-permute-done((bf16[2,64,256]{2,1,0:T(8,128)(2,1)S(1)}, bf16[2,64,256]{2,1,0:T(8,128)(2,1)S(1)}, u32[]{:S(2)}, u32[]{:S(2)}) %collective-permute-start.4) | collective-permute-done | bytes 65568 | tf_op jit(solution)/shard_map/ppermute | solution.py:27
  13.1 2.1 %collective-permute-start.5 = (bf16[4,64,256]{2,1,0:T(8,128)(2,1)S(1)}, bf16[4,64,256]{2,1,0:T(8,128)(2,1)S(1)}, u32[]{:S(2)}, u32[]{:S(2)}) collective-permute-start(bf16[4,64,256]{2,1,0:T(8,128)(2,1)S(1)} %pad_maximum_fusion.3), channel_id=1, source_target_pairs={{0,8},{4,12},{8,0},{12,4},{16,24},{20,28},{24,16},{28,20},{1,9},{5... | collective-permute-start | bytes 393224 | tf_op jit(solution)/shard_map/ppermute | solution.py:27
  15.2 0.0 collective-permute-done.1
  15.2 0.0 copy-start.2
  15.3 0.0 copy-start.4
  15.3 1.6 %collective-permute-start.2 = (bf16[4,64,256]{2,1,0:T(8,128)(2,1)S(1)}, bf16[4,64,256]{2,1,0:T(8,128)(2,1)S(1)}, u32[]{:S(2)}, u32[]{:S(2)}) collective-permute-start(bf16[4,64,256]{2,1,0:T(8,128)(2,1)S(1)} %pad_maximum_fusion.2), channel_id=1, source_target_pairs={{0,4},{4,0},{8,12},{12,8},{16,20},{20,16},{24,28},{28,24},{1,5},{5... | collective-permute-start | bytes 393224 | tf_op jit(solution)/shard_map/ppermute | solution.py:27
  16.9 1.3 %collective-permute-done.5 = bf16[4,64,256]{2,1,0:T(8,128)(2,1)S(1)} collective-permute-done((bf16[4,64,256]{2,1,0:T(8,128)(2,1)S(1)}, bf16[4,64,256]{2,1,0:T(8,128)(2,1)S(1)}, u32[]{:S(2)}, u32[]{:S(2)}) %collective-permute-start.5) | collective-permute-done | bytes 131104 | tf_op jit(solution)/shard_map/ppermute | solution.py:27
  18.2 2.1 %collective-permute-done.2 = bf16[4,64,256]{2,1,0:T(8,128)(2,1)S(1)} collective-permute-done((bf16[4,64,256]{2,1,0:T(8,128)(2,1)S(1)}, bf16[4,64,256]{2,1,0:T(8,128)(2,1)S(1)}, u32[]{:S(2)}, u32[]{:S(2)}) %collective-permute-start.2) | collective-permute-done | bytes 131104 | tf_op jit(solution)/shard_map/ppermute | solution.py:27
  20.3 0.0 copy-start
  20.3 1.6 %copy-done = bf16[32,1,64,512]{3,2,1,0:T(8,128)(2,1)S(1)} copy-done((bf16[32,1,64,512]{3,2,1,0:T(8,128)(2,1)S(1)}, bf16[32,1,64,512]{3,2,1,0:T(8,128)(2,1)}, u32[]{:S(2)}) %copy-start) | copy-done | bytes 2097176
  21.9 0.0 copy-start.5
  21.9 0.7 %copy-done.5 = s32[32,1,8]{0,2,1:T(8,128)S(1)} copy-done((s32[32,1,8]{0,2,1:T(8,128)S(1)}, s32[32,1,8]{0,2,1:T(8,128)}, u32[]{:S(2)}) %copy-start.5) | copy-done | bytes 1048
  22.6 0.0 copy-start.6
  22.6 0.7 %copy-done.6 = s32[32,1,8]{0,2,1:T(8,128)S(1)} copy-done((s32[32,1,8]{0,2,1:T(8,128)S(1)}, s32[32,1,8]{0,2,1:T(8,128)}, u32[]{:S(2)}) %copy-start.6) | copy-done | bytes 1048
  23.3 2.3 %tiles.1 = (f32[2,64,512]{2,1,0:T(8,128)S(1)}, bf16[2,64,512]{2,1,0:T(8,128)(2,1)S(1)}) custom-call(s32[8,32]{1,0:T(8,128)S(1)} %bitcast.25, s32[8,32]{1,0:T(8,128)S(1)} %bitcast.26, bf16[8,64,256]{2,1,0:T(8,128)(2,1)S(1)} %pad_maximum_fusion.refs_2_, bf16[8,64,256]{2,1,0:T(8,128)(2,1)S(1)} %pad_maximum_fusion.1.refs_3_, bf16[32,64,512]{2,1,0:T(8,128)(2,1)S(1)} %bitcast.14), custom_call_target="tpu_custom_call" | custom-call | tf_op jit(solution)/shard_map/tiles/pallas_call | solution.py:220
  25.7 0.1 collective-permute-start.6
  25.7 1.3 %collective-permute-done.6.refs_3_ = bf16[2,64,512]{2,1,0:T(8,128)(2,1)S(1)} collective-permute-done((bf16[2,64,512]{2,1,0:T(8,128)(2,1)S(1)}, bf16[2,64,512]{2,1,0:T(8,128)(2,1)S(1)}, u32[]{:S(2)}, u32[]{:S(2)}) %collective-permute-start.6) | collective-permute-done | bytes 131104 | tf_op jit(solution)/shard_map/ppermute | solution.py:27
  27.1 1.6 %collective-permute-start.7 = (bf16[1,64,512]{2,1,0:T(8,128)(2,1)S(1)}, bf16[1,64,512]{2,1,0:T(8,128)(2,1)S(1)}, u32[]{:S(2)}, u32[]{:S(2)}) collective-permute-start(bf16[1,64,512]{2,1,0:T(8,128)(2,1)S(1)} %slice_bitcast_fusion), channel_id=1, source_target_pairs={{0,2},{1,3},{2,0},{3,1},{4,6},{5,7},{6,4},{7,5},{8,10},{9,11},{10,... | collective-permute-start | bytes 196616 | tf_op jit(solution)/shard_map/ppermute | solution.py:27
  28.7 2.7 %collective-permute-done.7.refs_4_ = bf16[1,64,512]{2,1,0:T(8,128)(2,1)S(1)} collective-permute-done((bf16[1,64,512]{2,1,0:T(8,128)(2,1)S(1)}, bf16[1,64,512]{2,1,0:T(8,128)(2,1)S(1)}, u32[]{:S(2)}, u32[]{:S(2)}) %collective-permute-start.7) | collective-permute-done | bytes 65568 | tf_op jit(solution)/shard_map/ppermute | solution.py:27
  31.4 0.0 copy-done.2
  31.4 0.0 copy-done.4
  31.5 0.4 gram.1
  31.8 0.1 collective-permute-start.8
  31.9 1.2 %collective-permute-done.8 = f32[64,128]{1,0:T(8,128)S(1)} collective-permute-done((f32[64,128]{1,0:T(8,128)S(1)}, f32[64,128]{1,0:T(8,128)S(1)}, u32[]{:S(2)}, u32[]{:S(2)}) %collective-permute-start.8) | collective-permute-done | bytes 32800 | tf_op jit(solution)/shard_map/ppermute | solution.py:27
  33.1 1.5 %collective-permute-start.9 = (f32[64,128]{1,0:T(8,128)S(1)}, f32[64,128]{1,0:T(8,128)S(1)}, u32[]{:S(2)}, u32[]{:S(2)}) collective-permute-start(f32[64,128]{1,0:T(8,128)S(1)} %add.19), channel_id=1, source_target_pairs={{0,2},{1,3},{2,0},{3,1},{4,6},{5,7},{6,4},{7,5},{8,10},{9,11},{10,... | collective-permute-start | bytes 98312 | tf_op jit(solution)/shard_map/ppermute | solution.py:27
  34.6 2.4 %collective-permute-done.9 = f32[64,128]{1,0:T(8,128)S(1)} collective-permute-done((f32[64,128]{1,0:T(8,128)S(1)}, f32[64,128]{1,0:T(8,128)S(1)}, u32[]{:S(2)}, u32[]{:S(2)}) %collective-permute-start.9) | collective-permute-done | bytes 32800 | tf_op jit(solution)/shard_map/ppermute | solution.py:27
  37.0 1.5 %collective-permute-start.10 = (f32[64,128]{1,0:T(8,128)S(1)}, f32[64,128]{1,0:T(8,128)S(1)}, u32[]{:S(2)}, u32[]{:S(2)}) collective-permute-start(f32[64,128]{1,0:T(8,128)S(1)} %add.20), channel_id=1, source_target_pairs={{0,4},{4,0},{8,12},{12,8},{16,20},{20,16},{24,28},{28,24},{1,5},{5... | collective-permute-start | bytes 98312 | tf_op jit(solution)/shard_map/ppermute | solution.py:27
  38.6 2.4 %collective-permute-done.10 = f32[64,128]{1,0:T(8,128)S(1)} collective-permute-done((f32[64,128]{1,0:T(8,128)S(1)}, f32[64,128]{1,0:T(8,128)S(1)}, u32[]{:S(2)}, u32[]{:S(2)}) %collective-permute-start.10) | collective-permute-done | bytes 32800 | tf_op jit(solution)/shard_map/ppermute | solution.py:27
  40.9 1.7 %collective-permute-start.11 = (f32[64,128]{1,0:T(8,128)S(1)}, f32[64,128]{1,0:T(8,128)S(1)}, u32[]{:S(2)}, u32[]{:S(2)}) collective-permute-start(f32[64,128]{1,0:T(8,128)S(1)} %add.21), channel_id=1, source_target_pairs={{0,8},{4,12},{8,0},{12,4},{16,24},{20,28},{24,16},{28,20},{1,9},{5... | collective-permute-start | bytes 98312 | tf_op jit(solution)/shard_map/ppermute | solution.py:27
  42.7 2.2 %collective-permute-done.11 = f32[64,128]{1,0:T(8,128)S(1)} collective-permute-done((f32[64,128]{1,0:T(8,128)S(1)}, f32[64,128]{1,0:T(8,128)S(1)}, u32[]{:S(2)}, u32[]{:S(2)}) %collective-permute-start.11) | collective-permute-done | bytes 32800 | tf_op jit(solution)/shard_map/ppermute | solution.py:27
  44.9 3.5 %collective-permute-start.12 = (f32[64,128]{1,0:T(8,128)S(1)}, f32[64,128]{1,0:T(8,128)S(1)}, u32[]{:S(2)}, u32[]{:S(2)}) collective-permute-start(f32[64,128]{1,0:T(8,128)S(1)} %add.22), channel_id=1, source_target_pairs={{0,16},{4,20},{8,24},{12,28},{16,0},{20,4},{24,8},{28,12},{1,17},{... | collective-permute-start | bytes 98312 | tf_op jit(solution)/shard_map/ppermute | solution.py:27
  48.3 1.9 %collective-permute-done.12 = f32[64,128]{1,0:T(8,128)S(1)} collective-permute-done((f32[64,128]{1,0:T(8,128)S(1)}, f32[64,128]{1,0:T(8,128)S(1)}, u32[]{:S(2)}, u32[]{:S(2)}) %collective-permute-start.12) | collective-permute-done | bytes 32800 | tf_op jit(solution)/shard_map/ppermute | solution.py:27
  50.2 6.2 %finish.1 = (f32[64,512]{1,0:T(8,128)}, f32[64,64]{1,0:T(8,128)}) custom-call(f32[64,128]{1,0:T(8,128)S(1)} %add.23.refs_0_, bf16[192,512]{1,0:T(8,128)(2,1)S(1)} %get-tuple-element.13.refs_1_), custom_call_target="tpu_custom_call" | custom-call | tf_op jit(solution)/shard_map/finish/pallas_call | solution.py:260
  (14 shorter events, 0.2 us)
Async XLA Ops:
  0.6 0.8 %copy-start.1 = (bf16[64,512]{1,0:T(8,128)(2,1)S(1)}, bf16[64,512]{1,0:T(8,128)(2,1)}, u32[]{:S(2)}) copy-start(bf16[64,512]{1,0:T(8,128)(2,1)} %refs_0_.1) | copy-start | bytes 196612
  1.5 0.7 %copy-start.3 = (s32[512]{0:T(512)S(1)}, s32[512]{0:T(512)}, u32[]{:S(2)}) copy-start(s32[512]{0:T(512)} %param.6) | copy-start | bytes 6148
  2.2 5.6 %collective-permute-start.3 = (bf16[1,64,256]{2,1,0:T(8,128)(2,1)S(1)}, bf16[1,64,256]{2,1,0:T(8,128)(2,1)S(1)}, u32[]{:S(2)}, u32[]{:S(2)}) collective-permute-start(bf16[1,64,256]{2,1,0:T(8,128)(2,1)S(1)} %bitcast.19), channel_id=1, source_target_pairs={{0,4},{4,0},{8,12},{12,8},{16,20},{20,16},{24,28},{28,24},{1,5},{5... | collective-permute-start | bytes 98312 | tf_op jit(solution)/shard_map/ppermute | solution.py:27
  5.2 5.1 %collective-permute-start = (bf16[1,64,256]{2,1,0:T(8,128)(2,1)S(1)}, bf16[1,64,256]{2,1,0:T(8,128)(2,1)S(1)}, u32[]{:S(2)}, u32[]{:S(2)}) collective-permute-start(bf16[1,64,256]{2,1,0:T(8,128)(2,1)S(1)} %bitcast.15), channel_id=1, source_target_pairs={{0,16},{4,20},{8,24},{12,28},{16,0},{20,4},{24,8},{28,12},{1,17},{... | collective-permute-start | bytes 98312 | tf_op jit(solution)/shard_map/ppermute | solution.py:27
  7.8 5.3 %collective-permute-start.4 = (bf16[2,64,256]{2,1,0:T(8,128)(2,1)S(1)}, bf16[2,64,256]{2,1,0:T(8,128)(2,1)S(1)}, u32[]{:S(2)}, u32[]{:S(2)}) collective-permute-start(bf16[2,64,256]{2,1,0:T(8,128)(2,1)S(1)} %pad_maximum_fusion.5), channel_id=1, source_target_pairs={{0,16},{4,20},{8,24},{12,28},{16,0},{20,4},{24,8},{28,12},{1,17},{... | collective-permute-start | bytes 196616 | tf_op jit(solution)/shard_map/ppermute | solution.py:27
  10.3 4.9 %collective-permute-start.1 = (bf16[2,64,256]{2,1,0:T(8,128)(2,1)S(1)}, bf16[2,64,256]{2,1,0:T(8,128)(2,1)S(1)}, u32[]{:S(2)}, u32[]{:S(2)}) collective-permute-start(bf16[2,64,256]{2,1,0:T(8,128)(2,1)S(1)} %pad_maximum_fusion.4), channel_id=1, source_target_pairs={{0,8},{4,12},{8,0},{12,4},{16,24},{20,28},{24,16},{28,20},{1,9},{5... | collective-permute-start | bytes 196616 | tf_op jit(solution)/shard_map/ppermute | solution.py:27
  13.1 5.1 %collective-permute-start.5 = (bf16[4,64,256]{2,1,0:T(8,128)(2,1)S(1)}, bf16[4,64,256]{2,1,0:T(8,128)(2,1)S(1)}, u32[]{:S(2)}, u32[]{:S(2)}) collective-permute-start(bf16[4,64,256]{2,1,0:T(8,128)(2,1)S(1)} %pad_maximum_fusion.3), channel_id=1, source_target_pairs={{0,8},{4,12},{8,0},{12,4},{16,24},{20,28},{24,16},{28,20},{1,9},{5... | collective-permute-start | bytes 393224 | tf_op jit(solution)/shard_map/ppermute | solution.py:27
  15.2 16.2 %copy-start.2 = (bf16[64,512]{1,0:T(8,128)(2,1)S(1)}, bf16[64,512]{1,0:T(8,128)(2,1)}, u32[]{:S(2)}) copy-start(bf16[64,512]{1,0:T(8,128)(2,1)} %refs_0_.1) | copy-start | bytes 196612
  15.3 16.2 %copy-start.4 = (s32[512]{0:T(512)S(1)}, s32[512]{0:T(512)}, u32[]{:S(2)}) copy-start(s32[512]{0:T(512)} %param.6) | copy-start | bytes 6148
  15.3 5.0 %collective-permute-start.2 = (bf16[4,64,256]{2,1,0:T(8,128)(2,1)S(1)}, bf16[4,64,256]{2,1,0:T(8,128)(2,1)S(1)}, u32[]{:S(2)}, u32[]{:S(2)}) collective-permute-start(bf16[4,64,256]{2,1,0:T(8,128)(2,1)S(1)} %pad_maximum_fusion.2), channel_id=1, source_target_pairs={{0,4},{4,0},{8,12},{12,8},{16,20},{20,16},{24,28},{28,24},{1,5},{5... | collective-permute-start | bytes 393224 | tf_op jit(solution)/shard_map/ppermute | solution.py:27
  20.3 1.6 %copy-start = (bf16[32,1,64,512]{3,2,1,0:T(8,128)(2,1)S(1)}, bf16[32,1,64,512]{3,2,1,0:T(8,128)(2,1)}, u32[]{:S(2)}) copy-start(bf16[32,1,64,512]{3,2,1,0:T(8,128)(2,1)} %param.7) | copy-start | bytes 6291460
  21.9 0.7 %copy-start.5 = (s32[32,1,8]{0,2,1:T(8,128)S(1)}, s32[32,1,8]{0,2,1:T(8,128)}, u32[]{:S(2)}) copy-start(s32[32,1,8]{0,2,1:T(8,128)} %param.8) | copy-start | bytes 3076
  22.6 0.7 %copy-start.6 = (s32[32,1,8]{0,2,1:T(8,128)S(1)}, s32[32,1,8]{0,2,1:T(8,128)}, u32[]{:S(2)}) copy-start(s32[32,1,8]{0,2,1:T(8,128)} %param.9) | copy-start | bytes 3076
  25.7 1.4 %collective-permute-start.6 = (bf16[2,64,512]{2,1,0:T(8,128)(2,1)S(1)}, bf16[2,64,512]{2,1,0:T(8,128)(2,1)S(1)}, u32[]{:S(2)}, u32[]{:S(2)}) collective-permute-start(bf16[2,64,512]{2,1,0:T(8,128)(2,1)S(1)} %get-tuple-element.11), channel_id=1, source_target_pairs={{0,1},{1,0},{2,3},{3,2},{4,5},{5,4},{6,7},{7,6},{8,9},{9,8},{10,11... | collective-permute-start | bytes 393224 | tf_op jit(solution)/shard_map/ppermute | solution.py:27
  27.1 4.3 %collective-permute-start.7 = (bf16[1,64,512]{2,1,0:T(8,128)(2,1)S(1)}, bf16[1,64,512]{2,1,0:T(8,128)(2,1)S(1)}, u32[]{:S(2)}, u32[]{:S(2)}) collective-permute-start(bf16[1,64,512]{2,1,0:T(8,128)(2,1)S(1)} %slice_bitcast_fusion), channel_id=1, source_target_pairs={{0,2},{1,3},{2,0},{3,1},{4,6},{5,7},{6,4},{7,5},{8,10},{9,11},{10,... | collective-permute-start | bytes 196616 | tf_op jit(solution)/shard_map/ppermute | solution.py:27
  31.8 1.3 %collective-permute-start.8 = (f32[64,128]{1,0:T(8,128)S(1)}, f32[64,128]{1,0:T(8,128)S(1)}, u32[]{:S(2)}, u32[]{:S(2)}) collective-permute-start(f32[64,128]{1,0:T(8,128)S(1)} %get-tuple-element.12), channel_id=1, source_target_pairs={{0,1},{1,0},{2,3},{3,2},{4,5},{5,4},{6,7},{7,6},{8,9},{9,8},{10,11... | collective-permute-start | bytes 98312 | tf_op jit(solution)/shard_map/ppermute | solution.py:27
  33.1 3.9 %collective-permute-start.9 = (f32[64,128]{1,0:T(8,128)S(1)}, f32[64,128]{1,0:T(8,128)S(1)}, u32[]{:S(2)}, u32[]{:S(2)}) collective-permute-start(f32[64,128]{1,0:T(8,128)S(1)} %add.19), channel_id=1, source_target_pairs={{0,2},{1,3},{2,0},{3,1},{4,6},{5,7},{6,4},{7,5},{8,10},{9,11},{10,... | collective-permute-start | bytes 98312 | tf_op jit(solution)/shard_map/ppermute | solution.py:27
  37.0 3.9 %collective-permute-start.10 = (f32[64,128]{1,0:T(8,128)S(1)}, f32[64,128]{1,0:T(8,128)S(1)}, u32[]{:S(2)}, u32[]{:S(2)}) collective-permute-start(f32[64,128]{1,0:T(8,128)S(1)} %add.20), channel_id=1, source_target_pairs={{0,4},{4,0},{8,12},{12,8},{16,20},{20,16},{24,28},{28,24},{1,5},{5... | collective-permute-start | bytes 98312 | tf_op jit(solution)/shard_map/ppermute | solution.py:27
  40.9 3.9 %collective-permute-start.11 = (f32[64,128]{1,0:T(8,128)S(1)}, f32[64,128]{1,0:T(8,128)S(1)}, u32[]{:S(2)}, u32[]{:S(2)}) collective-permute-start(f32[64,128]{1,0:T(8,128)S(1)} %add.21), channel_id=1, source_target_pairs={{0,8},{4,12},{8,0},{12,4},{16,24},{20,28},{24,16},{28,20},{1,9},{5... | collective-permute-start | bytes 98312 | tf_op jit(solution)/shard_map/ppermute | solution.py:27
  44.9 5.4 %collective-permute-start.12 = (f32[64,128]{1,0:T(8,128)S(1)}, f32[64,128]{1,0:T(8,128)S(1)}, u32[]{:S(2)}, u32[]{:S(2)}) collective-permute-start(f32[64,128]{1,0:T(8,128)S(1)} %add.22), channel_id=1, source_target_pairs={{0,16},{4,20},{8,24},{12,28},{16,0},{20,4},{24,8},{28,12},{1,17},{... | collective-permute-start | bytes 98312 | tf_op jit(solution)/shard_map/ppermute | solution.py:27

commit v3 on v2

--- a/solution.py
+++ b/solution.py
@@ -15,6 +15,10 @@
     return pltpu.CompilerParams(vmem_limit_bytes=mib << 20)
 
 
+def hbm(value):
+    return pltpu.with_memory_space_constraint(value, pltpu.HBM)
+
+
 def vmem():
     return pl.BlockSpec(memory_space=pltpu.VMEM)
 
@@ -23,8 +27,10 @@
     return pl.BlockSpec(memory_space=pltpu.SMEM)
 
 
-def swap(value, axis, size, mask):
-    return lax.ppermute(value, axis, [(i, i ^ mask) for i in range(size)])
+def swap(value, row_mask, col_mask):
+    rows, cols = lax.axis_size("row"), lax.axis_size("col")
+    pairs = [(r * cols + c, (r ^ row_mask) * cols + (c ^ col_mask)) for r in range(rows) for c in range(cols)]
+    return lax.ppermute(value, ("row", "col"), pairs)
 
 
 def bits(size):
@@ -52,15 +58,31 @@
     right_ref[...] = scaled[:, half:]
 
 
-def tile_kernel(sources, groups, per_piece, left_order, right_order, column_ref, live_ref, left_ref, right_ref,
+def load_kernel(per_piece, zero_at, column_in, live_in, panel_in, index_ref, panel_ref, column_ref, live_ref, sem):
+    copies = [
+        pltpu.make_async_copy(column_in, column_ref, sem.at[0]),
+        pltpu.make_async_copy(live_in, live_ref, sem.at[1]),
+        pltpu.make_async_copy(panel_in, panel_ref, sem.at[2]),
+    ]
+    for copy in copies:
+        copy.start()
+    copies[0].wait()
+    copies[1].wait()
+    column = column_ref[...] ^ (lax.axis_index("row") * per_piece)
+    slot = lax.broadcasted_iota(jnp.int32, column.shape, 0)
+    column = column ^ (slot & 1)
+    index_ref[...] = jnp.where(live_ref[...] == 1, column, zero_at)
+    copies[2].wait()
+
+
+def tile_kernel(sources, groups, per_piece, left_order, right_order, index_ref, left_ref, right_ref,
                 panel_ref, keep_ref, send_ref, table_ref, lhs_ref):
     vectors = left_ref.shape[1]
     half = left_ref.shape[2]
     height = panel_ref.shape[1]
-    slots = column_ref.shape[0]
+    slots = index_ref.shape[0]
     wide = 2 * height
     pairs = half // wide
-    my_row = lax.axis_index("row")
     my_col = lax.axis_index("col")
     zero_at = sources * per_piece
     for side, order, ref in ((0, left_order, left_ref), (1, right_order, right_ref)):
@@ -73,19 +95,20 @@
     table_ref[zero_at] = jnp.zeros((vectors, wide), BF16)
     lane = lax.broadcasted_iota(jnp.int32, (vectors, wide), 1)
     is_low = lane < height
-    turn = my_row * per_piece
     pack = 4
     chunks = per_piece // pack
 
-    def group(piece_at, chunk, slot_of):
-        row0 = (piece_at ^ my_col) * per_piece + chunk * pack
+    def group(step, chunk, slot_of):
+        partner = step & ~1
+        flips = step & 1
+        for bit in bits(groups)[1:]:
+            flips = flips ^ ((step // bit) & 1)
+        row0 = ((partner | flips) ^ my_col) * per_piece + chunk * pack
         for inner in range(pack):
             row = row0 + inner
             for pair in range(slots // 2):
-                first = column_ref[2 * pair, row] ^ turn
-                second = column_ref[2 * pair + 1, row] ^ turn ^ 1
-                first = jnp.where(live_ref[2 * pair, row] == 1, first, zero_at)
-                second = jnp.where(live_ref[2 * pair + 1, row] == 1, second, zero_at)
+                first = index_ref[2 * pair, row]
+                second = index_ref[2 * pair + 1, row]
                 lhs_ref[slot_of, inner * vectors:(inner + 1) * vectors, pair * wide:(pair + 1) * wide] = jnp.where(
                     is_low, table_ref[first], table_ref[second])
         rhs = panel_ref[pl.ds(row0, pack)].reshape(pack * height, slots * height)
@@ -203,15 +226,32 @@
         out_specs=[vmem(), vmem()],
         compiler_params=limit(2),
         name="scale",
-    )(krylov_block, degree_row)
+    )(hbm(krylov_block), hbm(degree_row))
+    slots = tile_column.shape[2]
+    index, panel = pl.pallas_call(
+        lambda *refs: load_kernel(per_piece, sources * per_piece, *refs),
+        out_shape=[
+            jax.ShapeDtypeStruct((slots, block_rows), jnp.int32),
+            jax.ShapeDtypeStruct((block_rows, height, slot_width), BF16),
+        ],
+        in_specs=[pl.BlockSpec(memory_space=pl.ANY)] * 3,
+        out_specs=[vmem(), vmem()],
+        scratch_shapes=[
+            pltpu.VMEM((slots, block_rows), jnp.int32),
+            pltpu.VMEM((slots, block_rows), jnp.int32),
+            pltpu.SemaphoreType.DMA((3,)),
+        ],
+        compiler_params=limit(2),
+        name="load",
+    )(hbm(tile_column[:, 0].T), hbm(tile_live[:, 0].T), hbm(tile_values[:, 0]))
     row_bits = bits(sources)
     left_bits = row_bits[:0:-1] + row_bits[:1]
     right_bits = row_bits[:1] + row_bits[:0:-1]
     left, right = left[None], right[None]
     left_order, right_order = [0], [0]
     for left_bit, right_bit in zip(left_bits, right_bits):
-        new_left = swap(left, "row", sources, left_bit)
-        new_right = swap(right, "row", sources, right_bit)
+        new_left = swap(left, left_bit, 0)
+        new_right = swap(right, right_bit, 0)
         left = jnp.concatenate([left, new_left], axis=0)
         right = jnp.concatenate([right, new_right], axis=0)
         left_order = left_order + [at ^ left_bit for at in left_order]
@@ -223,7 +263,7 @@
             jax.ShapeDtypeStruct((many, vectors, owned), F32),
             jax.ShapeDtypeStruct((many, vectors, owned), BF16),
         ],
-        in_specs=[smem(), smem(), vmem(), vmem(), vmem()],
+        in_specs=[smem(), vmem(), vmem(), vmem()],
         out_specs=[vmem(), vmem()],
         scratch_shapes=[
             pltpu.VMEM((sources * per_piece + 1, vectors, 2 * height), BF16),
@@ -231,11 +271,11 @@
         ],
         compiler_params=limit(12),
         name="tiles",
-    )(tile_column[:, 0].T, tile_live[:, 0].T, left, right, tile_values[:, 0])
+    )(index, left, right, panel)
     running = keep
     received = []
     for bit in bits(groups):
-        got = swap(send, "col", groups, bit)
+        got = swap(send, 0, bit | 1)
         received.append(got)
         if running.shape[0] > 1:
             summed = running + got.astype(F32)
@@ -253,9 +293,10 @@
         compiler_params=limit(4),
         name="gram",
     )(krylov_block, degree_row, keep, *received)
-    for axis, size in (("col", groups), ("row", sources)):
-        for bit in bits(size):
-            gram = gram + swap(gram, axis, size, bit)
+    for bit in bits(groups):
+        gram = gram + swap(gram, 0, bit | 1)
+    for bit in bits(sources):
+        gram = gram + swap(gram, bit, 1)
     total_rows = sources * groups * owned
     orthonormal, quotient = pl.pallas_call(
         lambda *refs: finish_kernel(total_rows, *refs),

time: 56.7 us -> 50.3 us (0.89)
  local copies, waits for them, and re-layouts: 4.49 us -> 0.02 us
  waiting for transfers between devices: 18.7 us -> 15.6 us
  Pallas kernels: 8.94 us -> 11.3 us
  starting transfers between devices: 23.5 us -> 22.4 us
    unnamed x14 -> x4, local copies, waits for them, and re-layouts: 4.49 us -> 0.01 us
    ppermute x13, waiting for transfers between devices: 18.7 us -> 15.6 us  [swap(): return lax.ppermute(value, ('row', 'col'), pairs)]
    pallas_call x0 -> x1, Pallas kernels: none -> 1.65 us  [on_device(): pl.pallas_call(lambda *refs: load_kernel(per_piece, sources * per_piece,...]
    ppermute x13, starting transfers between devices: 23.5 us -> 22.4 us  [swap(): return lax.ppermute(value, ('row', 'col'), pairs)]
    pallas_call x1, Pallas kernels: 0.02 us -> 0.86 us  [on_device(): pl.pallas_call(scale_kernel, out_shape=[jax.ShapeDtypeStruct((vectors, ha...]
  transfers between devices with their start and end apart: 13 -> 13, of which waited for: 10 -> 9; matrix products, arithmetic and copies ran while one was open for 0% -> 0% of each run, Pallas kernels for 0% -> 3%
where the time goes in v3:
time: 50.3 us; the launch traced here: 50.1 us
  starting transfers between devices  22.4 us (45%)
  waiting for transfers between devices  15.6 us (31%)
  Pallas kernels  11.3 us (22%)
  between operations  0.74 us (1%)
    ppermute x13, starting transfers between devices, swap(): return lax.ppermute(value, ('row', 'col'), pairs)  22.4 us
    ppermute x13, waiting for transfers between devices, swap(): return lax.ppermute(value, ('row', 'col'), pairs)  15.6 us
    pallas_call x1, Pallas kernels, on_device(): pl.pallas_call(lambda *refs: finish_kernel(total_rows, *refs), out_shape=...  6.22 us
    pallas_call x1, Pallas kernels, on_device(): pl.pallas_call(lambda *refs: tile_kernel(sources, groups, per_piece, left...  2.17 us
    pallas_call x1, Pallas kernels, on_device(): pl.pallas_call(lambda *refs: load_kernel(per_piece, sources * per_piece,...  1.65 us
  transfers between devices with their start and end apart: 13, of which 9 were waited for; matrix products, arithmetic and copies ran while one was open for 0% of the time, Pallas kernels for 3%

profile of v3, /device:TPU:0, one launch (start us, length us, event | category | flops | bytes accessed | tf_op | source)
XLA Modules:
  0.0 50.1 jit_solution(3158188251642612142)
XLA Ops:
  0.6 0.9 %scale.1 = (bf16[64,256]{1,0:T(8,128)(2,1)S(1)}, bf16[64,256]{1,0:T(8,128)(2,1)S(1)}) custom-call(bf16[64,512]{1,0:T(8,128)(2,1)} %refs_0_.1, s32[1,512]{1,0:T(1,128)} %bitcast.22), custom_call_target="tpu_custom_call" | custom-call | tf_op jit(solution)/shard_map/scale/pallas_call | solution.py:222
  1.5 3.0 %collective-permute-start.3 = (bf16[1,64,256]{2,1,0:T(8,128)(2,1)S(1)}, bf16[1,64,256]{2,1,0:T(8,128)(2,1)S(1)}, u32[]{:S(2)}, u32[]{:S(2)}) collective-permute-start(bf16[1,64,256]{2,1,0:T(8,128)(2,1)S(1)} %bitcast.18), channel_id=1, source_target_pairs={{0,4},{1,5},{2,6},{3,7},{4,0},{5,1},{6,2},{7,3},{8,12},{9,13},{10,... | collective-permute-start | bytes 98312 | tf_op jit(solution)/shard_map/ppermute | solution.py:33
  4.5 2.6 %collective-permute-start = (bf16[1,64,256]{2,1,0:T(8,128)(2,1)S(1)}, bf16[1,64,256]{2,1,0:T(8,128)(2,1)S(1)}, u32[]{:S(2)}, u32[]{:S(2)}) collective-permute-start(bf16[1,64,256]{2,1,0:T(8,128)(2,1)S(1)} %bitcast.14), channel_id=1, source_target_pairs={{0,16},{1,17},{2,18},{3,19},{4,20},{5,21},{6,22},{7,23},{8,24},{9,... | collective-permute-start | bytes 98312 | tf_op jit(solution)/shard_map/ppermute | solution.py:33
  7.1 0.0 collective-permute-done.3
  7.1 2.5 %collective-permute-start.4 = (bf16[2,64,256]{2,1,0:T(8,128)(2,1)S(1)}, bf16[2,64,256]{2,1,0:T(8,128)(2,1)S(1)}, u32[]{:S(2)}, u32[]{:S(2)}) collective-permute-start(bf16[2,64,256]{2,1,0:T(8,128)(2,1)S(1)} %pad_maximum_fusion.5), channel_id=1, source_target_pairs={{0,16},{1,17},{2,18},{3,19},{4,20},{5,21},{6,22},{7,23},{8,24},{9,... | collective-permute-start | bytes 196616 | tf_op jit(solution)/shard_map/ppermute | solution.py:33
  9.6 0.0 collective-permute-done
  9.6 1.7 %collective-permute-start.1 = (bf16[2,64,256]{2,1,0:T(8,128)(2,1)S(1)}, bf16[2,64,256]{2,1,0:T(8,128)(2,1)S(1)}, u32[]{:S(2)}, u32[]{:S(2)}) collective-permute-start(bf16[2,64,256]{2,1,0:T(8,128)(2,1)S(1)} %pad_maximum_fusion.4), channel_id=1, source_target_pairs={{0,8},{1,9},{2,10},{3,11},{4,12},{5,13},{6,14},{7,15},{8,0},{9,1},... | collective-permute-start | bytes 196616 | tf_op jit(solution)/shard_map/ppermute | solution.py:33
  11.3 1.1 %collective-permute-done.4 = bf16[2,64,256]{2,1,0:T(8,128)(2,1)S(1)} collective-permute-done((bf16[2,64,256]{2,1,0:T(8,128)(2,1)S(1)}, bf16[2,64,256]{2,1,0:T(8,128)(2,1)S(1)}, u32[]{:S(2)}, u32[]{:S(2)}) %collective-permute-start.4) | collective-permute-done | bytes 65568 | tf_op jit(solution)/shard_map/ppermute | solution.py:33
  12.4 2.1 %collective-permute-start.5 = (bf16[4,64,256]{2,1,0:T(8,128)(2,1)S(1)}, bf16[4,64,256]{2,1,0:T(8,128)(2,1)S(1)}, u32[]{:S(2)}, u32[]{:S(2)}) collective-permute-start(bf16[4,64,256]{2,1,0:T(8,128)(2,1)S(1)} %pad_maximum_fusion.3), channel_id=1, source_target_pairs={{0,8},{1,9},{2,10},{3,11},{4,12},{5,13},{6,14},{7,15},{8,0},{9,1},... | collective-permute-start | bytes 393224 | tf_op jit(solution)/shard_map/ppermute | solution.py:33
  14.5 0.0 collective-permute-done.1
  14.6 1.6 %collective-permute-start.2 = (bf16[4,64,256]{2,1,0:T(8,128)(2,1)S(1)}, bf16[4,64,256]{2,1,0:T(8,128)(2,1)S(1)}, u32[]{:S(2)}, u32[]{:S(2)}) collective-permute-start(bf16[4,64,256]{2,1,0:T(8,128)(2,1)S(1)} %pad_maximum_fusion.2), channel_id=1, source_target_pairs={{0,4},{1,5},{2,6},{3,7},{4,0},{5,1},{6,2},{7,3},{8,12},{9,13},{10,... | collective-permute-start | bytes 393224 | tf_op jit(solution)/shard_map/ppermute | solution.py:33
  16.2 1.6 %load.1 = (s32[8,32]{1,0:T(8,128)S(1)}, bf16[32,64,512]{2,1,0:T(8,128)(2,1)S(1)}) custom-call(s32[8,32]{1,0:T(8,128)} %bitcast.25, s32[8,32]{1,0:T(8,128)} %bitcast.26, bf16[32,64,512]{2,1,0:T(8,128)(2,1)} %bitcast.24), custom_call_target="tpu_custom_call" | custom-call | tf_op jit(solution)/shard_map/load/pallas_call | solution.py:231
  17.8 0.0 copy-start
  17.8 0.0 copy-start.1
  17.8 0.0 collective-permute-done.5
  17.9 1.7 %collective-permute-done.2 = bf16[4,64,256]{2,1,0:T(8,128)(2,1)S(1)} collective-permute-done((bf16[4,64,256]{2,1,0:T(8,128)(2,1)S(1)}, bf16[4,64,256]{2,1,0:T(8,128)(2,1)S(1)}, u32[]{:S(2)}, u32[]{:S(2)}) %collective-permute-start.2) | collective-permute-done | bytes 131104 | tf_op jit(solution)/shard_map/ppermute | solution.py:33
  19.6 2.2 %tiles.1 = (f32[2,64,512]{2,1,0:T(8,128)S(1)}, bf16[2,64,512]{2,1,0:T(8,128)(2,1)S(1)}) custom-call(s32[8,32]{1,0:T(8,128)S(1)} %get-tuple-element.10.refs_0_, bf16[8,64,256]{2,1,0:T(8,128)(2,1)S(1)} %pad_maximum_fusion.refs_1_, bf16[8,64,256]{2,1,0:T(8,128)(2,1)S(1)} %pad_maximum_fusion.1.refs_2_, bf16[32,64,512]{2,1,0:T(8,128)(2,1)S(1)} %get-tuple-element.13.refs_3_), custom_call_target="tpu_custom_call" | custom-call | tf_op jit(solution)/shard_map/tiles/pallas_call | solution.py:260
  21.8 0.1 collective-permute-start.6
  21.9 1.3 %collective-permute-done.6.refs_3_ = bf16[2,64,512]{2,1,0:T(8,128)(2,1)S(1)} collective-permute-done((bf16[2,64,512]{2,1,0:T(8,128)(2,1)S(1)}, bf16[2,64,512]{2,1,0:T(8,128)(2,1)S(1)}, u32[]{:S(2)}, u32[]{:S(2)}) %collective-permute-start.6) | collective-permute-done | bytes 131104 | tf_op jit(solution)/shard_map/ppermute | solution.py:33
  23.3 1.3 %collective-permute-start.7 = (bf16[1,64,512]{2,1,0:T(8,128)(2,1)S(1)}, bf16[1,64,512]{2,1,0:T(8,128)(2,1)S(1)}, u32[]{:S(2)}, u32[]{:S(2)}) collective-permute-start(bf16[1,64,512]{2,1,0:T(8,128)(2,1)S(1)} %slice_bitcast_fusion), channel_id=1, source_target_pairs={{0,3},{1,2},{2,1},{3,0},{4,7},{5,6},{6,5},{7,4},{8,11},{9,10},{10,... | collective-permute-start | bytes 196616 | tf_op jit(solution)/shard_map/ppermute | solution.py:33
  24.6 2.8 %collective-permute-done.7.refs_4_ = bf16[1,64,512]{2,1,0:T(8,128)(2,1)S(1)} collective-permute-done((bf16[1,64,512]{2,1,0:T(8,128)(2,1)S(1)}, bf16[1,64,512]{2,1,0:T(8,128)(2,1)S(1)}, u32[]{:S(2)}, u32[]{:S(2)}) %collective-permute-start.7) | collective-permute-done | bytes 65568 | tf_op jit(solution)/shard_map/ppermute | solution.py:33
  27.4 0.0 copy-done
  27.4 0.0 copy-done.1
  27.4 0.4 gram.1
  27.8 0.2 collective-permute-start.8
  28.0 1.1 %collective-permute-done.8 = f32[64,128]{1,0:T(8,128)S(1)} collective-permute-done((f32[64,128]{1,0:T(8,128)S(1)}, f32[64,128]{1,0:T(8,128)S(1)}, u32[]{:S(2)}, u32[]{:S(2)}) %collective-permute-start.8) | collective-permute-done | bytes 32800 | tf_op jit(solution)/shard_map/ppermute | solution.py:33
  29.0 1.3 %collective-permute-start.9 = (f32[64,128]{1,0:T(8,128)S(1)}, f32[64,128]{1,0:T(8,128)S(1)}, u32[]{:S(2)}, u32[]{:S(2)}) collective-permute-start(f32[64,128]{1,0:T(8,128)S(1)} %add.19), channel_id=1, source_target_pairs={{0,3},{1,2},{2,1},{3,0},{4,7},{5,6},{6,5},{7,4},{8,11},{9,10},{10,... | collective-permute-start | bytes 98312 | tf_op jit(solution)/shard_map/ppermute | solution.py:33
  30.3 2.1 %collective-permute-done.9 = f32[64,128]{1,0:T(8,128)S(1)} collective-permute-done((f32[64,128]{1,0:T(8,128)S(1)}, f32[64,128]{1,0:T(8,128)S(1)}, u32[]{:S(2)}, u32[]{:S(2)}) %collective-permute-start.9) | collective-permute-done | bytes 32800 | tf_op jit(solution)/shard_map/ppermute | solution.py:33
  32.4 1.3 %collective-permute-start.10 = (f32[64,128]{1,0:T(8,128)S(1)}, f32[64,128]{1,0:T(8,128)S(1)}, u32[]{:S(2)}, u32[]{:S(2)}) collective-permute-start(f32[64,128]{1,0:T(8,128)S(1)} %add.20), channel_id=1, source_target_pairs={{0,5},{1,4},{2,7},{3,6},{4,1},{5,0},{6,3},{7,2},{8,13},{9,12},{10,... | collective-permute-start | bytes 98312 | tf_op jit(solution)/shard_map/ppermute | solution.py:33
  33.7 2.0 %collective-permute-done.10 = f32[64,128]{1,0:T(8,128)S(1)} collective-permute-done((f32[64,128]{1,0:T(8,128)S(1)}, f32[64,128]{1,0:T(8,128)S(1)}, u32[]{:S(2)}, u32[]{:S(2)}) %collective-permute-start.10) | collective-permute-done | bytes 32800 | tf_op jit(solution)/shard_map/ppermute | solution.py:33
  35.7 1.5 %collective-permute-start.11 = (f32[64,128]{1,0:T(8,128)S(1)}, f32[64,128]{1,0:T(8,128)S(1)}, u32[]{:S(2)}, u32[]{:S(2)}) collective-permute-start(f32[64,128]{1,0:T(8,128)S(1)} %add.21), channel_id=1, source_target_pairs={{0,9},{1,8},{2,11},{3,10},{4,13},{5,12},{6,15},{7,14},{8,1},{9,0},... | collective-permute-start | bytes 98312 | tf_op jit(solution)/shard_map/ppermute | solution.py:33
  37.2 1.9 %collective-permute-done.11 = f32[64,128]{1,0:T(8,128)S(1)} collective-permute-done((f32[64,128]{1,0:T(8,128)S(1)}, f32[64,128]{1,0:T(8,128)S(1)}, u32[]{:S(2)}, u32[]{:S(2)}) %collective-permute-start.11) | collective-permute-done | bytes 32800 | tf_op jit(solution)/shard_map/ppermute | solution.py:33
  39.1 3.2 %collective-permute-start.12 = (f32[64,128]{1,0:T(8,128)S(1)}, f32[64,128]{1,0:T(8,128)S(1)}, u32[]{:S(2)}, u32[]{:S(2)}) collective-permute-start(f32[64,128]{1,0:T(8,128)S(1)} %add.22), channel_id=1, source_target_pairs={{0,17},{1,16},{2,19},{3,18},{4,21},{5,20},{6,23},{7,22},{8,25},{9,... | collective-permute-start | bytes 98312 | tf_op jit(solution)/shard_map/ppermute | solution.py:33
  42.3 1.6 %collective-permute-done.12 = f32[64,128]{1,0:T(8,128)S(1)} collective-permute-done((f32[64,128]{1,0:T(8,128)S(1)}, f32[64,128]{1,0:T(8,128)S(1)}, u32[]{:S(2)}, u32[]{:S(2)}) %collective-permute-start.12) | collective-permute-done | bytes 32800 | tf_op jit(solution)/shard_map/ppermute | solution.py:33
  43.9 6.2 %finish.1 = (f32[64,512]{1,0:T(8,128)}, f32[64,64]{1,0:T(8,128)}) custom-call(f32[64,128]{1,0:T(8,128)S(1)} %add.23.refs_0_, bf16[192,512]{1,0:T(8,128)(2,1)S(1)} %get-tuple-element.17.refs_1_), custom_call_target="tpu_custom_call" | custom-call | tf_op jit(solution)/shard_map/finish/pallas_call | solution.py:301
  (13 shorter events, 0.2 us)
Async XLA Ops:
  1.5 5.6 %collective-permute-start.3 = (bf16[1,64,256]{2,1,0:T(8,128)(2,1)S(1)}, bf16[1,64,256]{2,1,0:T(8,128)(2,1)S(1)}, u32[]{:S(2)}, u32[]{:S(2)}) collective-permute-start(bf16[1,64,256]{2,1,0:T(8,128)(2,1)S(1)} %bitcast.18), channel_id=1, source_target_pairs={{0,4},{1,5},{2,6},{3,7},{4,0},{5,1},{6,2},{7,3},{8,12},{9,13},{10,... | collective-permute-start | bytes 98312 | tf_op jit(solution)/shard_map/ppermute | solution.py:33
  4.5 5.1 %collective-permute-start = (bf16[1,64,256]{2,1,0:T(8,128)(2,1)S(1)}, bf16[1,64,256]{2,1,0:T(8,128)(2,1)S(1)}, u32[]{:S(2)}, u32[]{:S(2)}) collective-permute-start(bf16[1,64,256]{2,1,0:T(8,128)(2,1)S(1)} %bitcast.14), channel_id=1, source_target_pairs={{0,16},{1,17},{2,18},{3,19},{4,20},{5,21},{6,22},{7,23},{8,24},{9,... | collective-permute-start | bytes 98312 | tf_op jit(solution)/shard_map/ppermute | solution.py:33
  7.1 5.3 %collective-permute-start.4 = (bf16[2,64,256]{2,1,0:T(8,128)(2,1)S(1)}, bf16[2,64,256]{2,1,0:T(8,128)(2,1)S(1)}, u32[]{:S(2)}, u32[]{:S(2)}) collective-permute-start(bf16[2,64,256]{2,1,0:T(8,128)(2,1)S(1)} %pad_maximum_fusion.5), channel_id=1, source_target_pairs={{0,16},{1,17},{2,18},{3,19},{4,20},{5,21},{6,22},{7,23},{8,24},{9,... | collective-permute-start | bytes 196616 | tf_op jit(solution)/shard_map/ppermute | solution.py:33
  9.6 4.9 %collective-permute-start.1 = (bf16[2,64,256]{2,1,0:T(8,128)(2,1)S(1)}, bf16[2,64,256]{2,1,0:T(8,128)(2,1)S(1)}, u32[]{:S(2)}, u32[]{:S(2)}) collective-permute-start(bf16[2,64,256]{2,1,0:T(8,128)(2,1)S(1)} %pad_maximum_fusion.4), channel_id=1, source_target_pairs={{0,8},{1,9},{2,10},{3,11},{4,12},{5,13},{6,14},{7,15},{8,0},{9,1},... | collective-permute-start | bytes 196616 | tf_op jit(solution)/shard_map/ppermute | solution.py:33
  12.4 5.4 %collective-permute-start.5 = (bf16[4,64,256]{2,1,0:T(8,128)(2,1)S(1)}, bf16[4,64,256]{2,1,0:T(8,128)(2,1)S(1)}, u32[]{:S(2)}, u32[]{:S(2)}) collective-permute-start(bf16[4,64,256]{2,1,0:T(8,128)(2,1)S(1)} %pad_maximum_fusion.3), channel_id=1, source_target_pairs={{0,8},{1,9},{2,10},{3,11},{4,12},{5,13},{6,14},{7,15},{8,0},{9,1},... | collective-permute-start | bytes 393224 | tf_op jit(solution)/shard_map/ppermute | solution.py:33
  14.6 5.0 %collective-permute-start.2 = (bf16[4,64,256]{2,1,0:T(8,128)(2,1)S(1)}, bf16[4,64,256]{2,1,0:T(8,128)(2,1)S(1)}, u32[]{:S(2)}, u32[]{:S(2)}) collective-permute-start(bf16[4,64,256]{2,1,0:T(8,128)(2,1)S(1)} %pad_maximum_fusion.2), channel_id=1, source_target_pairs={{0,4},{1,5},{2,6},{3,7},{4,0},{5,1},{6,2},{7,3},{8,12},{9,13},{10,... | collective-permute-start | bytes 393224 | tf_op jit(solution)/shard_map/ppermute | solution.py:33
  17.8 9.6 %copy-start = (bf16[64,512]{1,0:T(8,128)(2,1)S(1)}, bf16[64,512]{1,0:T(8,128)(2,1)}, u32[]{:S(2)}) copy-start(bf16[64,512]{1,0:T(8,128)(2,1)} %refs_0_.1) | copy-start | bytes 196612
  17.8 9.6 %copy-start.1 = (s32[512]{0:T(512)S(1)}, s32[512]{0:T(512)}, u32[]{:S(2)}) copy-start(s32[512]{0:T(512)} %param.6) | copy-start | bytes 6148
  21.8 1.4 %collective-permute-start.6 = (bf16[2,64,512]{2,1,0:T(8,128)(2,1)S(1)}, bf16[2,64,512]{2,1,0:T(8,128)(2,1)S(1)}, u32[]{:S(2)}, u32[]{:S(2)}) collective-permute-start(bf16[2,64,512]{2,1,0:T(8,128)(2,1)S(1)} %get-tuple-element.15), channel_id=1, source_target_pairs={{0,1},{1,0},{2,3},{3,2},{4,5},{5,4},{6,7},{7,6},{8,9},{9,8},{10,11... | collective-permute-start | bytes 393224 | tf_op jit(solution)/shard_map/ppermute | solution.py:33
  23.3 4.1 %collective-permute-start.7 = (bf16[1,64,512]{2,1,0:T(8,128)(2,1)S(1)}, bf16[1,64,512]{2,1,0:T(8,128)(2,1)S(1)}, u32[]{:S(2)}, u32[]{:S(2)}) collective-permute-start(bf16[1,64,512]{2,1,0:T(8,128)(2,1)S(1)} %slice_bitcast_fusion), channel_id=1, source_target_pairs={{0,3},{1,2},{2,1},{3,0},{4,7},{5,6},{6,5},{7,4},{8,11},{9,10},{10,... | collective-permute-start | bytes 196616 | tf_op jit(solution)/shard_map/ppermute | solution.py:33
  27.8 1.3 %collective-permute-start.8 = (f32[64,128]{1,0:T(8,128)S(1)}, f32[64,128]{1,0:T(8,128)S(1)}, u32[]{:S(2)}, u32[]{:S(2)}) collective-permute-start(f32[64,128]{1,0:T(8,128)S(1)} %get-tuple-element.16), channel_id=1, source_target_pairs={{0,1},{1,0},{2,3},{3,2},{4,5},{5,4},{6,7},{7,6},{8,9},{9,8},{10,11... | collective-permute-start | bytes 98312 | tf_op jit(solution)/shard_map/ppermute | solution.py:33
  29.0 3.3 %collective-permute-start.9 = (f32[64,128]{1,0:T(8,128)S(1)}, f32[64,128]{1,0:T(8,128)S(1)}, u32[]{:S(2)}, u32[]{:S(2)}) collective-permute-start(f32[64,128]{1,0:T(8,128)S(1)} %add.19), channel_id=1, source_target_pairs={{0,3},{1,2},{2,1},{3,0},{4,7},{5,6},{6,5},{7,4},{8,11},{9,10},{10,... | collective-permute-start | bytes 98312 | tf_op jit(solution)/shard_map/ppermute | solution.py:33
  32.4 3.3 %collective-permute-start.10 = (f32[64,128]{1,0:T(8,128)S(1)}, f32[64,128]{1,0:T(8,128)S(1)}, u32[]{:S(2)}, u32[]{:S(2)}) collective-permute-start(f32[64,128]{1,0:T(8,128)S(1)} %add.20), channel_id=1, source_target_pairs={{0,5},{1,4},{2,7},{3,6},{4,1},{5,0},{6,3},{7,2},{8,13},{9,12},{10,... | collective-permute-start | bytes 98312 | tf_op jit(solution)/shard_map/ppermute | solution.py:33
  35.7 3.3 %collective-permute-start.11 = (f32[64,128]{1,0:T(8,128)S(1)}, f32[64,128]{1,0:T(8,128)S(1)}, u32[]{:S(2)}, u32[]{:S(2)}) collective-permute-start(f32[64,128]{1,0:T(8,128)S(1)} %add.21), channel_id=1, source_target_pairs={{0,9},{1,8},{2,11},{3,10},{4,13},{5,12},{6,15},{7,14},{8,1},{9,0},... | collective-permute-start | bytes 98312 | tf_op jit(solution)/shard_map/ppermute | solution.py:33
  39.1 4.8 %collective-permute-start.12 = (f32[64,128]{1,0:T(8,128)S(1)}, f32[64,128]{1,0:T(8,128)S(1)}, u32[]{:S(2)}, u32[]{:S(2)}) collective-permute-start(f32[64,128]{1,0:T(8,128)S(1)} %add.22), channel_id=1, source_target_pairs={{0,17},{1,16},{2,19},{3,18},{4,21},{5,20},{6,23},{7,22},{8,25},{9,... | collective-permute-start | bytes 98312 | tf_op jit(solution)/shard_map/ppermute | solution.py:33

commit v4 on v3

--- a/solution.py
+++ b/solution.py
@@ -50,12 +50,16 @@
     return high, mid, low
 
 
-def scale_kernel(basis_ref, degree_ref, left_ref, right_ref):
+def scale_kernel(basis_ref, degree_ref, left_ref, right_ref, share_ref):
+    vectors = basis_ref.shape[0]
     half = left_ref.shape[1]
-    inv_root = lax.rsqrt(degree_ref[...].astype(F32))
-    scaled = (basis_ref[...].astype(F32) * inv_root).astype(BF16)
+    basis = basis_ref[...]
+    degree = degree_ref[...].astype(F32)
+    scaled = (basis.astype(F32) * lax.rsqrt(degree)).astype(BF16)
     left_ref[...] = scaled[:, :half]
     right_ref[...] = scaled[:, half:]
+    share_ref[:vectors, :] = basis
+    share_ref[vectors:, :] = jnp.broadcast_to(degree, (16, 2 * half)).astype(BF16)
 
 
 def load_kernel(per_piece, zero_at, column_in, live_in, panel_in, index_ref, panel_ref, column_ref, live_ref, sem):
@@ -144,22 +148,24 @@
         lax.fori_loop(0, groups // 2, body, 0)
 
 
-def gram_kernel(received, basis_ref, degree_ref, keep_ref, *refs):
-    parts = refs[:received]
-    split_ref, gram_ref, stack_ref = refs[received:]
-    vectors = basis_ref.shape[0]
-    spread = keep_ref[0]
-    for ref in parts:
-        spread = spread + ref[0].astype(F32)
-    basis = basis_ref[...]
-    inv_root = lax.rsqrt(degree_ref[...].astype(F32))
-    applied = basis.astype(F32) - inv_root * spread
-    for at, piece in enumerate(split3(applied)):
-        split_ref[at * vectors:(at + 1) * vectors, :] = piece
-        stack_ref[at * vectors:(at + 1) * vectors, :] = piece
-    stack_ref[3 * vectors:4 * vectors, :] = basis
-    stack = stack_ref[...]
-    prod = lax.dot_general(stack, stack, (((1,), (1,)), ((), ())), preferred_element_type=F32)
+def gram_kernel(last, mine_ref, theirs_ref, sums_ref, got_ref, split_ref, gram_ref, stack_ref):
+    vectors = mine_ref.shape[0] - 16
+    upper = (lax.axis_index("col") // last) & 1
+    for place, share_ref in ((0, mine_ref), (1, theirs_ref)):
+        basis = share_ref[:vectors, :]
+        inv_root = lax.rsqrt(share_ref[vectors:, :].astype(F32))[:1]
+        spread = sums_ref[place].astype(F32) + got_ref[1 - place].astype(F32)
+        applied = basis.astype(F32) - inv_root * spread
+        slot = upper if place == 0 else 1 - upper
+        for at, piece in enumerate(split3(applied)):
+            if place == 0:
+                split_ref[at * vectors:(at + 1) * vectors, :] = piece
+            stack_ref[slot, at * vectors:(at + 1) * vectors, :] = piece
+        stack_ref[slot, 3 * vectors:4 * vectors, :] = basis
+    dims = (((1,), (1,)), ((), ()))
+    first, second = stack_ref[0], stack_ref[1]
+    prod = lax.dot_general(first, first, dims, preferred_element_type=F32) + lax.dot_general(
+        second, second, dims, preferred_element_type=F32)
     wide = 2 * vectors
     near = prod[:, :wide]
     far = prod[:, wide:]
@@ -189,17 +195,28 @@
     work = jnp.where(lane < vectors, gram, jnp.where(lane == row + vectors, 1.0, 0.0))
     height = 8
     tiles = [work[at * height:(at + 1) * height] for at in range(vectors // height)]
-    row8 = lax.broadcasted_iota(jnp.int32, (height, wide), 0)
-    for step in range(vectors):
-        home = step // height
-        own = tiles[home][step % height:step % height + 1]
-        scaled = own / own[:, step:step + 1]
-        for at in range(home, vectors // height):
-            column = tiles[at][:, step:step + 1]
-            change = column * scaled
-            if at == home:
-                change = jnp.where(row8 > step % height, change, 0.0)
-            tiles[at] = tiles[at] - change
+    below = lax.broadcasted_iota(jnp.int32, (height, wide), 0)
+
+    def across(tile, at):
+        return jnp.broadcast_to(tile[:, at:at + 1], (height, wide))
+
+    def down(tile, at):
+        return jnp.broadcast_to(tile[at:at + 1], (height, wide))
+
+    for home in range(len(tiles)):
+        columns = [[across(tile, home * height + at) for at in range(height)] for tile in tiles[home:]]
+        for at in range(height):
+            own = columns[0]
+            scale = 1.0 / down(own[at], at)
+            pivot_row = down(tiles[home], at)
+            entries = [down(own[later], at) for later in range(height)]
+            for place, column in enumerate(columns):
+                factor = column[at] * scale
+                if place == 0:
+                    factor = jnp.where(below > at, factor, 0.0)
+                tiles[home + place] = tiles[home + place] - factor * pivot_row
+                for later in range(at + 1, height):
+                    column[later] = column[later] - factor * entries[later]
     done = jnp.concatenate(tiles, axis=0)
     pivot = jnp.sum(jnp.where(lane == row, done, 0.0), axis=1, keepdims=True)
     inverse = done * (lax.rsqrt(pivot) * math.sqrt(total_rows))
@@ -219,11 +236,15 @@
     per_piece = owned // height
     half = owned // 2
     degree_row = degree.reshape(1, owned)
-    left, right = pl.pallas_call(
+    left, right, share = pl.pallas_call(
         scale_kernel,
-        out_shape=[jax.ShapeDtypeStruct((vectors, half), BF16)] * 2,
+        out_shape=[
+            jax.ShapeDtypeStruct((vectors, half), BF16),
+            jax.ShapeDtypeStruct((vectors, half), BF16),
+            jax.ShapeDtypeStruct((vectors + 16, owned), BF16),
+        ],
         in_specs=[vmem(), vmem()],
-        out_specs=[vmem(), vmem()],
+        out_specs=[vmem(), vmem(), vmem()],
         compiler_params=limit(2),
         name="scale",
     )(hbm(krylov_block), hbm(degree_row))
@@ -252,6 +273,11 @@
     for left_bit, right_bit in zip(left_bits, right_bits):
         new_left = swap(left, left_bit, 0)
         new_right = swap(right, right_bit, 0)
+        if left_bit == left_bits[0]:
+            new_left, share = lax.optimization_barrier((new_left, share))
+            other_share = swap(share, 0, bits(groups)[-1] | 1)
+        elif left_bit == left_bits[-1]:
+            new_left, other_share = lax.optimization_barrier((new_left, other_share))
         left = jnp.concatenate([left, new_left], axis=0)
         right = jnp.concatenate([right, new_right], axis=0)
         left_order = left_order + [at ^ left_bit for at in left_order]
@@ -272,28 +298,28 @@
         compiler_params=limit(12),
         name="tiles",
     )(index, left, right, panel)
-    running = keep
-    received = []
-    for bit in bits(groups):
-        got = swap(send, 0, bit | 1)
-        received.append(got)
-        if running.shape[0] > 1:
-            summed = running + got.astype(F32)
+    col_bits = bits(groups)
+    last = col_bits.pop()
+    for bit in col_bits:
+        summed = keep + swap(send, 0, bit | 1).astype(F32)
+        if bit != col_bits[-1]:
             pairs = summed.reshape((-1, 2) + summed.shape[1:])
-            running, send = pairs[:, 0], pairs[:, 1].astype(BF16)
+            keep, send = pairs[:, 0], pairs[:, 1].astype(BF16)
+    sums = summed.astype(BF16)
+    got = swap(sums, 0, last | 1)
     pieces, gram = pl.pallas_call(
-        lambda *refs: gram_kernel(len(received), *refs),
+        lambda *refs: gram_kernel(last, *refs),
         out_shape=[
             jax.ShapeDtypeStruct((3 * vectors, owned), BF16),
             jax.ShapeDtypeStruct((vectors, 2 * vectors), F32),
         ],
-        in_specs=[vmem()] * (3 + len(received)),
+        in_specs=[vmem()] * 4,
         out_specs=[vmem(), vmem()],
-        scratch_shapes=[pltpu.VMEM((4 * vectors, owned), BF16)],
+        scratch_shapes=[pltpu.VMEM((2, 4 * vectors, owned), BF16)],
         compiler_params=limit(4),
         name="gram",
-    )(krylov_block, degree_row, keep, *received)
-    for bit in bits(groups):
+    )(share, other_share, sums, got)
+    for bit in col_bits:
         gram = gram + swap(gram, 0, bit | 1)
     for bit in bits(sources):
         gram = gram + swap(gram, bit, 1)

time: 50.3 us -> 45.6 us (0.907)
  Pallas kernels: 11.3 us -> 7.88 us
  starting transfers between devices: 22.4 us -> 21.7 us
  waiting for transfers between devices: 15.6 us -> 15 us
    pallas_call x1, Pallas kernels: 6.22 us -> 2.7 us  [on_device(): pl.pallas_call(lambda *refs: finish_kernel(total_rows, *refs), out_shape=...]
    ppermute x13, starting transfers between devices: 22.4 us -> 21.7 us  [swap(): return lax.ppermute(value, ('row', 'col'), pairs)]
    ppermute x13, waiting for transfers between devices: 15.6 us -> 15 us  [swap(): return lax.ppermute(value, ('row', 'col'), pairs)]
  transfers between devices with their start and end apart: 13 -> 13, of which waited for: 9 -> 11; matrix products, arithmetic and copies ran while one was open for 0% -> 0% of each run, Pallas kernels for 3% -> 4%
where the time goes in v4:
time: 45.6 us; the launch traced here: 45.4 us
  starting transfers between devices  21.7 us (48%)
  waiting for transfers between devices  15 us (33%)
  Pallas kernels  7.88 us (17%)
  between operations  0.7 us (2%)
    ppermute x13, starting transfers between devices, swap(): return lax.ppermute(value, ('row', 'col'), pairs)  21.7 us
    ppermute x13, waiting for transfers between devices, swap(): return lax.ppermute(value, ('row', 'col'), pairs)  15 us
    pallas_call x1, Pallas kernels, on_device(): pl.pallas_call(lambda *refs: finish_kernel(total_rows, *refs), out_shape=...  2.7 us
    pallas_call x1, Pallas kernels, on_device(): pl.pallas_call(lambda *refs: tile_kernel(sources, groups, per_piece, left...  2.17 us
    pallas_call x1, Pallas kernels, on_device(): pl.pallas_call(lambda *refs: load_kernel(per_piece, sources * per_piece,...  1.65 us
  transfers between devices with their start and end apart: 13, of which 11 were waited for; matrix products, arithmetic and copies ran while one was open for 0% of the time, Pallas kernels for 4%

profile of v4, /device:TPU:0, one launch (start us, length us, event | category | flops | bytes accessed | tf_op | source)
XLA Modules:
  0.0 45.4 jit_solution(4400958351735706865)
XLA Ops:
  0.6 0.9 %scale.1 = (bf16[64,256]{1,0:T(8,128)(2,1)S(1)}, bf16[64,256]{1,0:T(8,128)(2,1)S(1)}, bf16[80,512]{1,0:T(8,128)(2,1)S(1)}) custom-call(bf16[64,512]{1,0:T(8,128)(2,1)} %basis_ref.1, s32[1,512]{1,0:T(1,128)} %bitcast.21), custom_call_target="tpu_custom_call" | custom-call | tf_op jit(solution)/shard_map/scale/pallas_call | solution.py:239
  1.5 4.1 %collective-permute-start = (bf16[1,64,256]{2,1,0:T(8,128)(2,1)S(1)}, bf16[1,64,256]{2,1,0:T(8,128)(2,1)S(1)}, u32[]{:S(2)}, u32[]{:S(2)}) collective-permute-start(bf16[1,64,256]{2,1,0:T(8,128)(2,1)S(1)} %bitcast.14), channel_id=1, source_target_pairs={{0,16},{1,17},{2,18},{3,19},{4,20},{5,21},{6,22},{7,23},{8,24},{9,... | collective-permute-start | bytes 98312 | tf_op jit(solution)/shard_map/ppermute | solution.py:33
  5.6 1.5 %collective-permute-start.4 = (bf16[1,64,256]{2,1,0:T(8,128)(2,1)S(1)}, bf16[1,64,256]{2,1,0:T(8,128)(2,1)S(1)}, u32[]{:S(2)}, u32[]{:S(2)}) collective-permute-start(bf16[1,64,256]{2,1,0:T(8,128)(2,1)S(1)} %bitcast.10), channel_id=1, source_target_pairs={{0,4},{1,5},{2,6},{3,7},{4,0},{5,1},{6,2},{7,3},{8,12},{9,13},{10,... | collective-permute-start | bytes 98312 | tf_op jit(solution)/shard_map/ppermute | solution.py:33
  7.1 0.8 %collective-permute-done = bf16[1,64,256]{2,1,0:T(8,128)(2,1)S(1)} collective-permute-done((bf16[1,64,256]{2,1,0:T(8,128)(2,1)S(1)}, bf16[1,64,256]{2,1,0:T(8,128)(2,1)S(1)}, u32[]{:S(2)}, u32[]{:S(2)}) %collective-permute-start) | collective-permute-done | bytes 32800 | tf_op jit(solution)/shard_map/ppermute | solution.py:33
  7.9 1.6 %collective-permute-start.1 = (bf16[2,64,256]{2,1,0:T(8,128)(2,1)S(1)}, bf16[2,64,256]{2,1,0:T(8,128)(2,1)S(1)}, u32[]{:S(2)}, u32[]{:S(2)}) collective-permute-start(bf16[2,64,256]{2,1,0:T(8,128)(2,1)S(1)} %pad_maximum_fusion.4), channel_id=1, source_target_pairs={{0,8},{1,9},{2,10},{3,11},{4,12},{5,13},{6,14},{7,15},{8,0},{9,1},... | collective-permute-start | bytes 196616 | tf_op jit(solution)/shard_map/ppermute | solution.py:33
  9.5 0.0 collective-permute-done.4
  9.5 2.9 %collective-permute-start.5 = (bf16[2,64,256]{2,1,0:T(8,128)(2,1)S(1)}, bf16[2,64,256]{2,1,0:T(8,128)(2,1)S(1)}, u32[]{:S(2)}, u32[]{:S(2)}) collective-permute-start(bf16[2,64,256]{2,1,0:T(8,128)(2,1)S(1)} %pad_maximum_fusion.5), channel_id=1, source_target_pairs={{0,16},{1,17},{2,18},{3,19},{4,20},{5,21},{6,22},{7,23},{8,24},{9,... | collective-permute-start | bytes 196616 | tf_op jit(solution)/shard_map/ppermute | solution.py:33
  12.4 0.5 %collective-permute-done.1 = bf16[2,64,256]{2,1,0:T(8,128)(2,1)S(1)} collective-permute-done((bf16[2,64,256]{2,1,0:T(8,128)(2,1)S(1)}, bf16[2,64,256]{2,1,0:T(8,128)(2,1)S(1)}, u32[]{:S(2)}, u32[]{:S(2)}) %collective-permute-start.1) | collective-permute-done | bytes 65568 | tf_op jit(solution)/shard_map/ppermute | solution.py:33
  12.9 1.8 %collective-permute-start.2 = (bf16[4,64,256]{2,1,0:T(8,128)(2,1)S(1)}, bf16[4,64,256]{2,1,0:T(8,128)(2,1)S(1)}, u32[]{:S(2)}, u32[]{:S(2)}) collective-permute-start(bf16[4,64,256]{2,1,0:T(8,128)(2,1)S(1)} %pad_maximum_fusion.2), channel_id=1, source_target_pairs={{0,4},{1,5},{2,6},{3,7},{4,0},{5,1},{6,2},{7,3},{8,12},{9,13},{10,... | collective-permute-start | bytes 393224 | tf_op jit(solution)/shard_map/ppermute | solution.py:33
  14.7 0.0 collective-permute-start.3
  14.7 0.1 collective-permute-done.5
  14.8 1.6 %collective-permute-start.6 = (bf16[4,64,256]{2,1,0:T(8,128)(2,1)S(1)}, bf16[4,64,256]{2,1,0:T(8,128)(2,1)S(1)}, u32[]{:S(2)}, u32[]{:S(2)}) collective-permute-start(bf16[4,64,256]{2,1,0:T(8,128)(2,1)S(1)} %pad_maximum_fusion.3), channel_id=1, source_target_pairs={{0,8},{1,9},{2,10},{3,11},{4,12},{5,13},{6,14},{7,15},{8,0},{9,1},... | collective-permute-start | bytes 393224 | tf_op jit(solution)/shard_map/ppermute | solution.py:33
  16.4 1.6 %load.1 = (s32[8,32]{1,0:T(8,128)S(1)}, bf16[32,64,512]{2,1,0:T(8,128)(2,1)S(1)}) custom-call(s32[8,32]{1,0:T(8,128)} %bitcast.19, s32[8,32]{1,0:T(8,128)} %bitcast.20, bf16[32,64,512]{2,1,0:T(8,128)(2,1)} %bitcast.18), custom_call_target="tpu_custom_call" | custom-call | tf_op jit(solution)/shard_map/load/pallas_call | solution.py:252
  18.1 1.3 %collective-permute-done.3.refs_1_ = bf16[80,512]{1,0:T(8,128)(2,1)S(1)} collective-permute-done((bf16[80,512]{1,0:T(8,128)(2,1)S(1)}, bf16[80,512]{1,0:T(8,128)(2,1)S(1)}, u32[]{:S(2)}, u32[]{:S(2)}) %collective-permute-start.3) | collective-permute-done | bytes 81952 | tf_op jit(solution)/shard_map/ppermute | solution.py:33
  19.3 0.0 collective-permute-done.2
  19.4 1.3 %collective-permute-done.6 = bf16[4,64,256]{2,1,0:T(8,128)(2,1)S(1)} collective-permute-done((bf16[4,64,256]{2,1,0:T(8,128)(2,1)S(1)}, bf16[4,64,256]{2,1,0:T(8,128)(2,1)S(1)}, u32[]{:S(2)}, u32[]{:S(2)}) %collective-permute-start.6) | collective-permute-done | bytes 131104 | tf_op jit(solution)/shard_map/ppermute | solution.py:33
  20.7 2.2 %tiles.1 = (f32[2,64,512]{2,1,0:T(8,128)S(1)}, bf16[2,64,512]{2,1,0:T(8,128)(2,1)S(1)}) custom-call(s32[8,32]{1,0:T(8,128)S(1)} %get-tuple-element.20.refs_0_, bf16[8,64,256]{2,1,0:T(8,128)(2,1)S(1)} %pad_maximum_fusion.refs_1_, bf16[8,64,256]{2,1,0:T(8,128)(2,1)S(1)} %pad_maximum_fusion.1.refs_2_, bf16[32,64,512]{2,1,0:T(8,128)(2,1)S(1)} %get-tuple-element.23.refs_3_), custom_call_target="tpu_custom_call" | custom-call | tf_op jit(solution)/shard_map/tiles/pallas_call | solution.py:286
  22.9 0.4 collective-permute-start.7
  23.3 1.0 %collective-permute-done.7 = bf16[2,64,512]{2,1,0:T(8,128)(2,1)S(1)} collective-permute-done((bf16[2,64,512]{2,1,0:T(8,128)(2,1)S(1)}, bf16[2,64,512]{2,1,0:T(8,128)(2,1)S(1)}, u32[]{:S(2)}, u32[]{:S(2)}) %collective-permute-start.7) | collective-permute-done | bytes 131104 | tf_op jit(solution)/shard_map/ppermute | solution.py:33
  24.3 1.4 %collective-permute-start.8 = (bf16[2,64,512]{2,1,0:T(8,128)(2,1)S(1)}, bf16[2,64,512]{2,1,0:T(8,128)(2,1)S(1)}, u32[]{:S(2)}, u32[]{:S(2)}) collective-permute-start(bf16[2,64,512]{2,1,0:T(8,128)(2,1)S(1)} %add_convert_fusion.refs_2_), channel_id=1, source_target_pairs={{0,3},{1,2},{2,1},{3,0},{4,7},{5,6},{6,5},{7,4},{8,11},{9,10},{10,... | collective-permute-start | bytes 393224 | tf_op jit(solution)/shard_map/ppermute | solution.py:33
  25.8 4.0 %collective-permute-done.8.refs_3_ = bf16[2,64,512]{2,1,0:T(8,128)(2,1)S(1)} collective-permute-done((bf16[2,64,512]{2,1,0:T(8,128)(2,1)S(1)}, bf16[2,64,512]{2,1,0:T(8,128)(2,1)S(1)}, u32[]{:S(2)}, u32[]{:S(2)}) %collective-permute-start.8) | collective-permute-done | bytes 131104 | tf_op jit(solution)/shard_map/ppermute | solution.py:33
  29.8 0.5 %gram.1 = (bf16[192,512]{1,0:T(8,128)(2,1)S(1)}, f32[64,128]{1,0:T(8,128)S(1)}) custom-call(bf16[80,512]{1,0:T(8,128)(2,1)S(1)} %get-tuple-element.17.refs_0_, bf16[80,512]{1,0:T(8,128)(2,1)S(1)} %collective-permute-done.3.refs_1_, bf16[2,64,512]{2,1,0:T(8,128)(2,1)S(1)} %add_convert_fusion.refs_2_, bf16[2,64,512]{2,1,0:T(8,128)(2,1)S(1)} %collective-permute-done.8.refs_3_), custom_call_target="tpu_custom_call" | custom-call | tf_op jit(solution)/shard_map/gram/pallas_call | solution.py:310
  30.3 0.3 collective-permute-start.9
  30.6 0.9 %collective-permute-done.9 = f32[64,128]{1,0:T(8,128)S(1)} collective-permute-done((f32[64,128]{1,0:T(8,128)S(1)}, f32[64,128]{1,0:T(8,128)S(1)}, u32[]{:S(2)}, u32[]{:S(2)}) %collective-permute-start.9) | collective-permute-done | bytes 32800 | tf_op jit(solution)/shard_map/ppermute | solution.py:33
  31.5 1.5 %collective-permute-start.10 = (f32[64,128]{1,0:T(8,128)S(1)}, f32[64,128]{1,0:T(8,128)S(1)}, u32[]{:S(2)}, u32[]{:S(2)}) collective-permute-start(f32[64,128]{1,0:T(8,128)S(1)} %add.16), channel_id=1, source_target_pairs={{0,5},{1,4},{2,7},{3,6},{4,1},{5,0},{6,3},{7,2},{8,13},{9,12},{10,... | collective-permute-start | bytes 98312 | tf_op jit(solution)/shard_map/ppermute | solution.py:33
  33.1 1.8 %collective-permute-done.10 = f32[64,128]{1,0:T(8,128)S(1)} collective-permute-done((f32[64,128]{1,0:T(8,128)S(1)}, f32[64,128]{1,0:T(8,128)S(1)}, u32[]{:S(2)}, u32[]{:S(2)}) %collective-permute-start.10) | collective-permute-done | bytes 32800 | tf_op jit(solution)/shard_map/ppermute | solution.py:33
  34.9 2.0 %collective-permute-start.11 = (f32[64,128]{1,0:T(8,128)S(1)}, f32[64,128]{1,0:T(8,128)S(1)}, u32[]{:S(2)}, u32[]{:S(2)}) collective-permute-start(f32[64,128]{1,0:T(8,128)S(1)} %add.17), channel_id=1, source_target_pairs={{0,9},{1,8},{2,11},{3,10},{4,13},{5,12},{6,15},{7,14},{8,1},{9,0},... | collective-permute-start | bytes 98312 | tf_op jit(solution)/shard_map/ppermute | solution.py:33
  36.9 1.6 %collective-permute-done.11 = f32[64,128]{1,0:T(8,128)S(1)} collective-permute-done((f32[64,128]{1,0:T(8,128)S(1)}, f32[64,128]{1,0:T(8,128)S(1)}, u32[]{:S(2)}, u32[]{:S(2)}) %collective-permute-start.11) | collective-permute-done | bytes 32800 | tf_op jit(solution)/shard_map/ppermute | solution.py:33
  38.5 2.5 %collective-permute-start.12 = (f32[64,128]{1,0:T(8,128)S(1)}, f32[64,128]{1,0:T(8,128)S(1)}, u32[]{:S(2)}, u32[]{:S(2)}) collective-permute-start(f32[64,128]{1,0:T(8,128)S(1)} %add.18), channel_id=1, source_target_pairs={{0,17},{1,16},{2,19},{3,18},{4,21},{5,20},{6,23},{7,22},{8,25},{9,... | collective-permute-start | bytes 98312 | tf_op jit(solution)/shard_map/ppermute | solution.py:33
  41.0 1.7 %collective-permute-done.12 = f32[64,128]{1,0:T(8,128)S(1)} collective-permute-done((f32[64,128]{1,0:T(8,128)S(1)}, f32[64,128]{1,0:T(8,128)S(1)}, u32[]{:S(2)}, u32[]{:S(2)}) %collective-permute-start.12) | collective-permute-done | bytes 32800 | tf_op jit(solution)/shard_map/ppermute | solution.py:33
  42.7 2.7 %finish.1 = (f32[64,512]{1,0:T(8,128)}, f32[64,64]{1,0:T(8,128)}) custom-call(f32[64,128]{1,0:T(8,128)S(1)} %add.19.refs_0_, bf16[192,512]{1,0:T(8,128)(2,1)S(1)} %get-tuple-element.27.refs_1_), custom_call_target="tpu_custom_call" | custom-call | tf_op jit(solution)/shard_map/finish/pallas_call | solution.py:327
  (11 shorter events, 0.1 us)
Async XLA Ops:
  1.5 6.3 %collective-permute-start = (bf16[1,64,256]{2,1,0:T(8,128)(2,1)S(1)}, bf16[1,64,256]{2,1,0:T(8,128)(2,1)S(1)}, u32[]{:S(2)}, u32[]{:S(2)}) collective-permute-start(bf16[1,64,256]{2,1,0:T(8,128)(2,1)S(1)} %bitcast.14), channel_id=1, source_target_pairs={{0,16},{1,17},{2,18},{3,19},{4,20},{5,21},{6,22},{7,23},{8,24},{9,... | collective-permute-start | bytes 98312 | tf_op jit(solution)/shard_map/ppermute | solution.py:33
  5.6 3.9 %collective-permute-start.4 = (bf16[1,64,256]{2,1,0:T(8,128)(2,1)S(1)}, bf16[1,64,256]{2,1,0:T(8,128)(2,1)S(1)}, u32[]{:S(2)}, u32[]{:S(2)}) collective-permute-start(bf16[1,64,256]{2,1,0:T(8,128)(2,1)S(1)} %bitcast.10), channel_id=1, source_target_pairs={{0,4},{1,5},{2,6},{3,7},{4,0},{5,1},{6,2},{7,3},{8,12},{9,13},{10,... | collective-permute-start | bytes 98312 | tf_op jit(solution)/shard_map/ppermute | solution.py:33
  7.9 5.0 %collective-permute-start.1 = (bf16[2,64,256]{2,1,0:T(8,128)(2,1)S(1)}, bf16[2,64,256]{2,1,0:T(8,128)(2,1)S(1)}, u32[]{:S(2)}, u32[]{:S(2)}) collective-permute-start(bf16[2,64,256]{2,1,0:T(8,128)(2,1)S(1)} %pad_maximum_fusion.4), channel_id=1, source_target_pairs={{0,8},{1,9},{2,10},{3,11},{4,12},{5,13},{6,14},{7,15},{8,0},{9,1},... | collective-permute-start | bytes 196616 | tf_op jit(solution)/shard_map/ppermute | solution.py:33
  9.5 5.2 %collective-permute-start.5 = (bf16[2,64,256]{2,1,0:T(8,128)(2,1)S(1)}, bf16[2,64,256]{2,1,0:T(8,128)(2,1)S(1)}, u32[]{:S(2)}, u32[]{:S(2)}) collective-permute-start(bf16[2,64,256]{2,1,0:T(8,128)(2,1)S(1)} %pad_maximum_fusion.5), channel_id=1, source_target_pairs={{0,16},{1,17},{2,18},{3,19},{4,20},{5,21},{6,22},{7,23},{8,24},{9,... | collective-permute-start | bytes 196616 | tf_op jit(solution)/shard_map/ppermute | solution.py:33
  12.9 6.4 %collective-permute-start.2 = (bf16[4,64,256]{2,1,0:T(8,128)(2,1)S(1)}, bf16[4,64,256]{2,1,0:T(8,128)(2,1)S(1)}, u32[]{:S(2)}, u32[]{:S(2)}) collective-permute-start(bf16[4,64,256]{2,1,0:T(8,128)(2,1)S(1)} %pad_maximum_fusion.2), channel_id=1, source_target_pairs={{0,4},{1,5},{2,6},{3,7},{4,0},{5,1},{6,2},{7,3},{8,12},{9,13},{10,... | collective-permute-start | bytes 393224 | tf_op jit(solution)/shard_map/ppermute | solution.py:33
  14.7 4.7 %collective-permute-start.3 = (bf16[80,512]{1,0:T(8,128)(2,1)S(1)}, bf16[80,512]{1,0:T(8,128)(2,1)S(1)}, u32[]{:S(2)}, u32[]{:S(2)}) collective-permute-start(bf16[80,512]{1,0:T(8,128)(2,1)S(1)} %get-tuple-element.17.refs_0_), channel_id=1, source_target_pairs={{0,3},{1,2},{2,1},{3,0},{4,7},{5,6},{6,5},{7,4},{8,11},{9,10},{10,... | collective-permute-start | bytes 245768 | tf_op jit(solution)/shard_map/ppermute | solution.py:33
  14.8 5.9 %collective-permute-start.6 = (bf16[4,64,256]{2,1,0:T(8,128)(2,1)S(1)}, bf16[4,64,256]{2,1,0:T(8,128)(2,1)S(1)}, u32[]{:S(2)}, u32[]{:S(2)}) collective-permute-start(bf16[4,64,256]{2,1,0:T(8,128)(2,1)S(1)} %pad_maximum_fusion.3), channel_id=1, source_target_pairs={{0,8},{1,9},{2,10},{3,11},{4,12},{5,13},{6,14},{7,15},{8,0},{9,1},... | collective-permute-start | bytes 393224 | tf_op jit(solution)/shard_map/ppermute | solution.py:33
  22.9 1.4 %collective-permute-start.7 = (bf16[2,64,512]{2,1,0:T(8,128)(2,1)S(1)}, bf16[2,64,512]{2,1,0:T(8,128)(2,1)S(1)}, u32[]{:S(2)}, u32[]{:S(2)}) collective-permute-start(bf16[2,64,512]{2,1,0:T(8,128)(2,1)S(1)} %get-tuple-element.25), channel_id=1, source_target_pairs={{0,1},{1,0},{2,3},{3,2},{4,5},{5,4},{6,7},{7,6},{8,9},{9,8},{10,11... | collective-permute-start | bytes 393224 | tf_op jit(solution)/shard_map/ppermute | solution.py:33
  24.3 5.4 %collective-permute-start.8 = (bf16[2,64,512]{2,1,0:T(8,128)(2,1)S(1)}, bf16[2,64,512]{2,1,0:T(8,128)(2,1)S(1)}, u32[]{:S(2)}, u32[]{:S(2)}) collective-permute-start(bf16[2,64,512]{2,1,0:T(8,128)(2,1)S(1)} %add_convert_fusion.refs_2_), channel_id=1, source_target_pairs={{0,3},{1,2},{2,1},{3,0},{4,7},{5,6},{6,5},{7,4},{8,11},{9,10},{10,... | collective-permute-start | bytes 393224 | tf_op jit(solution)/shard_map/ppermute | solution.py:33
  30.3 1.3 %collective-permute-start.9 = (f32[64,128]{1,0:T(8,128)S(1)}, f32[64,128]{1,0:T(8,128)S(1)}, u32[]{:S(2)}, u32[]{:S(2)}) collective-permute-start(f32[64,128]{1,0:T(8,128)S(1)} %get-tuple-element.26), channel_id=1, source_target_pairs={{0,1},{1,0},{2,3},{3,2},{4,5},{5,4},{6,7},{7,6},{8,9},{9,8},{10,11... | collective-permute-start | bytes 98312 | tf_op jit(solution)/shard_map/ppermute | solution.py:33
  31.5 3.3 %collective-permute-start.10 = (f32[64,128]{1,0:T(8,128)S(1)}, f32[64,128]{1,0:T(8,128)S(1)}, u32[]{:S(2)}, u32[]{:S(2)}) collective-permute-start(f32[64,128]{1,0:T(8,128)S(1)} %add.16), channel_id=1, source_target_pairs={{0,5},{1,4},{2,7},{3,6},{4,1},{5,0},{6,3},{7,2},{8,13},{9,12},{10,... | collective-permute-start | bytes 98312 | tf_op jit(solution)/shard_map/ppermute | solution.py:33
  34.9 3.6 %collective-permute-start.11 = (f32[64,128]{1,0:T(8,128)S(1)}, f32[64,128]{1,0:T(8,128)S(1)}, u32[]{:S(2)}, u32[]{:S(2)}) collective-permute-start(f32[64,128]{1,0:T(8,128)S(1)} %add.17), channel_id=1, source_target_pairs={{0,9},{1,8},{2,11},{3,10},{4,13},{5,12},{6,15},{7,14},{8,1},{9,0},... | collective-permute-start | bytes 98312 | tf_op jit(solution)/shard_map/ppermute | solution.py:33
  38.5 4.2 %collective-permute-start.12 = (f32[64,128]{1,0:T(8,128)S(1)}, f32[64,128]{1,0:T(8,128)S(1)}, u32[]{:S(2)}, u32[]{:S(2)}) collective-permute-start(f32[64,128]{1,0:T(8,128)S(1)} %add.18), channel_id=1, source_target_pairs={{0,17},{1,16},{2,19},{3,18},{4,21},{5,20},{6,23},{7,22},{8,25},{9,... | collective-permute-start | bytes 98312 | tf_op jit(solution)/shard_map/ppermute | solution.py:33

commit v5 on v4

--- a/solution.py
+++ b/solution.py
@@ -50,19 +50,29 @@
     return high, mid, low
 
 
-def scale_kernel(basis_ref, degree_ref, left_ref, right_ref, share_ref):
-    vectors = basis_ref.shape[0]
-    half = left_ref.shape[1]
+def scale_kernel(basis_ref, degree_ref, scaled_ref, share_ref):
+    vectors, owned = basis_ref.shape
     basis = basis_ref[...]
     degree = degree_ref[...].astype(F32)
-    scaled = (basis.astype(F32) * lax.rsqrt(degree)).astype(BF16)
-    left_ref[...] = scaled[:, :half]
-    right_ref[...] = scaled[:, half:]
+    scaled_ref[...] = (basis.astype(F32) * lax.rsqrt(degree)).astype(BF16)
     share_ref[:vectors, :] = basis
-    share_ref[vectors:, :] = jnp.broadcast_to(degree, (16, 2 * half)).astype(BF16)
-
-
-def load_kernel(per_piece, zero_at, column_in, live_in, panel_in, index_ref, panel_ref, column_ref, live_ref, sem):
+    share_ref[vectors:, :] = jnp.broadcast_to(degree, (16, owned)).astype(BF16)
+
+
+def fill_table(table_ref, per_piece, height, orders, refs):
+    wide = 2 * height
+    pairs = refs[0].shape[2] // wide
+    for side, (order, ref) in enumerate(zip(orders, refs)):
+        for at, source in enumerate(order):
+            for pair in range(pairs):
+                tile = ref[at, :, pair * wide:(pair + 1) * wide]
+                block = source * per_piece + 2 * (side * pairs + pair)
+                table_ref[block] = tile
+                table_ref[block + 1] = jnp.concatenate([tile[:, height:], tile[:, :height]], axis=1)
+
+
+def load_kernel(per_piece, zero_at, orders, column_in, live_in, panel_in, left_ref, right_ref, index_ref, panel_ref,
+                table_ref, column_ref, live_ref, work_ref, sem):
     copies = [
         pltpu.make_async_copy(column_in, column_ref, sem.at[0]),
         pltpu.make_async_copy(live_in, live_ref, sem.at[1]),
@@ -70,44 +80,36 @@
     ]
     for copy in copies:
         copy.start()
+    fill_table(table_ref, per_piece, panel_ref.shape[1], orders, (left_ref, right_ref))
+    table_ref[zero_at] = jnp.zeros(table_ref.shape[1:], BF16)
     copies[0].wait()
     copies[1].wait()
     column = column_ref[...] ^ (lax.axis_index("row") * per_piece)
     slot = lax.broadcasted_iota(jnp.int32, column.shape, 0)
     column = column ^ (slot & 1)
-    index_ref[...] = jnp.where(live_ref[...] == 1, column, zero_at)
+    work_ref[...] = jnp.where(live_ref[...] == 1, column, zero_at)
+    last = pltpu.make_async_copy(work_ref, index_ref, sem.at[3])
+    last.start()
     copies[2].wait()
-
-
-def tile_kernel(sources, groups, per_piece, left_order, right_order, index_ref, left_ref, right_ref,
-                panel_ref, keep_ref, send_ref, table_ref, lhs_ref):
-    vectors = left_ref.shape[1]
-    half = left_ref.shape[2]
+    last.wait()
+
+
+def multiply(groups, per_piece, odd, index_ref, panel_ref, table_ref, lhs_ref, out_ref):
     height = panel_ref.shape[1]
     slots = index_ref.shape[0]
+    vectors = table_ref.shape[1]
     wide = 2 * height
-    pairs = half // wide
     my_col = lax.axis_index("col")
-    zero_at = sources * per_piece
-    for side, order, ref in ((0, left_order, left_ref), (1, right_order, right_ref)):
-        for at in range(sources):
-            for pair in range(pairs):
-                tile = ref[at, :, pair * wide:(pair + 1) * wide]
-                block = order[at] * per_piece + 2 * (side * pairs + pair)
-                table_ref[block] = tile
-                table_ref[block + 1] = jnp.concatenate([tile[:, height:], tile[:, :height]], axis=1)
-    table_ref[zero_at] = jnp.zeros((vectors, wide), BF16)
-    lane = lax.broadcasted_iota(jnp.int32, (vectors, wide), 1)
-    is_low = lane < height
+    is_low = lax.broadcasted_iota(jnp.int32, (vectors, wide), 1) < height
     pack = 4
-    chunks = per_piece // pack
-
-    def group(step, chunk, slot_of):
-        partner = step & ~1
-        flips = step & 1
-        for bit in bits(groups)[1:]:
+    span = pack * height
+
+    def chunk_of(step, chunk):
+        flips = odd
+        for bit in bits(groups)[:-1]:
             flips = flips ^ ((step // bit) & 1)
-        row0 = ((partner | flips) ^ my_col) * per_piece + chunk * pack
+        row0 = ((2 * step + flips) ^ my_col) * per_piece + chunk * pack
+        slot_of = chunk % 2
         for inner in range(pack):
             row = row0 + inner
             for pair in range(slots // 2):
@@ -117,35 +119,35 @@
                     is_low, table_ref[first], table_ref[second])
         rhs = panel_ref[pl.ds(row0, pack)].reshape(pack * height, slots * height)
         prod = lax.dot_general(lhs_ref[slot_of], rhs, (((1,), (1,)), ((), ())), preferred_element_type=F32)
-        out = []
         for pair in range(pack // 2):
             lanes = slice(pair * wide, (pair + 1) * wide)
             top = prod[2 * pair * vectors:(2 * pair + 1) * vectors, lanes]
             low = prod[(2 * pair + 1) * vectors:(2 * pair + 2) * vectors, lanes]
-            out.append(jnp.where(is_low, top, low))
-        return jnp.concatenate(out, axis=1)
-
-    span = pack * height
+            at = chunk * span + pair * wide
+            out_ref[step, :, at:at + wide] = jnp.where(is_low, top, low).astype(out_ref.dtype)
+
     if groups <= 4:
-        at = 0
-        for piece in [s for s in range(groups) if s % 2] + [s for s in range(groups) if s % 2 == 0]:
-            for chunk in range(chunks):
-                value = group(piece, chunk, at % 2)
-                at += 1
-                lanes = slice(chunk * span, (chunk + 1) * span)
-                if piece % 2:
-                    send_ref[piece // 2, :, lanes] = value.astype(BF16)
-                else:
-                    keep_ref[piece // 2, :, lanes] = value
+        for step in range(groups // 2):
+            for chunk in range(per_piece // pack):
+                chunk_of(step, chunk)
     else:
         def body(step, carry):
-            for chunk in range(chunks):
-                lanes = slice(chunk * span, (chunk + 1) * span)
-                send_ref[step, :, lanes] = group(2 * step + 1, chunk, 0).astype(BF16)
-                keep_ref[step, :, lanes] = group(2 * step, chunk, 1)
+            for chunk in range(per_piece // pack):
+                chunk_of(step, chunk)
             return carry
 
         lax.fori_loop(0, groups // 2, body, 0)
+
+
+def send_kernel(groups, per_piece, orders, index_ref, panel_ref, table_in, left_ref, right_ref, table_ref, send_ref,
+                lhs_ref):
+    del table_in
+    fill_table(table_ref, per_piece, panel_ref.shape[1], orders, (left_ref, right_ref))
+    multiply(groups, per_piece, 1, index_ref, panel_ref, table_ref, lhs_ref, send_ref)
+
+
+def keep_kernel(groups, per_piece, index_ref, panel_ref, table_ref, keep_ref, lhs_ref):
+    multiply(groups, per_piece, 0, index_ref, panel_ref, table_ref, lhs_ref, keep_ref)
 
 
 def gram_kernel(last, mine_ref, theirs_ref, sums_ref, got_ref, split_ref, gram_ref, stack_ref):
@@ -236,68 +238,80 @@
     per_piece = owned // height
     half = owned // 2
     degree_row = degree.reshape(1, owned)
-    left, right, share = pl.pallas_call(
+    scaled, share = pl.pallas_call(
         scale_kernel,
         out_shape=[
-            jax.ShapeDtypeStruct((vectors, half), BF16),
-            jax.ShapeDtypeStruct((vectors, half), BF16),
+            jax.ShapeDtypeStruct((vectors, owned), BF16),
             jax.ShapeDtypeStruct((vectors + 16, owned), BF16),
         ],
         in_specs=[vmem(), vmem()],
-        out_specs=[vmem(), vmem(), vmem()],
+        out_specs=[vmem(), vmem()],
         compiler_params=limit(2),
         name="scale",
     )(hbm(krylov_block), hbm(degree_row))
+    row_bits = bits(sources)
+    top = row_bits.pop()
+    other = swap(scaled, top, 0)
+    other_share = swap(share, 0, bits(groups)[-1] | 1)
+    other, other_share = lax.optimization_barrier((other, other_share))
+    left = jnp.stack([scaled[:, :half], other[:, :half]])
+    right = jnp.stack([scaled[:, half:], other[:, half:]])
+    left_order, right_order = [0, top], [0, top]
+    for left_bit, right_bit in zip(row_bits[::-1], row_bits):
+        if left_bit != row_bits[-1]:
+            left = jnp.concatenate([left, new_left], axis=0)
+            right = jnp.concatenate([right, new_right], axis=0)
+        early = (left_order, right_order)
+        new_left = swap(left, left_bit, 0)
+        new_right = swap(right, right_bit, 0)
+        late = ([at ^ left_bit for at in left_order], [at ^ right_bit for at in right_order])
+        left_order = left_order + late[0]
+        right_order = right_order + late[1]
     slots = tile_column.shape[2]
-    index, panel = pl.pallas_call(
-        lambda *refs: load_kernel(per_piece, sources * per_piece, *refs),
-        out_shape=[
-            jax.ShapeDtypeStruct((slots, block_rows), jnp.int32),
+    many = groups // 2
+    table_shape = (sources * per_piece + 1, vectors, 2 * height)
+    index, panel, table = pl.pallas_call(
+        lambda *refs: load_kernel(per_piece, sources * per_piece, early, *refs),
+        out_shape=[
+            pltpu.SMEM((slots, block_rows), jnp.int32),
             jax.ShapeDtypeStruct((block_rows, height, slot_width), BF16),
-        ],
-        in_specs=[pl.BlockSpec(memory_space=pl.ANY)] * 3,
-        out_specs=[vmem(), vmem()],
+            jax.ShapeDtypeStruct(table_shape, BF16),
+        ],
+        in_specs=[pl.BlockSpec(memory_space=pl.ANY)] * 3 + [vmem()] * 2,
+        out_specs=[smem(), vmem(), vmem()],
         scratch_shapes=[
             pltpu.VMEM((slots, block_rows), jnp.int32),
             pltpu.VMEM((slots, block_rows), jnp.int32),
-            pltpu.SemaphoreType.DMA((3,)),
+            pltpu.VMEM((slots, block_rows), jnp.int32),
+            pltpu.SemaphoreType.DMA((4,)),
         ],
         compiler_params=limit(2),
         name="load",
-    )(hbm(tile_column[:, 0].T), hbm(tile_live[:, 0].T), hbm(tile_values[:, 0]))
-    row_bits = bits(sources)
-    left_bits = row_bits[:0:-1] + row_bits[:1]
-    right_bits = row_bits[:1] + row_bits[:0:-1]
-    left, right = left[None], right[None]
-    left_order, right_order = [0], [0]
-    for left_bit, right_bit in zip(left_bits, right_bits):
-        new_left = swap(left, left_bit, 0)
-        new_right = swap(right, right_bit, 0)
-        if left_bit == left_bits[0]:
-            new_left, share = lax.optimization_barrier((new_left, share))
-            other_share = swap(share, 0, bits(groups)[-1] | 1)
-        elif left_bit == left_bits[-1]:
-            new_left, other_share = lax.optimization_barrier((new_left, other_share))
-        left = jnp.concatenate([left, new_left], axis=0)
-        right = jnp.concatenate([right, new_right], axis=0)
-        left_order = left_order + [at ^ left_bit for at in left_order]
-        right_order = right_order + [at ^ right_bit for at in right_order]
-    many = groups // 2
-    keep, send = pl.pallas_call(
-        lambda *refs: tile_kernel(sources, groups, per_piece, left_order, right_order, *refs),
-        out_shape=[
-            jax.ShapeDtypeStruct((many, vectors, owned), F32),
+    )(hbm(tile_column[:, 0].T), hbm(tile_live[:, 0].T), hbm(tile_values[:, 0]), left, right)
+    index = pltpu.with_memory_space_constraint(index, pltpu.SMEM)
+    lhs = pltpu.VMEM((2, 4 * vectors, slot_width), BF16)
+    table, send = pl.pallas_call(
+        lambda *refs: send_kernel(groups, per_piece, late, *refs),
+        out_shape=[
+            jax.ShapeDtypeStruct(table_shape, BF16),
             jax.ShapeDtypeStruct((many, vectors, owned), BF16),
         ],
-        in_specs=[smem(), vmem(), vmem(), vmem()],
+        in_specs=[smem()] + [vmem()] * 4,
         out_specs=[vmem(), vmem()],
-        scratch_shapes=[
-            pltpu.VMEM((sources * per_piece + 1, vectors, 2 * height), BF16),
-            pltpu.VMEM((2, 4 * vectors, slot_width), BF16),
-        ],
-        compiler_params=limit(12),
-        name="tiles",
-    )(index, left, right, panel)
+        scratch_shapes=[lhs],
+        input_output_aliases={2: 0},
+        compiler_params=limit(8),
+        name="send",
+    )(index, panel, table, new_left, new_right)
+    keep = pl.pallas_call(
+        lambda *refs: keep_kernel(groups, per_piece, *refs),
+        out_shape=jax.ShapeDtypeStruct((many, vectors, owned), F32),
+        in_specs=[smem(), vmem(), vmem()],
+        out_specs=vmem(),
+        scratch_shapes=[lhs],
+        compiler_params=limit(8),
+        name="keep",
+    )(index, panel, table)
     col_bits = bits(groups)
     last = col_bits.pop()
     for bit in col_bits:

time: 45.6 us -> 44.8 us (0.982)
  starting transfers between devices: 21.7 us -> 16.4 us
  waiting for transfers between devices: 15 us -> 20 us
  Pallas kernels: 7.88 us -> 7.38 us
    ppermute x13 -> x12, starting transfers between devices: 21.7 us -> 16.4 us  [swap(): return lax.ppermute(value, ('row', 'col'), pairs)]
    ppermute x13 -> x12, waiting for transfers between devices: 15 us -> 20 us  [swap(): return lax.ppermute(value, ('row', 'col'), pairs)]
    pallas_call x2 -> x3, Pallas kernels: 3.03 us -> 2.46 us  [the longest x1 0.87 us: on_device(): pl.pallas_call(lambda *refs: send_kernel(groups, per_piece, late, *refs),...]
  transfers between devices with their start and end apart: 13 -> 12, of which waited for: 11 -> 11; matrix products, arithmetic and copies ran while one was open for 0% -> 0% of each run, Pallas kernels for 4% -> 5%
where the time goes in v5:
time: 44.8 us; the launch traced here: 44.6 us
  waiting for transfers between devices  20 us (45%)
  starting transfers between devices  16.4 us (37%)
  Pallas kernels  7.38 us (16%)
  between operations  0.7 us (2%)
    ppermute x12, waiting for transfers between devices, swap(): return lax.ppermute(value, ('row', 'col'), pairs)  20 us
    ppermute x12, starting transfers between devices, swap(): return lax.ppermute(value, ('row', 'col'), pairs)  16.4 us
    pallas_call x1, Pallas kernels, on_device(): pl.pallas_call(lambda *refs: finish_kernel(total_rows, *refs), out_shape=...  2.7 us
    pallas_call x1, Pallas kernels, on_device(): pl.pallas_call(lambda *refs: load_kernel(per_piece, sources * per_piece,...  1.72 us
  transfers between devices with their start and end apart: 12, of which 11 were waited for; matrix products, arithmetic and copies ran while one was open for 0% of the time, Pallas kernels for 5%

profile of v5, /device:TPU:0, one launch (start us, length us, event | category | flops | bytes accessed | tf_op | source)
XLA Modules:
  0.0 44.6 jit_solution(1300320760319722988)
XLA Ops:
  0.6 0.9 %scale.1 = (bf16[64,512]{1,0:T(8,128)(2,1)S(1)}, bf16[80,512]{1,0:T(8,128)(2,1)S(1)}) custom-call(bf16[64,512]{1,0:T(8,128)(2,1)} %basis_ref.1, s32[1,512]{1,0:T(1,128)} %bitcast.19), custom_call_target="tpu_custom_call" | custom-call | tf_op jit(solution)/shard_map/scale/pallas_call | solution.py:241
  1.5 4.1 %collective-permute-start = (bf16[64,512]{1,0:T(8,128)(2,1)S(1)}, bf16[64,512]{1,0:T(8,128)(2,1)S(1)}, u32[]{:S(2)}, u32[]{:S(2)}) collective-permute-start(bf16[64,512]{1,0:T(8,128)(2,1)S(1)} %get-tuple-element.14), channel_id=1, source_target_pairs={{0,16},{1,17},{2,18},{3,19},{4,20},{5,21},{6,22},{7,23},{8,24},{9,... | collective-permute-start | bytes 196616 | tf_op jit(solution)/shard_map/ppermute | solution.py:33
  5.6 0.7 %collective-permute-start.1 = (bf16[80,512]{1,0:T(8,128)(2,1)S(1)}, bf16[80,512]{1,0:T(8,128)(2,1)S(1)}, u32[]{:S(2)}, u32[]{:S(2)}) collective-permute-start(bf16[80,512]{1,0:T(8,128)(2,1)S(1)} %get-tuple-element.13.refs_0_), channel_id=1, source_target_pairs={{0,3},{1,2},{2,1},{3,0},{4,7},{5,6},{6,5},{7,4},{8,11},{9,10},{10,... | collective-permute-start | bytes 245768 | tf_op jit(solution)/shard_map/ppermute | solution.py:33
  6.3 3.0 %collective-permute-done = bf16[64,512]{1,0:T(8,128)(2,1)S(1)} collective-permute-done((bf16[64,512]{1,0:T(8,128)(2,1)S(1)}, bf16[64,512]{1,0:T(8,128)(2,1)S(1)}, u32[]{:S(2)}, u32[]{:S(2)}) %collective-permute-start) | collective-permute-done | bytes 65568 | tf_op jit(solution)/shard_map/ppermute | solution.py:33
  9.2 1.0 %collective-permute-done.1.refs_1_ = bf16[80,512]{1,0:T(8,128)(2,1)S(1)} collective-permute-done((bf16[80,512]{1,0:T(8,128)(2,1)S(1)}, bf16[80,512]{1,0:T(8,128)(2,1)S(1)}, u32[]{:S(2)}, u32[]{:S(2)}) %collective-permute-start.1) | collective-permute-done | bytes 81952 | tf_op jit(solution)/shard_map/ppermute | solution.py:33
  10.3 1.6 %collective-permute-start.3 = (bf16[2,64,256]{2,1,0:T(8,128)(2,1)S(1)}, bf16[2,64,256]{2,1,0:T(8,128)(2,1)S(1)}, u32[]{:S(2)}, u32[]{:S(2)}) collective-permute-start(bf16[2,64,256]{2,1,0:T(8,128)(2,1)S(1)} %pad_maximum_fusion.3), channel_id=1, source_target_pairs={{0,4},{1,5},{2,6},{3,7},{4,0},{5,1},{6,2},{7,3},{8,12},{9,13},{10,... | collective-permute-start | bytes 196616 | tf_op jit(solution)/shard_map/ppermute | solution.py:33
  11.8 1.6 %collective-permute-start.2 = (bf16[2,64,256]{2,1,0:T(8,128)(2,1)S(1)}, bf16[2,64,256]{2,1,0:T(8,128)(2,1)S(1)}, u32[]{:S(2)}, u32[]{:S(2)}) collective-permute-start(bf16[2,64,256]{2,1,0:T(8,128)(2,1)S(1)} %pad_maximum_fusion.2), channel_id=1, source_target_pairs={{0,8},{1,9},{2,10},{3,11},{4,12},{5,13},{6,14},{7,15},{8,0},{9,1},... | collective-permute-start | bytes 196616 | tf_op jit(solution)/shard_map/ppermute | solution.py:33
  13.5 1.1 %collective-permute-done.3 = bf16[2,64,256]{2,1,0:T(8,128)(2,1)S(1)} collective-permute-done((bf16[2,64,256]{2,1,0:T(8,128)(2,1)S(1)}, bf16[2,64,256]{2,1,0:T(8,128)(2,1)S(1)}, u32[]{:S(2)}, u32[]{:S(2)}) %collective-permute-start.3) | collective-permute-done | bytes 65568 | tf_op jit(solution)/shard_map/ppermute | solution.py:33
  14.6 1.6 %collective-permute-start.5 = (bf16[4,64,256]{2,1,0:T(8,128)(2,1)S(1)}, bf16[4,64,256]{2,1,0:T(8,128)(2,1)S(1)}, u32[]{:S(2)}, u32[]{:S(2)}) collective-permute-start(bf16[4,64,256]{2,1,0:T(8,128)(2,1)S(1)} %pad_maximum_fusion.1.refs_4_), channel_id=1, source_target_pairs={{0,8},{1,9},{2,10},{3,11},{4,12},{5,13},{6,14},{7,15},{8,0},{9,1},... | collective-permute-start | bytes 393224 | tf_op jit(solution)/shard_map/ppermute | solution.py:33
  16.3 0.0 collective-permute-done.2
  16.3 1.6 %collective-permute-start.4 = (bf16[4,64,256]{2,1,0:T(8,128)(2,1)S(1)}, bf16[4,64,256]{2,1,0:T(8,128)(2,1)S(1)}, u32[]{:S(2)}, u32[]{:S(2)}) collective-permute-start(bf16[4,64,256]{2,1,0:T(8,128)(2,1)S(1)} %pad_maximum_fusion.refs_3_), channel_id=1, source_target_pairs={{0,4},{1,5},{2,6},{3,7},{4,0},{5,1},{6,2},{7,3},{8,12},{9,13},{10,... | collective-permute-start | bytes 393224 | tf_op jit(solution)/shard_map/ppermute | solution.py:33
  17.9 1.7 %load.1 = (s32[8,32]{1,0:T(8,128)S(4)}, bf16[32,64,512]{2,1,0:T(8,128)(2,1)S(1)}, bf16[65,64,128]{2,1,0:T(8,128)(2,1)S(1)}) custom-call(s32[8,32]{1,0:T(8,128)} %bitcast.17, s32[8,32]{1,0:T(8,128)} %bitcast.18, bf16[32,64,512]{2,1,0:T(8,128)(2,1)} %bitcast.16, bf16[4,64,256]{2,1,0:T(8,128)(2,1)S(1)} %pad_maximum_fusion.refs_3_, ...), custom_call_target="tpu_custom_call" | custom-call | tf_op jit(solution)/shard_map/load/pallas_call | solution.py:273
  19.6 0.1 collective-permute-done.5.refs_4_
  19.7 1.7 %collective-permute-done.4.refs_3_ = bf16[4,64,256]{2,1,0:T(8,128)(2,1)S(1)} collective-permute-done((bf16[4,64,256]{2,1,0:T(8,128)(2,1)S(1)}, bf16[4,64,256]{2,1,0:T(8,128)(2,1)S(1)}, u32[]{:S(2)}, u32[]{:S(2)}) %collective-permute-start.4) | collective-permute-done | bytes 131104 | tf_op jit(solution)/shard_map/ppermute | solution.py:33
  21.3 0.9 %send.1 = (bf16[65,64,128]{2,1,0:T(8,128)(2,1)S(1)}, bf16[2,64,512]{2,1,0:T(8,128)(2,1)S(1)}) custom-call(s32[8,32]{1,0:T(8,128)S(4)} %get-tuple-element.17.refs_0_, bf16[32,64,512]{2,1,0:T(8,128)(2,1)S(1)} %get-tuple-element.18.refs_1_, bf16[65,64,128]{2,1,0:T(8,128)(2,1)S(1)} %get-tuple-element.19.refs_2_, ...), custom_call_target="tpu_custom_call", output_to_operand_aliasing={{0}: (2, {})} | custom-call | tf_op jit(solution)/shard_map/send/pallas_call | solution.py:293
  22.2 0.1 collective-permute-start.6
  22.3 0.7 %keep.1 = f32[2,64,512]{2,1,0:T(8,128)S(1)} custom-call(s32[8,32]{1,0:T(8,128)S(4)} %get-tuple-element.17.refs_0_, bf16[32,64,512]{2,1,0:T(8,128)(2,1)S(1)} %get-tuple-element.18.refs_1_, bf16[65,64,128]{2,1,0:T(8,128)(2,1)S(1)} %get-tuple-element.20.refs_2_), custom_call_target="tpu_custom_call" | custom-call | tf_op jit(solution)/shard_map/keep/pallas_call | solution.py:306
  23.0 0.6 %collective-permute-done.6 = bf16[2,64,512]{2,1,0:T(8,128)(2,1)S(1)} collective-permute-done((bf16[2,64,512]{2,1,0:T(8,128)(2,1)S(1)}, bf16[2,64,512]{2,1,0:T(8,128)(2,1)S(1)}, u32[]{:S(2)}, u32[]{:S(2)}) %collective-permute-start.6) | collective-permute-done | bytes 131104 | tf_op jit(solution)/shard_map/ppermute | solution.py:33
  23.7 1.3 %collective-permute-start.7 = (bf16[2,64,512]{2,1,0:T(8,128)(2,1)S(1)}, bf16[2,64,512]{2,1,0:T(8,128)(2,1)S(1)}, u32[]{:S(2)}, u32[]{:S(2)}) collective-permute-start(bf16[2,64,512]{2,1,0:T(8,128)(2,1)S(1)} %add_convert_fusion.refs_2_), channel_id=1, source_target_pairs={{0,3},{1,2},{2,1},{3,0},{4,7},{5,6},{6,5},{7,4},{8,11},{9,10},{10,... | collective-permute-start | bytes 393224 | tf_op jit(solution)/shard_map/ppermute | solution.py:33
  25.0 4.2 %collective-permute-done.7.refs_3_ = bf16[2,64,512]{2,1,0:T(8,128)(2,1)S(1)} collective-permute-done((bf16[2,64,512]{2,1,0:T(8,128)(2,1)S(1)}, bf16[2,64,512]{2,1,0:T(8,128)(2,1)S(1)}, u32[]{:S(2)}, u32[]{:S(2)}) %collective-permute-start.7) | collective-permute-done | bytes 131104 | tf_op jit(solution)/shard_map/ppermute | solution.py:33
  29.2 0.5 %gram.1 = (bf16[192,512]{1,0:T(8,128)(2,1)S(1)}, f32[64,128]{1,0:T(8,128)S(1)}) custom-call(bf16[80,512]{1,0:T(8,128)(2,1)S(1)} %get-tuple-element.13.refs_0_, bf16[80,512]{1,0:T(8,128)(2,1)S(1)} %collective-permute-done.1.refs_1_, bf16[2,64,512]{2,1,0:T(8,128)(2,1)S(1)} %add_convert_fusion.refs_2_, bf16[2,64,512]{2,1,0:T(8,128)(2,1)S(1)} %collective-permute-done.7.refs_3_), custom_call_target="tpu_custom_call" | custom-call | tf_op jit(solution)/shard_map/gram/pallas_call | solution.py:324
  29.7 0.2 collective-permute-start.8
  29.9 1.1 %collective-permute-done.8 = f32[64,128]{1,0:T(8,128)S(1)} collective-permute-done((f32[64,128]{1,0:T(8,128)S(1)}, f32[64,128]{1,0:T(8,128)S(1)}, u32[]{:S(2)}, u32[]{:S(2)}) %collective-permute-start.8) | collective-permute-done | bytes 32800 | tf_op jit(solution)/shard_map/ppermute | solution.py:33
  31.0 1.3 %collective-permute-start.9 = (f32[64,128]{1,0:T(8,128)S(1)}, f32[64,128]{1,0:T(8,128)S(1)}, u32[]{:S(2)}, u32[]{:S(2)}) collective-permute-start(f32[64,128]{1,0:T(8,128)S(1)} %add.16), channel_id=1, source_target_pairs={{0,5},{1,4},{2,7},{3,6},{4,1},{5,0},{6,3},{7,2},{8,13},{9,12},{10,... | collective-permute-start | bytes 98312 | tf_op jit(solution)/shard_map/ppermute | solution.py:33
  32.2 2.1 %collective-permute-done.9 = f32[64,128]{1,0:T(8,128)S(1)} collective-permute-done((f32[64,128]{1,0:T(8,128)S(1)}, f32[64,128]{1,0:T(8,128)S(1)}, u32[]{:S(2)}, u32[]{:S(2)}) %collective-permute-start.9) | collective-permute-done | bytes 32800 | tf_op jit(solution)/shard_map/ppermute | solution.py:33
  34.3 1.2 %collective-permute-start.10 = (f32[64,128]{1,0:T(8,128)S(1)}, f32[64,128]{1,0:T(8,128)S(1)}, u32[]{:S(2)}, u32[]{:S(2)}) collective-permute-start(f32[64,128]{1,0:T(8,128)S(1)} %add.17), channel_id=1, source_target_pairs={{0,9},{1,8},{2,11},{3,10},{4,13},{5,12},{6,15},{7,14},{8,1},{9,0},... | collective-permute-start | bytes 98312 | tf_op jit(solution)/shard_map/ppermute | solution.py:33
  35.6 2.1 %collective-permute-done.10 = f32[64,128]{1,0:T(8,128)S(1)} collective-permute-done((f32[64,128]{1,0:T(8,128)S(1)}, f32[64,128]{1,0:T(8,128)S(1)}, u32[]{:S(2)}, u32[]{:S(2)}) %collective-permute-start.10) | collective-permute-done | bytes 32800 | tf_op jit(solution)/shard_map/ppermute | solution.py:33
  37.7 1.2 %collective-permute-start.11 = (f32[64,128]{1,0:T(8,128)S(1)}, f32[64,128]{1,0:T(8,128)S(1)}, u32[]{:S(2)}, u32[]{:S(2)}) collective-permute-start(f32[64,128]{1,0:T(8,128)S(1)} %add.18), channel_id=1, source_target_pairs={{0,17},{1,16},{2,19},{3,18},{4,21},{5,20},{6,23},{7,22},{8,25},{9,... | collective-permute-start | bytes 98312 | tf_op jit(solution)/shard_map/ppermute | solution.py:33
  38.9 3.1 %collective-permute-done.11 = f32[64,128]{1,0:T(8,128)S(1)} collective-permute-done((f32[64,128]{1,0:T(8,128)S(1)}, f32[64,128]{1,0:T(8,128)S(1)}, u32[]{:S(2)}, u32[]{:S(2)}) %collective-permute-start.11) | collective-permute-done | bytes 32800 | tf_op jit(solution)/shard_map/ppermute | solution.py:33
  41.9 2.7 %finish.1 = (f32[64,512]{1,0:T(8,128)}, f32[64,64]{1,0:T(8,128)}) custom-call(f32[64,128]{1,0:T(8,128)S(1)} %add.19.refs_0_, bf16[192,512]{1,0:T(8,128)(2,1)S(1)} %get-tuple-element.23.refs_1_), custom_call_target="tpu_custom_call" | custom-call | tf_op jit(solution)/shard_map/finish/pallas_call | solution.py:341
  (11 shorter events, 0.1 us)
Async XLA Ops:
  1.5 7.8 %collective-permute-start = (bf16[64,512]{1,0:T(8,128)(2,1)S(1)}, bf16[64,512]{1,0:T(8,128)(2,1)S(1)}, u32[]{:S(2)}, u32[]{:S(2)}) collective-permute-start(bf16[64,512]{1,0:T(8,128)(2,1)S(1)} %get-tuple-element.14), channel_id=1, source_target_pairs={{0,16},{1,17},{2,18},{3,19},{4,20},{5,21},{6,22},{7,23},{8,24},{9,... | collective-permute-start | bytes 196616 | tf_op jit(solution)/shard_map/ppermute | solution.py:33
  5.6 4.7 %collective-permute-start.1 = (bf16[80,512]{1,0:T(8,128)(2,1)S(1)}, bf16[80,512]{1,0:T(8,128)(2,1)S(1)}, u32[]{:S(2)}, u32[]{:S(2)}) collective-permute-start(bf16[80,512]{1,0:T(8,128)(2,1)S(1)} %get-tuple-element.13.refs_0_), channel_id=1, source_target_pairs={{0,3},{1,2},{2,1},{3,0},{4,7},{5,6},{6,5},{7,4},{8,11},{9,10},{10,... | collective-permute-start | bytes 245768 | tf_op jit(solution)/shard_map/ppermute | solution.py:33
  10.3 4.3 %collective-permute-start.3 = (bf16[2,64,256]{2,1,0:T(8,128)(2,1)S(1)}, bf16[2,64,256]{2,1,0:T(8,128)(2,1)S(1)}, u32[]{:S(2)}, u32[]{:S(2)}) collective-permute-start(bf16[2,64,256]{2,1,0:T(8,128)(2,1)S(1)} %pad_maximum_fusion.3), channel_id=1, source_target_pairs={{0,4},{1,5},{2,6},{3,7},{4,0},{5,1},{6,2},{7,3},{8,12},{9,13},{10,... | collective-permute-start | bytes 196616 | tf_op jit(solution)/shard_map/ppermute | solution.py:33
  11.8 4.4 %collective-permute-start.2 = (bf16[2,64,256]{2,1,0:T(8,128)(2,1)S(1)}, bf16[2,64,256]{2,1,0:T(8,128)(2,1)S(1)}, u32[]{:S(2)}, u32[]{:S(2)}) collective-permute-start(bf16[2,64,256]{2,1,0:T(8,128)(2,1)S(1)} %pad_maximum_fusion.2), channel_id=1, source_target_pairs={{0,8},{1,9},{2,10},{3,11},{4,12},{5,13},{6,14},{7,15},{8,0},{9,1},... | collective-permute-start | bytes 196616 | tf_op jit(solution)/shard_map/ppermute | solution.py:33
  14.6 5.0 %collective-permute-start.5 = (bf16[4,64,256]{2,1,0:T(8,128)(2,1)S(1)}, bf16[4,64,256]{2,1,0:T(8,128)(2,1)S(1)}, u32[]{:S(2)}, u32[]{:S(2)}) collective-permute-start(bf16[4,64,256]{2,1,0:T(8,128)(2,1)S(1)} %pad_maximum_fusion.1.refs_4_), channel_id=1, source_target_pairs={{0,8},{1,9},{2,10},{3,11},{4,12},{5,13},{6,14},{7,15},{8,0},{9,1},... | collective-permute-start | bytes 393224 | tf_op jit(solution)/shard_map/ppermute | solution.py:33
  16.3 5.0 %collective-permute-start.4 = (bf16[4,64,256]{2,1,0:T(8,128)(2,1)S(1)}, bf16[4,64,256]{2,1,0:T(8,128)(2,1)S(1)}, u32[]{:S(2)}, u32[]{:S(2)}) collective-permute-start(bf16[4,64,256]{2,1,0:T(8,128)(2,1)S(1)} %pad_maximum_fusion.refs_3_), channel_id=1, source_target_pairs={{0,4},{1,5},{2,6},{3,7},{4,0},{5,1},{6,2},{7,3},{8,12},{9,13},{10,... | collective-permute-start | bytes 393224 | tf_op jit(solution)/shard_map/ppermute | solution.py:33
  22.2 1.4 %collective-permute-start.6 = (bf16[2,64,512]{2,1,0:T(8,128)(2,1)S(1)}, bf16[2,64,512]{2,1,0:T(8,128)(2,1)S(1)}, u32[]{:S(2)}, u32[]{:S(2)}) collective-permute-start(bf16[2,64,512]{2,1,0:T(8,128)(2,1)S(1)} %get-tuple-element.21), channel_id=1, source_target_pairs={{0,1},{1,0},{2,3},{3,2},{4,5},{5,4},{6,7},{7,6},{8,9},{9,8},{10,11... | collective-permute-start | bytes 393224 | tf_op jit(solution)/shard_map/ppermute | solution.py:33
  23.7 5.5 %collective-permute-start.7 = (bf16[2,64,512]{2,1,0:T(8,128)(2,1)S(1)}, bf16[2,64,512]{2,1,0:T(8,128)(2,1)S(1)}, u32[]{:S(2)}, u32[]{:S(2)}) collective-permute-start(bf16[2,64,512]{2,1,0:T(8,128)(2,1)S(1)} %add_convert_fusion.refs_2_), channel_id=1, source_target_pairs={{0,3},{1,2},{2,1},{3,0},{4,7},{5,6},{6,5},{7,4},{8,11},{9,10},{10,... | collective-permute-start | bytes 393224 | tf_op jit(solution)/shard_map/ppermute | solution.py:33
  29.7 1.3 %collective-permute-start.8 = (f32[64,128]{1,0:T(8,128)S(1)}, f32[64,128]{1,0:T(8,128)S(1)}, u32[]{:S(2)}, u32[]{:S(2)}) collective-permute-start(f32[64,128]{1,0:T(8,128)S(1)} %get-tuple-element.22), channel_id=1, source_target_pairs={{0,1},{1,0},{2,3},{3,2},{4,5},{5,4},{6,7},{7,6},{8,9},{9,8},{10,11... | collective-permute-start | bytes 98312 | tf_op jit(solution)/shard_map/ppermute | solution.py:33
  31.0 3.3 %collective-permute-start.9 = (f32[64,128]{1,0:T(8,128)S(1)}, f32[64,128]{1,0:T(8,128)S(1)}, u32[]{:S(2)}, u32[]{:S(2)}) collective-permute-start(f32[64,128]{1,0:T(8,128)S(1)} %add.16), channel_id=1, source_target_pairs={{0,5},{1,4},{2,7},{3,6},{4,1},{5,0},{6,3},{7,2},{8,13},{9,12},{10,... | collective-permute-start | bytes 98312 | tf_op jit(solution)/shard_map/ppermute | solution.py:33
  34.3 3.3 %collective-permute-start.10 = (f32[64,128]{1,0:T(8,128)S(1)}, f32[64,128]{1,0:T(8,128)S(1)}, u32[]{:S(2)}, u32[]{:S(2)}) collective-permute-start(f32[64,128]{1,0:T(8,128)S(1)} %add.17), channel_id=1, source_target_pairs={{0,9},{1,8},{2,11},{3,10},{4,13},{5,12},{6,15},{7,14},{8,1},{9,0},... | collective-permute-start | bytes 98312 | tf_op jit(solution)/shard_map/ppermute | solution.py:33
  37.7 4.2 %collective-permute-start.11 = (f32[64,128]{1,0:T(8,128)S(1)}, f32[64,128]{1,0:T(8,128)S(1)}, u32[]{:S(2)}, u32[]{:S(2)}) collective-permute-start(f32[64,128]{1,0:T(8,128)S(1)} %add.18), channel_id=1, source_target_pairs={{0,17},{1,16},{2,19},{3,18},{4,21},{5,20},{6,23},{7,22},{8,25},{9,... | collective-permute-start | bytes 98312 | tf_op jit(solution)/shard_map/ppermute | solution.py:33

commit v6 on v5

--- a/solution.py
+++ b/solution.py
@@ -59,19 +59,17 @@
     share_ref[vectors:, :] = jnp.broadcast_to(degree, (16, owned)).astype(BF16)
 
 
-def fill_table(table_ref, per_piece, height, orders, refs):
+def fill_table(table_ref, per_piece, height, sources, tiles_of):
     wide = 2 * height
-    pairs = refs[0].shape[2] // wide
-    for side, (order, ref) in enumerate(zip(orders, refs)):
-        for at, source in enumerate(order):
-            for pair in range(pairs):
-                tile = ref[at, :, pair * wide:(pair + 1) * wide]
-                block = source * per_piece + 2 * (side * pairs + pair)
-                table_ref[block] = tile
-                table_ref[block + 1] = jnp.concatenate([tile[:, height:], tile[:, :height]], axis=1)
-
-
-def load_kernel(per_piece, zero_at, orders, column_in, live_in, panel_in, left_ref, right_ref, index_ref, panel_ref,
+    for source, ref in zip(sources, tiles_of):
+        for pair in range(per_piece // 2):
+            tile = ref[:, pair * wide:(pair + 1) * wide]
+            block = source * per_piece + 2 * pair
+            table_ref[block] = tile
+            table_ref[block + 1] = jnp.concatenate([tile[:, height:], tile[:, :height]], axis=1)
+
+
+def load_kernel(per_piece, zero_at, order, column_in, live_in, panel_in, near_ref, index_ref, panel_ref,
                 table_ref, column_ref, live_ref, work_ref, sem):
     copies = [
         pltpu.make_async_copy(column_in, column_ref, sem.at[0]),
@@ -80,7 +78,7 @@
     ]
     for copy in copies:
         copy.start()
-    fill_table(table_ref, per_piece, panel_ref.shape[1], orders, (left_ref, right_ref))
+    fill_table(table_ref, per_piece, panel_ref.shape[1], order, [near_ref.at[at] for at in range(len(order))])
     table_ref[zero_at] = jnp.zeros(table_ref.shape[1:], BF16)
     copies[0].wait()
     copies[1].wait()
@@ -139,10 +137,10 @@
         lax.fori_loop(0, groups // 2, body, 0)
 
 
-def send_kernel(groups, per_piece, orders, index_ref, panel_ref, table_in, left_ref, right_ref, table_ref, send_ref,
-                lhs_ref):
-    del table_in
-    fill_table(table_ref, per_piece, panel_ref.shape[1], orders, (left_ref, right_ref))
+def send_kernel(groups, per_piece, orders, index_ref, panel_ref, table_in, *refs):
+    table_ref, send_ref, lhs_ref = refs[len(orders):]
+    for order, ref in zip(orders, refs):
+        fill_table(table_ref, per_piece, panel_ref.shape[1], order, [ref.at[at] for at in range(len(order))])
     multiply(groups, per_piece, 1, index_ref, panel_ref, table_ref, lhs_ref, send_ref)
 
 
@@ -236,7 +234,6 @@
     sources = lax.axis_size("row")
     groups = lax.axis_size("col")
     per_piece = owned // height
-    half = owned // 2
     degree_row = degree.reshape(1, owned)
     scaled, share = pl.pallas_call(
         scale_kernel,
@@ -252,32 +249,37 @@
     row_bits = bits(sources)
     top = row_bits.pop()
     other = swap(scaled, top, 0)
+    low = row_bits[:2]
+    diag = low[0] | low[1]
+    other, share = lax.optimization_barrier((other, share))
+    blocks = [(0, scaled), (top, other)]
+    for bit in row_bits[:1:-1]:
+        stack = swap(jnp.stack([block for _, block in blocks]), bit, 0)
+        blocks = blocks + [(at ^ bit, stack[place]) for place, (at, _) in enumerate(blocks)]
+    base = [at for at, _ in blocks]
+    named = dict(blocks)
+    direct = [mask for mask in (low[0], low[1], diag)]
+    relayed = [(mask, at) for at in base[1:] for mask in (low[0], low[1], diag) if (mask ^ at) not in direct]
+    pieces = [(mask, swap(scaled, mask, 0)) for mask in direct]
+    early = blocks + pieces[:2]
+    late = pieces[2:] + [(mask ^ at, swap(named[at], mask, 0)) for mask, at in relayed]
     other_share = swap(share, 0, bits(groups)[-1] | 1)
-    other, other_share = lax.optimization_barrier((other, other_share))
-    left = jnp.stack([scaled[:, :half], other[:, :half]])
-    right = jnp.stack([scaled[:, half:], other[:, half:]])
-    left_order, right_order = [0, top], [0, top]
-    for left_bit, right_bit in zip(row_bits[::-1], row_bits):
-        if left_bit != row_bits[-1]:
-            left = jnp.concatenate([left, new_left], axis=0)
-            right = jnp.concatenate([right, new_right], axis=0)
-        early = (left_order, right_order)
-        new_left = swap(left, left_bit, 0)
-        new_right = swap(right, right_bit, 0)
-        late = ([at ^ left_bit for at in left_order], [at ^ right_bit for at in right_order])
-        left_order = left_order + late[0]
-        right_order = right_order + late[1]
+    order = [at for at, _ in early]
+    whole = jnp.stack([block for _, block in early])
+    far = [block[None] for _, block in late]
+    late = [[at] for at, _ in late]
+    far[0], other_share = lax.optimization_barrier((far[0], other_share))
     slots = tile_column.shape[2]
     many = groups // 2
     table_shape = (sources * per_piece + 1, vectors, 2 * height)
     index, panel, table = pl.pallas_call(
-        lambda *refs: load_kernel(per_piece, sources * per_piece, early, *refs),
+        lambda *refs: load_kernel(per_piece, sources * per_piece, order, *refs),
         out_shape=[
             pltpu.SMEM((slots, block_rows), jnp.int32),
             jax.ShapeDtypeStruct((block_rows, height, slot_width), BF16),
             jax.ShapeDtypeStruct(table_shape, BF16),
         ],
-        in_specs=[pl.BlockSpec(memory_space=pl.ANY)] * 3 + [vmem()] * 2,
+        in_specs=[pl.BlockSpec(memory_space=pl.ANY)] * 3 + [vmem()],
         out_specs=[smem(), vmem(), vmem()],
         scratch_shapes=[
             pltpu.VMEM((slots, block_rows), jnp.int32),
@@ -287,7 +289,7 @@
         ],
         compiler_params=limit(2),
         name="load",
-    )(hbm(tile_column[:, 0].T), hbm(tile_live[:, 0].T), hbm(tile_values[:, 0]), left, right)
+    )(hbm(tile_column[:, 0].T), hbm(tile_live[:, 0].T), hbm(tile_values[:, 0]), whole)
     index = pltpu.with_memory_space_constraint(index, pltpu.SMEM)
     lhs = pltpu.VMEM((2, 4 * vectors, slot_width), BF16)
     table, send = pl.pallas_call(
@@ -296,13 +298,13 @@
             jax.ShapeDtypeStruct(table_shape, BF16),
             jax.ShapeDtypeStruct((many, vectors, owned), BF16),
         ],
-        in_specs=[smem()] + [vmem()] * 4,
+        in_specs=[smem()] + [vmem()] * (2 + len(far)),
         out_specs=[vmem(), vmem()],
         scratch_shapes=[lhs],
         input_output_aliases={2: 0},
         compiler_params=limit(8),
         name="send",
-    )(index, panel, table, new_left, new_right)
+    )(index, panel, table, *far)
     keep = pl.pallas_call(
         lambda *refs: keep_kernel(groups, per_piece, *refs),
         out_shape=jax.ShapeDtypeStruct((many, vectors, owned), F32),

time: 44.8 us -> 41 us (0.915)
  waiting for transfers between devices: 20 us -> 16 us
    ppermute x12 -> x14, waiting for transfers between devices: 20 us -> 16 us  [swap(): return lax.ppermute(value, ('row', 'col'), pairs)]
    ppermute x12 -> x14, starting transfers between devices: 16.4 us -> 16.6 us  [swap(): return lax.ppermute(value, ('row', 'col'), pairs)]
  transfers between devices with their start and end apart: 12 -> 14, of which waited for: 11 -> 8; matrix products, arithmetic and copies ran while one was open for 0% -> 0% of each run, Pallas kernels for 5% -> 6%
where the time goes in v6:
time: 41 us; the launch traced here: 40.8 us
  starting transfers between devices  16.6 us (40%)
  waiting for transfers between devices  16 us (39%)
  Pallas kernels  7.38 us (18%)
  between operations  0.7 us (2%)
    ppermute x14, starting transfers between devices, swap(): return lax.ppermute(value, ('row', 'col'), pairs)  16.6 us
    ppermute x14, waiting for transfers between devices, swap(): return lax.ppermute(value, ('row', 'col'), pairs)  16 us
    pallas_call x1, Pallas kernels, on_device(): pl.pallas_call(lambda *refs: finish_kernel(total_rows, *refs), out_shape=...  2.7 us
    pallas_call x1, Pallas kernels, on_device(): pl.pallas_call(lambda *refs: load_kernel(per_piece, sources * per_piece,...  1.72 us
    pallas_call x1, Pallas kernels, on_device(): pl.pallas_call(lambda *refs: send_kernel(groups, per_piece, late, *refs),...  0.88 us
    pallas_call x1, Pallas kernels, on_device(): pl.pallas_call(scale_kernel, out_shape=[jax.ShapeDtypeStruct((vectors, ow...  0.86 us
  transfers between devices with their start and end apart: 14, of which 8 were waited for; matrix products, arithmetic and copies ran while one was open for 0% of the time, Pallas kernels for 6%

profile of v6, /device:TPU:0, one launch (start us, length us, event | category | flops | bytes accessed | tf_op | source)
XLA Modules:
  0.0 40.8 jit_solution(3766850062526522094)
XLA Ops:
  0.6 0.9 %scale.1 = (bf16[64,512]{1,0:T(8,128)(2,1)S(1)}, bf16[80,512]{1,0:T(8,128)(2,1)S(1)}) custom-call(bf16[64,512]{1,0:T(8,128)(2,1)} %basis_ref.1, s32[1,512]{1,0:T(1,128)} %bitcast.27), custom_call_target="tpu_custom_call" | custom-call | tf_op jit(solution)/shard_map/scale/pallas_call | solution.py:238
  1.5 4.1 %collective-permute-start = (bf16[64,512]{1,0:T(8,128)(2,1)S(1)}, bf16[64,512]{1,0:T(8,128)(2,1)S(1)}, u32[]{:S(2)}, u32[]{:S(2)}) collective-permute-start(bf16[64,512]{1,0:T(8,128)(2,1)S(1)} %get-tuple-element.15), channel_id=1, source_target_pairs={{0,16},{1,17},{2,18},{3,19},{4,20},{5,21},{6,22},{7,23},{8,24},{9,... | collective-permute-start | bytes 196616 | tf_op jit(solution)/shard_map/ppermute | solution.py:33
  5.6 1.6 %collective-permute-start.4 = (bf16[64,512]{1,0:T(8,128)(2,1)S(1)}, bf16[64,512]{1,0:T(8,128)(2,1)S(1)}, u32[]{:S(2)}, u32[]{:S(2)}) collective-permute-start(bf16[64,512]{1,0:T(8,128)(2,1)S(1)} %get-tuple-element.15), channel_id=1, source_target_pairs={{0,8},{1,9},{2,10},{3,11},{4,12},{5,13},{6,14},{7,15},{8,0},{9,1},... | collective-permute-start | bytes 196616 | tf_op jit(solution)/shard_map/ppermute | solution.py:33
  7.2 1.5 %collective-permute-start.3 = (bf16[64,512]{1,0:T(8,128)(2,1)S(1)}, bf16[64,512]{1,0:T(8,128)(2,1)S(1)}, u32[]{:S(2)}, u32[]{:S(2)}) collective-permute-start(bf16[64,512]{1,0:T(8,128)(2,1)S(1)} %get-tuple-element.15), channel_id=1, source_target_pairs={{0,4},{1,5},{2,6},{3,7},{4,0},{5,1},{6,2},{7,3},{8,12},{9,13},{10,... | collective-permute-start | bytes 196616 | tf_op jit(solution)/shard_map/ppermute | solution.py:33
  8.7 0.4 %collective-permute-start.1 = (bf16[64,512]{1,0:T(8,128)(2,1)S(1)}, bf16[64,512]{1,0:T(8,128)(2,1)S(1)}, u32[]{:S(2)}, u32[]{:S(2)}) collective-permute-start(bf16[64,512]{1,0:T(8,128)(2,1)S(1)} %get-tuple-element.15), channel_id=1, source_target_pairs={{0,12},{1,13},{2,14},{3,15},{4,8},{5,9},{6,10},{7,11},{8,4},{9,5},... | collective-permute-start | bytes 196616 | tf_op jit(solution)/shard_map/ppermute | solution.py:33
  9.1 0.0 collective-permute-done
  9.1 2.5 %collective-permute-start.7 = (bf16[64,512]{1,0:T(8,128)(2,1)S(1)}, bf16[64,512]{1,0:T(8,128)(2,1)S(1)}, u32[]{:S(2)}, u32[]{:S(2)}) collective-permute-start(bf16[64,512]{1,0:T(8,128)(2,1)S(1)} %collective-permute-done), channel_id=1, source_target_pairs={{0,12},{1,13},{2,14},{3,15},{4,8},{5,9},{6,10},{7,11},{8,4},{9,5},... | collective-permute-start | bytes 196616 | tf_op jit(solution)/shard_map/ppermute | solution.py:33
  11.6 0.4 %collective-permute-start.6 = (bf16[64,512]{1,0:T(8,128)(2,1)S(1)}, bf16[64,512]{1,0:T(8,128)(2,1)S(1)}, u32[]{:S(2)}, u32[]{:S(2)}) collective-permute-start(bf16[64,512]{1,0:T(8,128)(2,1)S(1)} %collective-permute-done), channel_id=1, source_target_pairs={{0,8},{1,9},{2,10},{3,11},{4,12},{5,13},{6,14},{7,15},{8,0},{9,1},... | collective-permute-start | bytes 196616 | tf_op jit(solution)/shard_map/ppermute | solution.py:33
  12.0 0.0 collective-permute-done.4
  12.0 0.5 %collective-permute-start.5 = (bf16[64,512]{1,0:T(8,128)(2,1)S(1)}, bf16[64,512]{1,0:T(8,128)(2,1)S(1)}, u32[]{:S(2)}, u32[]{:S(2)}) collective-permute-start(bf16[64,512]{1,0:T(8,128)(2,1)S(1)} %collective-permute-done), channel_id=1, source_target_pairs={{0,4},{1,5},{2,6},{3,7},{4,0},{5,1},{6,2},{7,3},{8,12},{9,13},{10,... | collective-permute-start | bytes 196616 | tf_op jit(solution)/shard_map/ppermute | solution.py:33
  12.6 0.3 collective-permute-done.3
  12.8 0.0 collective-permute-start.2
  12.9 1.7 %load.1 = (s32[8,32]{1,0:T(8,128)S(4)}, bf16[32,64,512]{2,1,0:T(8,128)(2,1)S(1)}, bf16[65,64,128]{2,1,0:T(8,128)(2,1)S(1)}) custom-call(s32[8,32]{1,0:T(8,128)} %bitcast.25, s32[8,32]{1,0:T(8,128)} %bitcast.26, bf16[32,64,512]{2,1,0:T(8,128)(2,1)} %bitcast.21, bf16[4,64,512]{2,1,0:T(8,128)(2,1)S(1)} %pad_maximum_fusion.refs_3_), custom_call_target="tpu_custom_call" | custom-call | tf_op jit(solution)/shard_map/load/pallas_call | solution.py:275
  14.6 0.0 collective-permute-done.1
  14.6 2.9 %collective-permute-done.2.refs_1_ = bf16[80,512]{1,0:T(8,128)(2,1)S(1)} collective-permute-done((bf16[80,512]{1,0:T(8,128)(2,1)S(1)}, bf16[80,512]{1,0:T(8,128)(2,1)S(1)}, u32[]{:S(2)}, u32[]{:S(2)}) %collective-permute-start.2) | collective-permute-done | bytes 81952 | tf_op jit(solution)/shard_map/ppermute | solution.py:33
  17.5 0.0 collective-permute-done.7
  17.5 0.0 collective-permute-done.6
  17.5 0.0 collective-permute-done.5
  17.5 0.9 %send.1 = (bf16[65,64,128]{2,1,0:T(8,128)(2,1)S(1)}, bf16[2,64,512]{2,1,0:T(8,128)(2,1)S(1)}) custom-call(s32[8,32]{1,0:T(8,128)S(4)} %get-tuple-element.20.refs_0_, bf16[32,64,512]{2,1,0:T(8,128)(2,1)S(1)} %get-tuple-element.21.refs_1_, bf16[65,64,128]{2,1,0:T(8,128)(2,1)S(1)} %get-tuple-element.22.refs_2_, ...), custom_call_target="tpu_custom_call", output_to_operand_aliasing={{0}: (2, {})} | custom-call | tf_op jit(solution)/shard_map/send/pallas_call | solution.py:295
  18.4 0.2 collective-permute-start.8
  18.6 0.7 %keep.1 = f32[2,64,512]{2,1,0:T(8,128)S(1)} custom-call(s32[8,32]{1,0:T(8,128)S(4)} %get-tuple-element.20.refs_0_, bf16[32,64,512]{2,1,0:T(8,128)(2,1)S(1)} %get-tuple-element.21.refs_1_, bf16[65,64,128]{2,1,0:T(8,128)(2,1)S(1)} %get-tuple-element.24.refs_2_), custom_call_target="tpu_custom_call" | custom-call | tf_op jit(solution)/shard_map/keep/pallas_call | solution.py:308
  19.3 0.5 %collective-permute-done.8 = bf16[2,64,512]{2,1,0:T(8,128)(2,1)S(1)} collective-permute-done((bf16[2,64,512]{2,1,0:T(8,128)(2,1)S(1)}, bf16[2,64,512]{2,1,0:T(8,128)(2,1)S(1)}, u32[]{:S(2)}, u32[]{:S(2)}) %collective-permute-start.8) | collective-permute-done | bytes 131104 | tf_op jit(solution)/shard_map/ppermute | solution.py:33
  19.9 0.5 %collective-permute-start.9 = (bf16[2,64,512]{2,1,0:T(8,128)(2,1)S(1)}, bf16[2,64,512]{2,1,0:T(8,128)(2,1)S(1)}, u32[]{:S(2)}, u32[]{:S(2)}) collective-permute-start(bf16[2,64,512]{2,1,0:T(8,128)(2,1)S(1)} %add_convert_fusion.refs_2_), channel_id=1, source_target_pairs={{0,3},{1,2},{2,1},{3,0},{4,7},{5,6},{6,5},{7,4},{8,11},{9,10},{10,... | collective-permute-start | bytes 393224 | tf_op jit(solution)/shard_map/ppermute | solution.py:33
  20.4 5.0 %collective-permute-done.9.refs_3_ = bf16[2,64,512]{2,1,0:T(8,128)(2,1)S(1)} collective-permute-done((bf16[2,64,512]{2,1,0:T(8,128)(2,1)S(1)}, bf16[2,64,512]{2,1,0:T(8,128)(2,1)S(1)}, u32[]{:S(2)}, u32[]{:S(2)}) %collective-permute-start.9) | collective-permute-done | bytes 131104 | tf_op jit(solution)/shard_map/ppermute | solution.py:33
  25.4 0.5 %gram.1 = (bf16[192,512]{1,0:T(8,128)(2,1)S(1)}, f32[64,128]{1,0:T(8,128)S(1)}) custom-call(bf16[80,512]{1,0:T(8,128)(2,1)S(1)} %get-tuple-element.17.refs_0_, bf16[80,512]{1,0:T(8,128)(2,1)S(1)} %collective-permute-done.2.refs_1_, bf16[2,64,512]{2,1,0:T(8,128)(2,1)S(1)} %add_convert_fusion.refs_2_, bf16[2,64,512]{2,1,0:T(8,128)(2,1)S(1)} %collective-permute-done.9.refs_3_), custom_call_target="tpu_custom_call" | custom-call | tf_op jit(solution)/shard_map/gram/pallas_call | solution.py:326
  25.9 0.2 collective-permute-start.10
  26.1 1.1 %collective-permute-done.10 = f32[64,128]{1,0:T(8,128)S(1)} collective-permute-done((f32[64,128]{1,0:T(8,128)S(1)}, f32[64,128]{1,0:T(8,128)S(1)}, u32[]{:S(2)}, u32[]{:S(2)}) %collective-permute-start.10) | collective-permute-done | bytes 32800 | tf_op jit(solution)/shard_map/ppermute | solution.py:33
  27.2 1.7 %collective-permute-start.11 = (f32[64,128]{1,0:T(8,128)S(1)}, f32[64,128]{1,0:T(8,128)S(1)}, u32[]{:S(2)}, u32[]{:S(2)}) collective-permute-start(f32[64,128]{1,0:T(8,128)S(1)} %add.16), channel_id=1, source_target_pairs={{0,5},{1,4},{2,7},{3,6},{4,1},{5,0},{6,3},{7,2},{8,13},{9,12},{10,... | collective-permute-start | bytes 98312 | tf_op jit(solution)/shard_map/ppermute | solution.py:33
  28.8 1.7 %collective-permute-done.11 = f32[64,128]{1,0:T(8,128)S(1)} collective-permute-done((f32[64,128]{1,0:T(8,128)S(1)}, f32[64,128]{1,0:T(8,128)S(1)}, u32[]{:S(2)}, u32[]{:S(2)}) %collective-permute-start.11) | collective-permute-done | bytes 32800 | tf_op jit(solution)/shard_map/ppermute | solution.py:33
  30.5 1.1 %collective-permute-start.12 = (f32[64,128]{1,0:T(8,128)S(1)}, f32[64,128]{1,0:T(8,128)S(1)}, u32[]{:S(2)}, u32[]{:S(2)}) collective-permute-start(f32[64,128]{1,0:T(8,128)S(1)} %add.17), channel_id=1, source_target_pairs={{0,9},{1,8},{2,11},{3,10},{4,13},{5,12},{6,15},{7,14},{8,1},{9,0},... | collective-permute-start | bytes 98312 | tf_op jit(solution)/shard_map/ppermute | solution.py:33
  31.6 2.2 %collective-permute-done.12 = f32[64,128]{1,0:T(8,128)S(1)} collective-permute-done((f32[64,128]{1,0:T(8,128)S(1)}, f32[64,128]{1,0:T(8,128)S(1)}, u32[]{:S(2)}, u32[]{:S(2)}) %collective-permute-start.12) | collective-permute-done | bytes 32800 | tf_op jit(solution)/shard_map/ppermute | solution.py:33
  33.9 1.8 %collective-permute-start.13 = (f32[64,128]{1,0:T(8,128)S(1)}, f32[64,128]{1,0:T(8,128)S(1)}, u32[]{:S(2)}, u32[]{:S(2)}) collective-permute-start(f32[64,128]{1,0:T(8,128)S(1)} %add.18), channel_id=1, source_target_pairs={{0,17},{1,16},{2,19},{3,18},{4,21},{5,20},{6,23},{7,22},{8,25},{9,... | collective-permute-start | bytes 98312 | tf_op jit(solution)/shard_map/ppermute | solution.py:33
  35.7 2.4 %collective-permute-done.13 = f32[64,128]{1,0:T(8,128)S(1)} collective-permute-done((f32[64,128]{1,0:T(8,128)S(1)}, f32[64,128]{1,0:T(8,128)S(1)}, u32[]{:S(2)}, u32[]{:S(2)}) %collective-permute-start.13) | collective-permute-done | bytes 32800 | tf_op jit(solution)/shard_map/ppermute | solution.py:33
  38.1 2.7 %finish.1 = (f32[64,512]{1,0:T(8,128)}, f32[64,64]{1,0:T(8,128)}) custom-call(f32[64,128]{1,0:T(8,128)S(1)} %add.19.refs_0_, bf16[192,512]{1,0:T(8,128)(2,1)S(1)} %get-tuple-element.27.refs_1_), custom_call_target="tpu_custom_call" | custom-call | tf_op jit(solution)/shard_map/finish/pallas_call | solution.py:343
  (6 shorter events, 0.1 us)
Async XLA Ops:
  1.5 7.6 %collective-permute-start = (bf16[64,512]{1,0:T(8,128)(2,1)S(1)}, bf16[64,512]{1,0:T(8,128)(2,1)S(1)}, u32[]{:S(2)}, u32[]{:S(2)}) collective-permute-start(bf16[64,512]{1,0:T(8,128)(2,1)S(1)} %get-tuple-element.15), channel_id=1, source_target_pairs={{0,16},{1,17},{2,18},{3,19},{4,20},{5,21},{6,22},{7,23},{8,24},{9,... | collective-permute-start | bytes 196616 | tf_op jit(solution)/shard_map/ppermute | solution.py:33
  5.6 6.5 %collective-permute-start.4 = (bf16[64,512]{1,0:T(8,128)(2,1)S(1)}, bf16[64,512]{1,0:T(8,128)(2,1)S(1)}, u32[]{:S(2)}, u32[]{:S(2)}) collective-permute-start(bf16[64,512]{1,0:T(8,128)(2,1)S(1)} %get-tuple-element.15), channel_id=1, source_target_pairs={{0,8},{1,9},{2,10},{3,11},{4,12},{5,13},{6,14},{7,15},{8,0},{9,1},... | collective-permute-start | bytes 196616 | tf_op jit(solution)/shard_map/ppermute | solution.py:33
  7.2 5.7 %collective-permute-start.3 = (bf16[64,512]{1,0:T(8,128)(2,1)S(1)}, bf16[64,512]{1,0:T(8,128)(2,1)S(1)}, u32[]{:S(2)}, u32[]{:S(2)}) collective-permute-start(bf16[64,512]{1,0:T(8,128)(2,1)S(1)} %get-tuple-element.15), channel_id=1, source_target_pairs={{0,4},{1,5},{2,6},{3,7},{4,0},{5,1},{6,2},{7,3},{8,12},{9,13},{10,... | collective-permute-start | bytes 196616 | tf_op jit(solution)/shard_map/ppermute | solution.py:33
  8.7 6.0 %collective-permute-start.1 = (bf16[64,512]{1,0:T(8,128)(2,1)S(1)}, bf16[64,512]{1,0:T(8,128)(2,1)S(1)}, u32[]{:S(2)}, u32[]{:S(2)}) collective-permute-start(bf16[64,512]{1,0:T(8,128)(2,1)S(1)} %get-tuple-element.15), channel_id=1, source_target_pairs={{0,12},{1,13},{2,14},{3,15},{4,8},{5,9},{6,10},{7,11},{8,4},{9,5},... | collective-permute-start | bytes 196616 | tf_op jit(solution)/shard_map/ppermute | solution.py:33
  9.1 8.4 %collective-permute-start.7 = (bf16[64,512]{1,0:T(8,128)(2,1)S(1)}, bf16[64,512]{1,0:T(8,128)(2,1)S(1)}, u32[]{:S(2)}, u32[]{:S(2)}) collective-permute-start(bf16[64,512]{1,0:T(8,128)(2,1)S(1)} %collective-permute-done), channel_id=1, source_target_pairs={{0,12},{1,13},{2,14},{3,15},{4,8},{5,9},{6,10},{7,11},{8,4},{9,5},... | collective-permute-start | bytes 196616 | tf_op jit(solution)/shard_map/ppermute | solution.py:33
  11.6 5.9 %collective-permute-start.6 = (bf16[64,512]{1,0:T(8,128)(2,1)S(1)}, bf16[64,512]{1,0:T(8,128)(2,1)S(1)}, u32[]{:S(2)}, u32[]{:S(2)}) collective-permute-start(bf16[64,512]{1,0:T(8,128)(2,1)S(1)} %collective-permute-done), channel_id=1, source_target_pairs={{0,8},{1,9},{2,10},{3,11},{4,12},{5,13},{6,14},{7,15},{8,0},{9,1},... | collective-permute-start | bytes 196616 | tf_op jit(solution)/shard_map/ppermute | solution.py:33
  12.0 5.5 %collective-permute-start.5 = (bf16[64,512]{1,0:T(8,128)(2,1)S(1)}, bf16[64,512]{1,0:T(8,128)(2,1)S(1)}, u32[]{:S(2)}, u32[]{:S(2)}) collective-permute-start(bf16[64,512]{1,0:T(8,128)(2,1)S(1)} %collective-permute-done), channel_id=1, source_target_pairs={{0,4},{1,5},{2,6},{3,7},{4,0},{5,1},{6,2},{7,3},{8,12},{9,13},{10,... | collective-permute-start | bytes 196616 | tf_op jit(solution)/shard_map/ppermute | solution.py:33
  12.8 4.7 %collective-permute-start.2 = (bf16[80,512]{1,0:T(8,128)(2,1)S(1)}, bf16[80,512]{1,0:T(8,128)(2,1)S(1)}, u32[]{:S(2)}, u32[]{:S(2)}) collective-permute-start(bf16[80,512]{1,0:T(8,128)(2,1)S(1)} %get-tuple-element.17.refs_0_), channel_id=1, source_target_pairs={{0,3},{1,2},{2,1},{3,0},{4,7},{5,6},{6,5},{7,4},{8,11},{9,10},{10,... | collective-permute-start | bytes 245768 | tf_op jit(solution)/shard_map/ppermute | solution.py:33
  18.4 1.4 %collective-permute-start.8 = (bf16[2,64,512]{2,1,0:T(8,128)(2,1)S(1)}, bf16[2,64,512]{2,1,0:T(8,128)(2,1)S(1)}, u32[]{:S(2)}, u32[]{:S(2)}) collective-permute-start(bf16[2,64,512]{2,1,0:T(8,128)(2,1)S(1)} %get-tuple-element.25), channel_id=1, source_target_pairs={{0,1},{1,0},{2,3},{3,2},{4,5},{5,4},{6,7},{7,6},{8,9},{9,8},{10,11... | collective-permute-start | bytes 393224 | tf_op jit(solution)/shard_map/ppermute | solution.py:33
  19.9 5.5 %collective-permute-start.9 = (bf16[2,64,512]{2,1,0:T(8,128)(2,1)S(1)}, bf16[2,64,512]{2,1,0:T(8,128)(2,1)S(1)}, u32[]{:S(2)}, u32[]{:S(2)}) collective-permute-start(bf16[2,64,512]{2,1,0:T(8,128)(2,1)S(1)} %add_convert_fusion.refs_2_), channel_id=1, source_target_pairs={{0,3},{1,2},{2,1},{3,0},{4,7},{5,6},{6,5},{7,4},{8,11},{9,10},{10,... | collective-permute-start | bytes 393224 | tf_op jit(solution)/shard_map/ppermute | solution.py:33
  25.9 1.3 %collective-permute-start.10 = (f32[64,128]{1,0:T(8,128)S(1)}, f32[64,128]{1,0:T(8,128)S(1)}, u32[]{:S(2)}, u32[]{:S(2)}) collective-permute-start(f32[64,128]{1,0:T(8,128)S(1)} %get-tuple-element.26), channel_id=1, source_target_pairs={{0,1},{1,0},{2,3},{3,2},{4,5},{5,4},{6,7},{7,6},{8,9},{9,8},{10,11... | collective-permute-start | bytes 98312 | tf_op jit(solution)/shard_map/ppermute | solution.py:33
  27.2 3.3 %collective-permute-start.11 = (f32[64,128]{1,0:T(8,128)S(1)}, f32[64,128]{1,0:T(8,128)S(1)}, u32[]{:S(2)}, u32[]{:S(2)}) collective-permute-start(f32[64,128]{1,0:T(8,128)S(1)} %add.16), channel_id=1, source_target_pairs={{0,5},{1,4},{2,7},{3,6},{4,1},{5,0},{6,3},{7,2},{8,13},{9,12},{10,... | collective-permute-start | bytes 98312 | tf_op jit(solution)/shard_map/ppermute | solution.py:33
  30.5 3.3 %collective-permute-start.12 = (f32[64,128]{1,0:T(8,128)S(1)}, f32[64,128]{1,0:T(8,128)S(1)}, u32[]{:S(2)}, u32[]{:S(2)}) collective-permute-start(f32[64,128]{1,0:T(8,128)S(1)} %add.17), channel_id=1, source_target_pairs={{0,9},{1,8},{2,11},{3,10},{4,13},{5,12},{6,15},{7,14},{8,1},{9,0},... | collective-permute-start | bytes 98312 | tf_op jit(solution)/shard_map/ppermute | solution.py:33
  33.9 4.2 %collective-permute-start.13 = (f32[64,128]{1,0:T(8,128)S(1)}, f32[64,128]{1,0:T(8,128)S(1)}, u32[]{:S(2)}, u32[]{:S(2)}) collective-permute-start(f32[64,128]{1,0:T(8,128)S(1)} %add.18), channel_id=1, source_target_pairs={{0,17},{1,16},{2,19},{3,18},{4,21},{5,20},{6,23},{7,22},{8,25},{9,... | collective-permute-start | bytes 98312 | tf_op jit(solution)/shard_map/ppermute | solution.py:33

commit v7 on v6

--- a/solution.py
+++ b/solution.py
@@ -211,12 +211,14 @@
             pivot_row = down(tiles[home], at)
             entries = [down(own[later], at) for later in range(height)]
             for place, column in enumerate(columns):
-                factor = column[at] * scale
-                if place == 0:
-                    factor = jnp.where(below > at, factor, 0.0)
+                lower = jnp.where(below > at, column[at], 0.0) if place == 0 else column[at]
+                factor = lower * scale
                 tiles[home + place] = tiles[home + place] - factor * pivot_row
                 for later in range(at + 1, height):
-                    column[later] = column[later] - factor * entries[later]
+                    if place == 0 and later == at + 1:
+                        column[later] = column[later] - (lower * entries[later]) * scale
+                    else:
+                        column[later] = column[later] - factor * entries[later]
     done = jnp.concatenate(tiles, axis=0)
     pivot = jnp.sum(jnp.where(lane == row, done, 0.0), axis=1, keepdims=True)
     inverse = done * (lax.rsqrt(pivot) * math.sqrt(total_rows))
@@ -268,7 +270,6 @@
     whole = jnp.stack([block for _, block in early])
     far = [block[None] for _, block in late]
     late = [[at] for at, _ in late]
-    far[0], other_share = lax.optimization_barrier((far[0], other_share))
     slots = tile_column.shape[2]
     many = groups // 2
     table_shape = (sources * per_piece + 1, vectors, 2 * height)
@@ -305,6 +306,7 @@
         compiler_params=limit(8),
         name="send",
     )(index, panel, table, *far)
+    send, other_share = lax.optimization_barrier((send, other_share))
     keep = pl.pallas_call(
         lambda *refs: keep_kernel(groups, per_piece, *refs),
         out_shape=jax.ShapeDtypeStruct((many, vectors, owned), F32),
@@ -337,8 +339,11 @@
     )(share, other_share, sums, got)
     for bit in col_bits:
         gram = gram + swap(gram, 0, bit | 1)
-    for bit in bits(sources):
+    row_bits = bits(sources)
+    for bit in row_bits[2:]:
         gram = gram + swap(gram, bit, 1)
+    near = [swap(gram, mask, 1) for mask in (row_bits[0] | row_bits[1], row_bits[0], row_bits[1])]
+    gram = (gram + near[0]) + (near[1] + near[2])
     total_rows = sources * groups * owned
     orthonormal, quotient = pl.pallas_call(
         lambda *refs: finish_kernel(total_rows, *refs),

time: 41 us -> 40.6 us (level)
  waiting for transfers between devices: 16 us -> 13.9 us
  starting transfers between devices: 16.6 us -> 18.3 us
    ppermute x14 -> x15, waiting for transfers between devices: 16 us -> 13.9 us  [swap(): return lax.ppermute(value, ('row', 'col'), pairs)]
    ppermute x14 -> x15, starting transfers between devices: 16.6 us -> 18.3 us  [swap(): return lax.ppermute(value, ('row', 'col'), pairs)]
  transfers between devices with their start and end apart: 14 -> 15, of which waited for: 8 -> 8; matrix products, arithmetic and copies ran while one was open for 0% -> 0% of each run, Pallas kernels for 6% -> 6%
where the time goes in v7:
time: 40.6 us; the launch traced here: 40.4 us
  starting transfers between devices  18.3 us (45%)
  waiting for transfers between devices  13.9 us (34%)
  Pallas kernels  7.32 us (18%)
  between operations  0.73 us (2%)
    ppermute x15, starting transfers between devices, swap(): return lax.ppermute(value, ('row', 'col'), pairs)  18.3 us
    ppermute x15, waiting for transfers between devices, swap(): return lax.ppermute(value, ('row', 'col'), pairs)  13.9 us
    pallas_call x1, Pallas kernels, on_device(): pl.pallas_call(lambda *refs: finish_kernel(total_rows, *refs), out_shape=...  2.64 us
    pallas_call x1, Pallas kernels, on_device(): pl.pallas_call(lambda *refs: load_kernel(per_piece, sources * per_piece,...  1.72 us
    pallas_call x1, Pallas kernels, on_device(): pl.pallas_call(lambda *refs: send_kernel(groups, per_piece, late, *refs),...  0.88 us
    pallas_call x1, Pallas kernels, on_device(): pl.pallas_call(scale_kernel, out_shape=[jax.ShapeDtypeStruct((vectors, ow...  0.86 us
  transfers between devices with their start and end apart: 15, of which 8 were waited for; matrix products, arithmetic and copies ran while one was open for 0% of the time, Pallas kernels for 6%

profile of v7, /device:TPU:0, one launch (start us, length us, event | category | flops | bytes accessed | tf_op | source)
XLA Modules:
  0.0 40.4 jit_solution(15262871147471410868)
XLA Ops:
  0.6 0.9 %scale.1 = (bf16[64,512]{1,0:T(8,128)(2,1)S(1)}, bf16[80,512]{1,0:T(8,128)(2,1)S(1)}) custom-call(bf16[64,512]{1,0:T(8,128)(2,1)} %basis_ref.1, s32[1,512]{1,0:T(1,128)} %bitcast.27), custom_call_target="tpu_custom_call" | custom-call | tf_op jit(solution)/shard_map/scale/pallas_call | solution.py:240
  1.5 4.1 %collective-permute-start = (bf16[64,512]{1,0:T(8,128)(2,1)S(1)}, bf16[64,512]{1,0:T(8,128)(2,1)S(1)}, u32[]{:S(2)}, u32[]{:S(2)}) collective-permute-start(bf16[64,512]{1,0:T(8,128)(2,1)S(1)} %get-tuple-element.15), channel_id=1, source_target_pairs={{0,16},{1,17},{2,18},{3,19},{4,20},{5,21},{6,22},{7,23},{8,24},{9,... | collective-permute-start | bytes 196616 | tf_op jit(solution)/shard_map/ppermute | solution.py:33
  5.6 1.6 %collective-permute-start.2 = (bf16[64,512]{1,0:T(8,128)(2,1)S(1)}, bf16[64,512]{1,0:T(8,128)(2,1)S(1)}, u32[]{:S(2)}, u32[]{:S(2)}) collective-permute-start(bf16[64,512]{1,0:T(8,128)(2,1)S(1)} %get-tuple-element.15), channel_id=1, source_target_pairs={{0,8},{1,9},{2,10},{3,11},{4,12},{5,13},{6,14},{7,15},{8,0},{9,1},... | collective-permute-start | bytes 196616 | tf_op jit(solution)/shard_map/ppermute | solution.py:33
  7.2 1.5 %collective-permute-start.1 = (bf16[64,512]{1,0:T(8,128)(2,1)S(1)}, bf16[64,512]{1,0:T(8,128)(2,1)S(1)}, u32[]{:S(2)}, u32[]{:S(2)}) collective-permute-start(bf16[64,512]{1,0:T(8,128)(2,1)S(1)} %get-tuple-element.15), channel_id=1, source_target_pairs={{0,4},{1,5},{2,6},{3,7},{4,0},{5,1},{6,2},{7,3},{8,12},{9,13},{10,... | collective-permute-start | bytes 196616 | tf_op jit(solution)/shard_map/ppermute | solution.py:33
  8.7 0.4 %collective-permute-start.3 = (bf16[64,512]{1,0:T(8,128)(2,1)S(1)}, bf16[64,512]{1,0:T(8,128)(2,1)S(1)}, u32[]{:S(2)}, u32[]{:S(2)}) collective-permute-start(bf16[64,512]{1,0:T(8,128)(2,1)S(1)} %get-tuple-element.15), channel_id=1, source_target_pairs={{0,12},{1,13},{2,14},{3,15},{4,8},{5,9},{6,10},{7,11},{8,4},{9,5},... | collective-permute-start | bytes 196616 | tf_op jit(solution)/shard_map/ppermute | solution.py:33
  9.1 0.0 collective-permute-done
  9.1 1.5 %collective-permute-start.4 = (bf16[64,512]{1,0:T(8,128)(2,1)S(1)}, bf16[64,512]{1,0:T(8,128)(2,1)S(1)}, u32[]{:S(2)}, u32[]{:S(2)}) collective-permute-start(bf16[64,512]{1,0:T(8,128)(2,1)S(1)} %collective-permute-done), channel_id=1, source_target_pairs={{0,4},{1,5},{2,6},{3,7},{4,0},{5,1},{6,2},{7,3},{8,12},{9,13},{10,... | collective-permute-start | bytes 196616 | tf_op jit(solution)/shard_map/ppermute | solution.py:33
  10.6 1.6 %collective-permute-start.5 = (bf16[64,512]{1,0:T(8,128)(2,1)S(1)}, bf16[64,512]{1,0:T(8,128)(2,1)S(1)}, u32[]{:S(2)}, u32[]{:S(2)}) collective-permute-start(bf16[64,512]{1,0:T(8,128)(2,1)S(1)} %collective-permute-done), channel_id=1, source_target_pairs={{0,8},{1,9},{2,10},{3,11},{4,12},{5,13},{6,14},{7,15},{8,0},{9,1},... | collective-permute-start | bytes 196616 | tf_op jit(solution)/shard_map/ppermute | solution.py:33
  12.2 0.0 collective-permute-done.2
  12.2 0.8 %collective-permute-start.6 = (bf16[64,512]{1,0:T(8,128)(2,1)S(1)}, bf16[64,512]{1,0:T(8,128)(2,1)S(1)}, u32[]{:S(2)}, u32[]{:S(2)}) collective-permute-start(bf16[64,512]{1,0:T(8,128)(2,1)S(1)} %collective-permute-done), channel_id=1, source_target_pairs={{0,12},{1,13},{2,14},{3,15},{4,8},{5,9},{6,10},{7,11},{8,4},{9,5},... | collective-permute-start | bytes 196616 | tf_op jit(solution)/shard_map/ppermute | solution.py:33
  13.0 0.0 collective-permute-done.1
  13.0 0.0 collective-permute-start.7
  13.1 1.7 %load.1 = (s32[8,32]{1,0:T(8,128)S(4)}, bf16[32,64,512]{2,1,0:T(8,128)(2,1)S(1)}, bf16[65,64,128]{2,1,0:T(8,128)(2,1)S(1)}) custom-call(s32[8,32]{1,0:T(8,128)} %bitcast.25, s32[8,32]{1,0:T(8,128)} %bitcast.26, bf16[32,64,512]{2,1,0:T(8,128)(2,1)} %bitcast.21, bf16[4,64,512]{2,1,0:T(8,128)(2,1)S(1)} %pad_maximum_fusion.refs_3_), custom_call_target="tpu_custom_call" | custom-call | tf_op jit(solution)/shard_map/load/pallas_call | solution.py:276
  14.8 0.0 collective-permute-done.3
  14.8 0.0 collective-permute-done.4
  14.8 0.0 collective-permute-done.5
  14.8 2.5 %collective-permute-done.6 = bf16[64,512]{1,0:T(8,128)(2,1)S(1)} collective-permute-done((bf16[64,512]{1,0:T(8,128)(2,1)S(1)}, bf16[64,512]{1,0:T(8,128)(2,1)S(1)}, u32[]{:S(2)}, u32[]{:S(2)}) %collective-permute-start.6) | collective-permute-done | bytes 65568 | tf_op jit(solution)/shard_map/ppermute | solution.py:33
  17.3 0.9 %send.1 = (bf16[65,64,128]{2,1,0:T(8,128)(2,1)S(1)}, bf16[2,64,512]{2,1,0:T(8,128)(2,1)S(1)}) custom-call(s32[8,32]{1,0:T(8,128)S(4)} %get-tuple-element.19.refs_0_, bf16[32,64,512]{2,1,0:T(8,128)(2,1)S(1)} %get-tuple-element.20.refs_1_, bf16[65,64,128]{2,1,0:T(8,128)(2,1)S(1)} %get-tuple-element.21.refs_2_, ...), custom_call_target="tpu_custom_call", output_to_operand_aliasing={{0}: (2, {})} | custom-call | tf_op jit(solution)/shard_map/send/pallas_call | solution.py:296
  18.2 0.0 collective-permute-done.7.refs_1_
  18.2 0.1 collective-permute-start.8
  18.3 0.7 %keep.1 = f32[2,64,512]{2,1,0:T(8,128)S(1)} custom-call(s32[8,32]{1,0:T(8,128)S(4)} %get-tuple-element.19.refs_0_, bf16[32,64,512]{2,1,0:T(8,128)(2,1)S(1)} %get-tuple-element.20.refs_1_, bf16[65,64,128]{2,1,0:T(8,128)(2,1)S(1)} %get-tuple-element.24.refs_2_), custom_call_target="tpu_custom_call" | custom-call | tf_op jit(solution)/shard_map/keep/pallas_call | solution.py:310
  19.0 0.6 %collective-permute-done.8 = bf16[2,64,512]{2,1,0:T(8,128)(2,1)S(1)} collective-permute-done((bf16[2,64,512]{2,1,0:T(8,128)(2,1)S(1)}, bf16[2,64,512]{2,1,0:T(8,128)(2,1)S(1)}, u32[]{:S(2)}, u32[]{:S(2)}) %collective-permute-start.8) | collective-permute-done | bytes 131104 | tf_op jit(solution)/shard_map/ppermute | solution.py:33
  19.7 1.3 %collective-permute-start.9 = (bf16[2,64,512]{2,1,0:T(8,128)(2,1)S(1)}, bf16[2,64,512]{2,1,0:T(8,128)(2,1)S(1)}, u32[]{:S(2)}, u32[]{:S(2)}) collective-permute-start(bf16[2,64,512]{2,1,0:T(8,128)(2,1)S(1)} %add_convert_fusion.refs_2_), channel_id=1, source_target_pairs={{0,3},{1,2},{2,1},{3,0},{4,7},{5,6},{6,5},{7,4},{8,11},{9,10},{10,... | collective-permute-start | bytes 393224 | tf_op jit(solution)/shard_map/ppermute | solution.py:33
  21.0 4.2 %collective-permute-done.9.refs_3_ = bf16[2,64,512]{2,1,0:T(8,128)(2,1)S(1)} collective-permute-done((bf16[2,64,512]{2,1,0:T(8,128)(2,1)S(1)}, bf16[2,64,512]{2,1,0:T(8,128)(2,1)S(1)}, u32[]{:S(2)}, u32[]{:S(2)}) %collective-permute-start.9) | collective-permute-done | bytes 131104 | tf_op jit(solution)/shard_map/ppermute | solution.py:33
  25.2 0.5 %gram.1 = (bf16[192,512]{1,0:T(8,128)(2,1)S(1)}, f32[64,128]{1,0:T(8,128)S(1)}) custom-call(bf16[80,512]{1,0:T(8,128)(2,1)S(1)} %get-tuple-element.17.refs_0_, bf16[80,512]{1,0:T(8,128)(2,1)S(1)} %collective-permute-done.7.refs_1_, bf16[2,64,512]{2,1,0:T(8,128)(2,1)S(1)} %add_convert_fusion.refs_2_, bf16[2,64,512]{2,1,0:T(8,128)(2,1)S(1)} %collective-permute-done.9.refs_3_), custom_call_target="tpu_custom_call" | custom-call | tf_op jit(solution)/shard_map/gram/pallas_call | solution.py:328
  25.7 0.2 collective-permute-start.10
  25.9 1.1 %collective-permute-done.10 = f32[64,128]{1,0:T(8,128)S(1)} collective-permute-done((f32[64,128]{1,0:T(8,128)S(1)}, f32[64,128]{1,0:T(8,128)S(1)}, u32[]{:S(2)}, u32[]{:S(2)}) %collective-permute-start.10) | collective-permute-done | bytes 32800 | tf_op jit(solution)/shard_map/ppermute | solution.py:33
  27.0 2.3 %collective-permute-start.11 = (f32[64,128]{1,0:T(8,128)S(1)}, f32[64,128]{1,0:T(8,128)S(1)}, u32[]{:S(2)}, u32[]{:S(2)}) collective-permute-start(f32[64,128]{1,0:T(8,128)S(1)} %add.19), channel_id=1, source_target_pairs={{0,17},{1,16},{2,19},{3,18},{4,21},{5,20},{6,23},{7,22},{8,25},{9,... | collective-permute-start | bytes 98312 | tf_op jit(solution)/shard_map/ppermute | solution.py:33
  29.3 2.9 %collective-permute-done.11 = f32[64,128]{1,0:T(8,128)S(1)} collective-permute-done((f32[64,128]{1,0:T(8,128)S(1)}, f32[64,128]{1,0:T(8,128)S(1)}, u32[]{:S(2)}, u32[]{:S(2)}) %collective-permute-start.11) | collective-permute-done | bytes 32800 | tf_op jit(solution)/shard_map/ppermute | solution.py:33
  32.2 0.0 collective-permute-start.13
  32.2 0.9 %collective-permute-start.14 = (f32[64,128]{1,0:T(8,128)S(1)}, f32[64,128]{1,0:T(8,128)S(1)}, u32[]{:S(2)}, u32[]{:S(2)}) collective-permute-start(f32[64,128]{1,0:T(8,128)S(1)} %add.20), channel_id=1, source_target_pairs={{0,9},{1,8},{2,11},{3,10},{4,13},{5,12},{6,15},{7,14},{8,1},{9,0},... | collective-permute-start | bytes 98312 | tf_op jit(solution)/shard_map/ppermute | solution.py:33
  33.2 2.0 %collective-permute-start.12 = (f32[64,128]{1,0:T(8,128)S(1)}, f32[64,128]{1,0:T(8,128)S(1)}, u32[]{:S(2)}, u32[]{:S(2)}) collective-permute-start(f32[64,128]{1,0:T(8,128)S(1)} %add.20), channel_id=1, source_target_pairs={{0,13},{1,12},{2,15},{3,14},{4,9},{5,8},{6,11},{7,10},{8,5},{9,4},... | collective-permute-start | bytes 98312 | tf_op jit(solution)/shard_map/ppermute | solution.py:33
  35.2 0.5 %collective-permute-done.13 = f32[64,128]{1,0:T(8,128)S(1)} collective-permute-done((f32[64,128]{1,0:T(8,128)S(1)}, f32[64,128]{1,0:T(8,128)S(1)}, u32[]{:S(2)}, u32[]{:S(2)}) %collective-permute-start.13) | collective-permute-done | bytes 32800 | tf_op jit(solution)/shard_map/ppermute | solution.py:33
  35.6 0.1 collective-permute-done.14
  35.7 2.1 %collective-permute-done.12 = f32[64,128]{1,0:T(8,128)S(1)} collective-permute-done((f32[64,128]{1,0:T(8,128)S(1)}, f32[64,128]{1,0:T(8,128)S(1)}, u32[]{:S(2)}, u32[]{:S(2)}) %collective-permute-start.12) | collective-permute-done | bytes 32800 | tf_op jit(solution)/shard_map/ppermute | solution.py:33
  37.8 2.6 %finish.1 = (f32[64,512]{1,0:T(8,128)}, f32[64,64]{1,0:T(8,128)}) custom-call(f32[64,128]{1,0:T(8,128)S(1)} %add_add_fusion.refs_0_, bf16[192,512]{1,0:T(8,128)(2,1)S(1)} %get-tuple-element.27.refs_1_), custom_call_target="tpu_custom_call" | custom-call | tf_op jit(solution)/shard_map/finish/pallas_call | solution.py:348
  (5 shorter events, 0.1 us)
Async XLA Ops:
  1.5 7.6 %collective-permute-start = (bf16[64,512]{1,0:T(8,128)(2,1)S(1)}, bf16[64,512]{1,0:T(8,128)(2,1)S(1)}, u32[]{:S(2)}, u32[]{:S(2)}) collective-permute-start(bf16[64,512]{1,0:T(8,128)(2,1)S(1)} %get-tuple-element.15), channel_id=1, source_target_pairs={{0,16},{1,17},{2,18},{3,19},{4,20},{5,21},{6,22},{7,23},{8,24},{9,... | collective-permute-start | bytes 196616 | tf_op jit(solution)/shard_map/ppermute | solution.py:33
  5.6 6.6 %collective-permute-start.2 = (bf16[64,512]{1,0:T(8,128)(2,1)S(1)}, bf16[64,512]{1,0:T(8,128)(2,1)S(1)}, u32[]{:S(2)}, u32[]{:S(2)}) collective-permute-start(bf16[64,512]{1,0:T(8,128)(2,1)S(1)} %get-tuple-element.15), channel_id=1, source_target_pairs={{0,8},{1,9},{2,10},{3,11},{4,12},{5,13},{6,14},{7,15},{8,0},{9,1},... | collective-permute-start | bytes 196616 | tf_op jit(solution)/shard_map/ppermute | solution.py:33
  7.2 5.8 %collective-permute-start.1 = (bf16[64,512]{1,0:T(8,128)(2,1)S(1)}, bf16[64,512]{1,0:T(8,128)(2,1)S(1)}, u32[]{:S(2)}, u32[]{:S(2)}) collective-permute-start(bf16[64,512]{1,0:T(8,128)(2,1)S(1)} %get-tuple-element.15), channel_id=1, source_target_pairs={{0,4},{1,5},{2,6},{3,7},{4,0},{5,1},{6,2},{7,3},{8,12},{9,13},{10,... | collective-permute-start | bytes 196616 | tf_op jit(solution)/shard_map/ppermute | solution.py:33
  8.7 6.1 %collective-permute-start.3 = (bf16[64,512]{1,0:T(8,128)(2,1)S(1)}, bf16[64,512]{1,0:T(8,128)(2,1)S(1)}, u32[]{:S(2)}, u32[]{:S(2)}) collective-permute-start(bf16[64,512]{1,0:T(8,128)(2,1)S(1)} %get-tuple-element.15), channel_id=1, source_target_pairs={{0,12},{1,13},{2,14},{3,15},{4,8},{5,9},{6,10},{7,11},{8,4},{9,5},... | collective-permute-start | bytes 196616 | tf_op jit(solution)/shard_map/ppermute | solution.py:33
  9.1 5.7 %collective-permute-start.4 = (bf16[64,512]{1,0:T(8,128)(2,1)S(1)}, bf16[64,512]{1,0:T(8,128)(2,1)S(1)}, u32[]{:S(2)}, u32[]{:S(2)}) collective-permute-start(bf16[64,512]{1,0:T(8,128)(2,1)S(1)} %collective-permute-done), channel_id=1, source_target_pairs={{0,4},{1,5},{2,6},{3,7},{4,0},{5,1},{6,2},{7,3},{8,12},{9,13},{10,... | collective-permute-start | bytes 196616 | tf_op jit(solution)/shard_map/ppermute | solution.py:33
  10.6 4.3 %collective-permute-start.5 = (bf16[64,512]{1,0:T(8,128)(2,1)S(1)}, bf16[64,512]{1,0:T(8,128)(2,1)S(1)}, u32[]{:S(2)}, u32[]{:S(2)}) collective-permute-start(bf16[64,512]{1,0:T(8,128)(2,1)S(1)} %collective-permute-done), channel_id=1, source_target_pairs={{0,8},{1,9},{2,10},{3,11},{4,12},{5,13},{6,14},{7,15},{8,0},{9,1},... | collective-permute-start | bytes 196616 | tf_op jit(solution)/shard_map/ppermute | solution.py:33
  12.2 5.2 %collective-permute-start.6 = (bf16[64,512]{1,0:T(8,128)(2,1)S(1)}, bf16[64,512]{1,0:T(8,128)(2,1)S(1)}, u32[]{:S(2)}, u32[]{:S(2)}) collective-permute-start(bf16[64,512]{1,0:T(8,128)(2,1)S(1)} %collective-permute-done), channel_id=1, source_target_pairs={{0,12},{1,13},{2,14},{3,15},{4,8},{5,9},{6,10},{7,11},{8,4},{9,5},... | collective-permute-start | bytes 196616 | tf_op jit(solution)/shard_map/ppermute | solution.py:33
  13.0 5.2 %collective-permute-start.7 = (bf16[80,512]{1,0:T(8,128)(2,1)S(1)}, bf16[80,512]{1,0:T(8,128)(2,1)S(1)}, u32[]{:S(2)}, u32[]{:S(2)}) collective-permute-start(bf16[80,512]{1,0:T(8,128)(2,1)S(1)} %get-tuple-element.17.refs_0_), channel_id=1, source_target_pairs={{0,3},{1,2},{2,1},{3,0},{4,7},{5,6},{6,5},{7,4},{8,11},{9,10},{10,... | collective-permute-start | bytes 245768 | tf_op jit(solution)/shard_map/ppermute | solution.py:33
  18.2 1.4 %collective-permute-start.8 = (bf16[2,64,512]{2,1,0:T(8,128)(2,1)S(1)}, bf16[2,64,512]{2,1,0:T(8,128)(2,1)S(1)}, u32[]{:S(2)}, u32[]{:S(2)}) collective-permute-start(bf16[2,64,512]{2,1,0:T(8,128)(2,1)S(1)} %get-tuple-element.25), channel_id=1, source_target_pairs={{0,1},{1,0},{2,3},{3,2},{4,5},{5,4},{6,7},{7,6},{8,9},{9,8},{10,11... | collective-permute-start | bytes 393224 | tf_op jit(solution)/shard_map/ppermute | solution.py:33
  19.7 5.5 %collective-permute-start.9 = (bf16[2,64,512]{2,1,0:T(8,128)(2,1)S(1)}, bf16[2,64,512]{2,1,0:T(8,128)(2,1)S(1)}, u32[]{:S(2)}, u32[]{:S(2)}) collective-permute-start(bf16[2,64,512]{2,1,0:T(8,128)(2,1)S(1)} %add_convert_fusion.refs_2_), channel_id=1, source_target_pairs={{0,3},{1,2},{2,1},{3,0},{4,7},{5,6},{6,5},{7,4},{8,11},{9,10},{10,... | collective-permute-start | bytes 393224 | tf_op jit(solution)/shard_map/ppermute | solution.py:33
  25.7 1.3 %collective-permute-start.10 = (f32[64,128]{1,0:T(8,128)S(1)}, f32[64,128]{1,0:T(8,128)S(1)}, u32[]{:S(2)}, u32[]{:S(2)}) collective-permute-start(f32[64,128]{1,0:T(8,128)S(1)} %get-tuple-element.26), channel_id=1, source_target_pairs={{0,1},{1,0},{2,3},{3,2},{4,5},{5,4},{6,7},{7,6},{8,9},{9,8},{10,11... | collective-permute-start | bytes 98312 | tf_op jit(solution)/shard_map/ppermute | solution.py:33
  27.0 5.2 %collective-permute-start.11 = (f32[64,128]{1,0:T(8,128)S(1)}, f32[64,128]{1,0:T(8,128)S(1)}, u32[]{:S(2)}, u32[]{:S(2)}) collective-permute-start(f32[64,128]{1,0:T(8,128)S(1)} %add.19), channel_id=1, source_target_pairs={{0,17},{1,16},{2,19},{3,18},{4,21},{5,20},{6,23},{7,22},{8,25},{9,... | collective-permute-start | bytes 98312 | tf_op jit(solution)/shard_map/ppermute | solution.py:33
  32.2 3.4 %collective-permute-start.13 = (f32[64,128]{1,0:T(8,128)S(1)}, f32[64,128]{1,0:T(8,128)S(1)}, u32[]{:S(2)}, u32[]{:S(2)}) collective-permute-start(f32[64,128]{1,0:T(8,128)S(1)} %add.20), channel_id=1, source_target_pairs={{0,5},{1,4},{2,7},{3,6},{4,1},{5,0},{6,3},{7,2},{8,13},{9,12},{10,... | collective-permute-start | bytes 98312 | tf_op jit(solution)/shard_map/ppermute | solution.py:33
  32.2 3.5 %collective-permute-start.14 = (f32[64,128]{1,0:T(8,128)S(1)}, f32[64,128]{1,0:T(8,128)S(1)}, u32[]{:S(2)}, u32[]{:S(2)}) collective-permute-start(f32[64,128]{1,0:T(8,128)S(1)} %add.20), channel_id=1, source_target_pairs={{0,9},{1,8},{2,11},{3,10},{4,13},{5,12},{6,15},{7,14},{8,1},{9,0},... | collective-permute-start | bytes 98312 | tf_op jit(solution)/shard_map/ppermute | solution.py:33
  33.2 4.6 %collective-permute-start.12 = (f32[64,128]{1,0:T(8,128)S(1)}, f32[64,128]{1,0:T(8,128)S(1)}, u32[]{:S(2)}, u32[]{:S(2)}) collective-permute-start(f32[64,128]{1,0:T(8,128)S(1)} %add.20), channel_id=1, source_target_pairs={{0,13},{1,12},{2,15},{3,14},{4,9},{5,8},{6,11},{7,10},{8,5},{9,4},... | collective-permute-start | bytes 98312 | tf_op jit(solution)/shard_map/ppermute | solution.py:33

commit v8 on v7

--- a/solution.py
+++ b/solution.py
@@ -261,7 +261,7 @@
     base = [at for at, _ in blocks]
     named = dict(blocks)
     direct = [mask for mask in (low[0], low[1], diag)]
-    relayed = [(mask, at) for at in base[1:] for mask in (low[0], low[1], diag) if (mask ^ at) not in direct]
+    relayed = [(mask, at) for at in base[1:] for mask in (diag, low[1], low[0]) if (mask ^ at) not in direct]
     pieces = [(mask, swap(scaled, mask, 0)) for mask in direct]
     early = blocks + pieces[:2]
     late = pieces[2:] + [(mask ^ at, swap(named[at], mask, 0)) for mask, at in relayed]

time: 40.6 us -> 40.2 us (level)
  starting transfers between devices: 18.3 us -> 17.4 us
  waiting for transfers between devices: 13.9 us -> 14.5 us
    ppermute x15, starting transfers between devices: 18.3 us -> 17.4 us  [swap(): return lax.ppermute(value, ('row', 'col'), pairs)]
    ppermute x15, waiting for transfers between devices: 13.9 us -> 14.5 us  [swap(): return lax.ppermute(value, ('row', 'col'), pairs)]
  transfers between devices with their start and end apart: 15 -> 15, of which waited for: 8 -> 12; matrix products, arithmetic and copies ran while one was open for 0% -> 0% of each run, Pallas kernels for 6% -> 6%
where the time goes in v8:
time: 40.2 us; the launch traced here: 40 us
  starting transfers between devices  17.4 us (43%)
  waiting for transfers between devices  14.5 us (36%)
  Pallas kernels  7.31 us (18%)
  between operations  0.7 us (2%)
    ppermute x15, starting transfers between devices, swap(): return lax.ppermute(value, ('row', 'col'), pairs)  17.4 us
    ppermute x15, waiting for transfers between devices, swap(): return lax.ppermute(value, ('row', 'col'), pairs)  14.5 us
    pallas_call x1, Pallas kernels, on_device(): pl.pallas_call(lambda *refs: finish_kernel(total_rows, *refs), out_shape=...  2.64 us
    pallas_call x1, Pallas kernels, on_device(): pl.pallas_call(lambda *refs: load_kernel(per_piece, sources * per_piece,...  1.72 us
    pallas_call x1, Pallas kernels, on_device(): pl.pallas_call(lambda *refs: send_kernel(groups, per_piece, late, *refs),...  0.88 us
    pallas_call x1, Pallas kernels, on_device(): pl.pallas_call(scale_kernel, out_shape=[jax.ShapeDtypeStruct((vectors, ow...  0.86 us
  transfers between devices with their start and end apart: 15, of which 12 were waited for; matrix products, arithmetic and copies ran while one was open for 0% of the time, Pallas kernels for 6%

profile of v8, /device:TPU:0, one launch (start us, length us, event | category | flops | bytes accessed | tf_op | source)
XLA Modules:
  0.0 40.0 jit_solution(6941046774311763878)
XLA Ops:
  0.6 0.9 %scale.1 = (bf16[64,512]{1,0:T(8,128)(2,1)S(1)}, bf16[80,512]{1,0:T(8,128)(2,1)S(1)}) custom-call(bf16[64,512]{1,0:T(8,128)(2,1)} %basis_ref.1, s32[1,512]{1,0:T(1,128)} %bitcast.27), custom_call_target="tpu_custom_call" | custom-call | tf_op jit(solution)/shard_map/scale/pallas_call | solution.py:240
  1.5 4.1 %collective-permute-start = (bf16[64,512]{1,0:T(8,128)(2,1)S(1)}, bf16[64,512]{1,0:T(8,128)(2,1)S(1)}, u32[]{:S(2)}, u32[]{:S(2)}) collective-permute-start(bf16[64,512]{1,0:T(8,128)(2,1)S(1)} %get-tuple-element.15), channel_id=1, source_target_pairs={{0,16},{1,17},{2,18},{3,19},{4,20},{5,21},{6,22},{7,23},{8,24},{9,... | collective-permute-start | bytes 196616 | tf_op jit(solution)/shard_map/ppermute | solution.py:33
  5.6 1.6 %collective-permute-start.2 = (bf16[64,512]{1,0:T(8,128)(2,1)S(1)}, bf16[64,512]{1,0:T(8,128)(2,1)S(1)}, u32[]{:S(2)}, u32[]{:S(2)}) collective-permute-start(bf16[64,512]{1,0:T(8,128)(2,1)S(1)} %get-tuple-element.15), channel_id=1, source_target_pairs={{0,8},{1,9},{2,10},{3,11},{4,12},{5,13},{6,14},{7,15},{8,0},{9,1},... | collective-permute-start | bytes 196616 | tf_op jit(solution)/shard_map/ppermute | solution.py:33
  7.2 1.5 %collective-permute-start.1 = (bf16[64,512]{1,0:T(8,128)(2,1)S(1)}, bf16[64,512]{1,0:T(8,128)(2,1)S(1)}, u32[]{:S(2)}, u32[]{:S(2)}) collective-permute-start(bf16[64,512]{1,0:T(8,128)(2,1)S(1)} %get-tuple-element.15), channel_id=1, source_target_pairs={{0,4},{1,5},{2,6},{3,7},{4,0},{5,1},{6,2},{7,3},{8,12},{9,13},{10,... | collective-permute-start | bytes 196616 | tf_op jit(solution)/shard_map/ppermute | solution.py:33
  8.7 0.4 %collective-permute-start.3 = (bf16[64,512]{1,0:T(8,128)(2,1)S(1)}, bf16[64,512]{1,0:T(8,128)(2,1)S(1)}, u32[]{:S(2)}, u32[]{:S(2)}) collective-permute-start(bf16[64,512]{1,0:T(8,128)(2,1)S(1)} %get-tuple-element.15), channel_id=1, source_target_pairs={{0,12},{1,13},{2,14},{3,15},{4,8},{5,9},{6,10},{7,11},{8,4},{9,5},... | collective-permute-start | bytes 196616 | tf_op jit(solution)/shard_map/ppermute | solution.py:33
  9.1 0.0 collective-permute-done
  9.1 2.5 %collective-permute-start.4 = (bf16[64,512]{1,0:T(8,128)(2,1)S(1)}, bf16[64,512]{1,0:T(8,128)(2,1)S(1)}, u32[]{:S(2)}, u32[]{:S(2)}) collective-permute-start(bf16[64,512]{1,0:T(8,128)(2,1)S(1)} %collective-permute-done), channel_id=1, source_target_pairs={{0,12},{1,13},{2,14},{3,15},{4,8},{5,9},{6,10},{7,11},{8,4},{9,5},... | collective-permute-start | bytes 196616 | tf_op jit(solution)/shard_map/ppermute | solution.py:33
  11.6 0.4 %collective-permute-start.5 = (bf16[64,512]{1,0:T(8,128)(2,1)S(1)}, bf16[64,512]{1,0:T(8,128)(2,1)S(1)}, u32[]{:S(2)}, u32[]{:S(2)}) collective-permute-start(bf16[64,512]{1,0:T(8,128)(2,1)S(1)} %collective-permute-done), channel_id=1, source_target_pairs={{0,8},{1,9},{2,10},{3,11},{4,12},{5,13},{6,14},{7,15},{8,0},{9,1},... | collective-permute-start | bytes 196616 | tf_op jit(solution)/shard_map/ppermute | solution.py:33
  12.0 0.0 collective-permute-done.2
  12.0 0.5 %collective-permute-start.6 = (bf16[64,512]{1,0:T(8,128)(2,1)S(1)}, bf16[64,512]{1,0:T(8,128)(2,1)S(1)}, u32[]{:S(2)}, u32[]{:S(2)}) collective-permute-start(bf16[64,512]{1,0:T(8,128)(2,1)S(1)} %collective-permute-done), channel_id=1, source_target_pairs={{0,4},{1,5},{2,6},{3,7},{4,0},{5,1},{6,2},{7,3},{8,12},{9,13},{10,... | collective-permute-start | bytes 196616 | tf_op jit(solution)/shard_map/ppermute | solution.py:33
  12.6 0.3 collective-permute-done.1
  12.8 0.0 collective-permute-start.7
  12.9 1.7 %load.1 = (s32[8,32]{1,0:T(8,128)S(4)}, bf16[32,64,512]{2,1,0:T(8,128)(2,1)S(1)}, bf16[65,64,128]{2,1,0:T(8,128)(2,1)S(1)}) custom-call(s32[8,32]{1,0:T(8,128)} %bitcast.25, s32[8,32]{1,0:T(8,128)} %bitcast.26, bf16[32,64,512]{2,1,0:T(8,128)(2,1)} %bitcast.21, bf16[4,64,512]{2,1,0:T(8,128)(2,1)S(1)} %pad_maximum_fusion.refs_3_), custom_call_target="tpu_custom_call" | custom-call | tf_op jit(solution)/shard_map/load/pallas_call | solution.py:276
  14.6 0.0 collective-permute-done.3
  14.6 0.2 collective-permute-done.4
  14.8 1.0 %collective-permute-done.5 = bf16[64,512]{1,0:T(8,128)(2,1)S(1)} collective-permute-done((bf16[64,512]{1,0:T(8,128)(2,1)S(1)}, bf16[64,512]{1,0:T(8,128)(2,1)S(1)}, u32[]{:S(2)}, u32[]{:S(2)}) %collective-permute-start.5) | collective-permute-done | bytes 65568 | tf_op jit(solution)/shard_map/ppermute | solution.py:33
  15.9 0.5 %collective-permute-done.6 = bf16[64,512]{1,0:T(8,128)(2,1)S(1)} collective-permute-done((bf16[64,512]{1,0:T(8,128)(2,1)S(1)}, bf16[64,512]{1,0:T(8,128)(2,1)S(1)}, u32[]{:S(2)}, u32[]{:S(2)}) %collective-permute-start.6) | collective-permute-done | bytes 65568 | tf_op jit(solution)/shard_map/ppermute | solution.py:33
  16.3 0.9 %send.1 = (bf16[65,64,128]{2,1,0:T(8,128)(2,1)S(1)}, bf16[2,64,512]{2,1,0:T(8,128)(2,1)S(1)}) custom-call(s32[8,32]{1,0:T(8,128)S(4)} %get-tuple-element.19.refs_0_, bf16[32,64,512]{2,1,0:T(8,128)(2,1)S(1)} %get-tuple-element.20.refs_1_, bf16[65,64,128]{2,1,0:T(8,128)(2,1)S(1)} %get-tuple-element.21.refs_2_, ...), custom_call_target="tpu_custom_call", output_to_operand_aliasing={{0}: (2, {})} | custom-call | tf_op jit(solution)/shard_map/send/pallas_call | solution.py:296
  17.2 0.3 collective-permute-done.7.refs_1_
  17.5 0.1 collective-permute-start.8
  17.6 0.7 %keep.1 = f32[2,64,512]{2,1,0:T(8,128)S(1)} custom-call(s32[8,32]{1,0:T(8,128)S(4)} %get-tuple-element.19.refs_0_, bf16[32,64,512]{2,1,0:T(8,128)(2,1)S(1)} %get-tuple-element.20.refs_1_, bf16[65,64,128]{2,1,0:T(8,128)(2,1)S(1)} %get-tuple-element.24.refs_2_), custom_call_target="tpu_custom_call" | custom-call | tf_op jit(solution)/shard_map/keep/pallas_call | solution.py:310
  18.4 0.5 %collective-permute-done.8 = bf16[2,64,512]{2,1,0:T(8,128)(2,1)S(1)} collective-permute-done((bf16[2,64,512]{2,1,0:T(8,128)(2,1)S(1)}, bf16[2,64,512]{2,1,0:T(8,128)(2,1)S(1)}, u32[]{:S(2)}, u32[]{:S(2)}) %collective-permute-start.8) | collective-permute-done | bytes 131104 | tf_op jit(solution)/shard_map/ppermute | solution.py:33
  18.9 1.1 %collective-permute-start.9 = (bf16[2,64,512]{2,1,0:T(8,128)(2,1)S(1)}, bf16[2,64,512]{2,1,0:T(8,128)(2,1)S(1)}, u32[]{:S(2)}, u32[]{:S(2)}) collective-permute-start(bf16[2,64,512]{2,1,0:T(8,128)(2,1)S(1)} %add_convert_fusion.refs_2_), channel_id=1, source_target_pairs={{0,3},{1,2},{2,1},{3,0},{4,7},{5,6},{6,5},{7,4},{8,11},{9,10},{10,... | collective-permute-start | bytes 393224 | tf_op jit(solution)/shard_map/ppermute | solution.py:33
  20.0 4.4 %collective-permute-done.9.refs_3_ = bf16[2,64,512]{2,1,0:T(8,128)(2,1)S(1)} collective-permute-done((bf16[2,64,512]{2,1,0:T(8,128)(2,1)S(1)}, bf16[2,64,512]{2,1,0:T(8,128)(2,1)S(1)}, u32[]{:S(2)}, u32[]{:S(2)}) %collective-permute-start.9) | collective-permute-done | bytes 131104 | tf_op jit(solution)/shard_map/ppermute | solution.py:33
  24.4 0.5 %gram.1 = (bf16[192,512]{1,0:T(8,128)(2,1)S(1)}, f32[64,128]{1,0:T(8,128)S(1)}) custom-call(bf16[80,512]{1,0:T(8,128)(2,1)S(1)} %get-tuple-element.17.refs_0_, bf16[80,512]{1,0:T(8,128)(2,1)S(1)} %collective-permute-done.7.refs_1_, bf16[2,64,512]{2,1,0:T(8,128)(2,1)S(1)} %add_convert_fusion.refs_2_, bf16[2,64,512]{2,1,0:T(8,128)(2,1)S(1)} %collective-permute-done.9.refs_3_), custom_call_target="tpu_custom_call" | custom-call | tf_op jit(solution)/shard_map/gram/pallas_call | solution.py:328
  24.9 0.2 collective-permute-start.10
  25.1 1.1 %collective-permute-done.10 = f32[64,128]{1,0:T(8,128)S(1)} collective-permute-done((f32[64,128]{1,0:T(8,128)S(1)}, f32[64,128]{1,0:T(8,128)S(1)}, u32[]{:S(2)}, u32[]{:S(2)}) %collective-permute-start.10) | collective-permute-done | bytes 32800 | tf_op jit(solution)/shard_map/ppermute | solution.py:33
  26.2 1.7 %collective-permute-start.11 = (f32[64,128]{1,0:T(8,128)S(1)}, f32[64,128]{1,0:T(8,128)S(1)}, u32[]{:S(2)}, u32[]{:S(2)}) collective-permute-start(f32[64,128]{1,0:T(8,128)S(1)} %add.19), channel_id=1, source_target_pairs={{0,17},{1,16},{2,19},{3,18},{4,21},{5,20},{6,23},{7,22},{8,25},{9,... | collective-permute-start | bytes 98312 | tf_op jit(solution)/shard_map/ppermute | solution.py:33
  27.9 2.5 %collective-permute-done.11 = f32[64,128]{1,0:T(8,128)S(1)} collective-permute-done((f32[64,128]{1,0:T(8,128)S(1)}, f32[64,128]{1,0:T(8,128)S(1)}, u32[]{:S(2)}, u32[]{:S(2)}) %collective-permute-start.11) | collective-permute-done | bytes 32800 | tf_op jit(solution)/shard_map/ppermute | solution.py:33
  30.5 2.4 %collective-permute-start.13 = (f32[64,128]{1,0:T(8,128)S(1)}, f32[64,128]{1,0:T(8,128)S(1)}, u32[]{:S(2)}, u32[]{:S(2)}) collective-permute-start(f32[64,128]{1,0:T(8,128)S(1)} %add.20), channel_id=1, source_target_pairs={{0,5},{1,4},{2,7},{3,6},{4,1},{5,0},{6,3},{7,2},{8,13},{9,12},{10,... | collective-permute-start | bytes 98312 | tf_op jit(solution)/shard_map/ppermute | solution.py:33
  32.8 0.3 collective-permute-start.14
  33.1 0.5 %collective-permute-start.12 = (f32[64,128]{1,0:T(8,128)S(1)}, f32[64,128]{1,0:T(8,128)S(1)}, u32[]{:S(2)}, u32[]{:S(2)}) collective-permute-start(f32[64,128]{1,0:T(8,128)S(1)} %add.20), channel_id=1, source_target_pairs={{0,13},{1,12},{2,15},{3,14},{4,9},{5,8},{6,11},{7,10},{8,5},{9,4},... | collective-permute-start | bytes 98312 | tf_op jit(solution)/shard_map/ppermute | solution.py:33
  33.6 1.0 %collective-permute-done.13 = f32[64,128]{1,0:T(8,128)S(1)} collective-permute-done((f32[64,128]{1,0:T(8,128)S(1)}, f32[64,128]{1,0:T(8,128)S(1)}, u32[]{:S(2)}, u32[]{:S(2)}) %collective-permute-start.13) | collective-permute-done | bytes 32800 | tf_op jit(solution)/shard_map/ppermute | solution.py:33
  34.6 1.8 %collective-permute-done.14 = f32[64,128]{1,0:T(8,128)S(1)} collective-permute-done((f32[64,128]{1,0:T(8,128)S(1)}, f32[64,128]{1,0:T(8,128)S(1)}, u32[]{:S(2)}, u32[]{:S(2)}) %collective-permute-start.14) | collective-permute-done | bytes 32800 | tf_op jit(solution)/shard_map/ppermute | solution.py:33
  36.4 1.0 %collective-permute-done.12 = f32[64,128]{1,0:T(8,128)S(1)} collective-permute-done((f32[64,128]{1,0:T(8,128)S(1)}, f32[64,128]{1,0:T(8,128)S(1)}, u32[]{:S(2)}, u32[]{:S(2)}) %collective-permute-start.12) | collective-permute-done | bytes 32800 | tf_op jit(solution)/shard_map/ppermute | solution.py:33
  37.3 2.6 %finish.1 = (f32[64,512]{1,0:T(8,128)}, f32[64,64]{1,0:T(8,128)}) custom-call(f32[64,128]{1,0:T(8,128)S(1)} %add_add_fusion.refs_0_, bf16[192,512]{1,0:T(8,128)(2,1)S(1)} %get-tuple-element.27.refs_1_), custom_call_target="tpu_custom_call" | custom-call | tf_op jit(solution)/shard_map/finish/pallas_call | solution.py:348
  (5 shorter events, 0.1 us)
Async XLA Ops:
  1.5 7.6 %collective-permute-start = (bf16[64,512]{1,0:T(8,128)(2,1)S(1)}, bf16[64,512]{1,0:T(8,128)(2,1)S(1)}, u32[]{:S(2)}, u32[]{:S(2)}) collective-permute-start(bf16[64,512]{1,0:T(8,128)(2,1)S(1)} %get-tuple-element.15), channel_id=1, source_target_pairs={{0,16},{1,17},{2,18},{3,19},{4,20},{5,21},{6,22},{7,23},{8,24},{9,... | collective-permute-start | bytes 196616 | tf_op jit(solution)/shard_map/ppermute | solution.py:33
  5.6 6.5 %collective-permute-start.2 = (bf16[64,512]{1,0:T(8,128)(2,1)S(1)}, bf16[64,512]{1,0:T(8,128)(2,1)S(1)}, u32[]{:S(2)}, u32[]{:S(2)}) collective-permute-start(bf16[64,512]{1,0:T(8,128)(2,1)S(1)} %get-tuple-element.15), channel_id=1, source_target_pairs={{0,8},{1,9},{2,10},{3,11},{4,12},{5,13},{6,14},{7,15},{8,0},{9,1},... | collective-permute-start | bytes 196616 | tf_op jit(solution)/shard_map/ppermute | solution.py:33
  7.2 5.7 %collective-permute-start.1 = (bf16[64,512]{1,0:T(8,128)(2,1)S(1)}, bf16[64,512]{1,0:T(8,128)(2,1)S(1)}, u32[]{:S(2)}, u32[]{:S(2)}) collective-permute-start(bf16[64,512]{1,0:T(8,128)(2,1)S(1)} %get-tuple-element.15), channel_id=1, source_target_pairs={{0,4},{1,5},{2,6},{3,7},{4,0},{5,1},{6,2},{7,3},{8,12},{9,13},{10,... | collective-permute-start | bytes 196616 | tf_op jit(solution)/shard_map/ppermute | solution.py:33
  8.7 6.0 %collective-permute-start.3 = (bf16[64,512]{1,0:T(8,128)(2,1)S(1)}, bf16[64,512]{1,0:T(8,128)(2,1)S(1)}, u32[]{:S(2)}, u32[]{:S(2)}) collective-permute-start(bf16[64,512]{1,0:T(8,128)(2,1)S(1)} %get-tuple-element.15), channel_id=1, source_target_pairs={{0,12},{1,13},{2,14},{3,15},{4,8},{5,9},{6,10},{7,11},{8,4},{9,5},... | collective-permute-start | bytes 196616 | tf_op jit(solution)/shard_map/ppermute | solution.py:33
  9.1 5.7 %collective-permute-start.4 = (bf16[64,512]{1,0:T(8,128)(2,1)S(1)}, bf16[64,512]{1,0:T(8,128)(2,1)S(1)}, u32[]{:S(2)}, u32[]{:S(2)}) collective-permute-start(bf16[64,512]{1,0:T(8,128)(2,1)S(1)} %collective-permute-done), channel_id=1, source_target_pairs={{0,12},{1,13},{2,14},{3,15},{4,8},{5,9},{6,10},{7,11},{8,4},{9,5},... | collective-permute-start | bytes 196616 | tf_op jit(solution)/shard_map/ppermute | solution.py:33
  11.6 4.3 %collective-permute-start.5 = (bf16[64,512]{1,0:T(8,128)(2,1)S(1)}, bf16[64,512]{1,0:T(8,128)(2,1)S(1)}, u32[]{:S(2)}, u32[]{:S(2)}) collective-permute-start(bf16[64,512]{1,0:T(8,128)(2,1)S(1)} %collective-permute-done), channel_id=1, source_target_pairs={{0,8},{1,9},{2,10},{3,11},{4,12},{5,13},{6,14},{7,15},{8,0},{9,1},... | collective-permute-start | bytes 196616 | tf_op jit(solution)/shard_map/ppermute | solution.py:33
  12.0 4.3 %collective-permute-start.6 = (bf16[64,512]{1,0:T(8,128)(2,1)S(1)}, bf16[64,512]{1,0:T(8,128)(2,1)S(1)}, u32[]{:S(2)}, u32[]{:S(2)}) collective-permute-start(bf16[64,512]{1,0:T(8,128)(2,1)S(1)} %collective-permute-done), channel_id=1, source_target_pairs={{0,4},{1,5},{2,6},{3,7},{4,0},{5,1},{6,2},{7,3},{8,12},{9,13},{10,... | collective-permute-start | bytes 196616 | tf_op jit(solution)/shard_map/ppermute | solution.py:33
  12.8 4.7 %collective-permute-start.7 = (bf16[80,512]{1,0:T(8,128)(2,1)S(1)}, bf16[80,512]{1,0:T(8,128)(2,1)S(1)}, u32[]{:S(2)}, u32[]{:S(2)}) collective-permute-start(bf16[80,512]{1,0:T(8,128)(2,1)S(1)} %get-tuple-element.17.refs_0_), channel_id=1, source_target_pairs={{0,3},{1,2},{2,1},{3,0},{4,7},{5,6},{6,5},{7,4},{8,11},{9,10},{10,... | collective-permute-start | bytes 245768 | tf_op jit(solution)/shard_map/ppermute | solution.py:33
  17.5 1.3 %collective-permute-start.8 = (bf16[2,64,512]{2,1,0:T(8,128)(2,1)S(1)}, bf16[2,64,512]{2,1,0:T(8,128)(2,1)S(1)}, u32[]{:S(2)}, u32[]{:S(2)}) collective-permute-start(bf16[2,64,512]{2,1,0:T(8,128)(2,1)S(1)} %get-tuple-element.25), channel_id=1, source_target_pairs={{0,1},{1,0},{2,3},{3,2},{4,5},{5,4},{6,7},{7,6},{8,9},{9,8},{10,11... | collective-permute-start | bytes 393224 | tf_op jit(solution)/shard_map/ppermute | solution.py:33
  18.9 5.5 %collective-permute-start.9 = (bf16[2,64,512]{2,1,0:T(8,128)(2,1)S(1)}, bf16[2,64,512]{2,1,0:T(8,128)(2,1)S(1)}, u32[]{:S(2)}, u32[]{:S(2)}) collective-permute-start(bf16[2,64,512]{2,1,0:T(8,128)(2,1)S(1)} %add_convert_fusion.refs_2_), channel_id=1, source_target_pairs={{0,3},{1,2},{2,1},{3,0},{4,7},{5,6},{6,5},{7,4},{8,11},{9,10},{10,... | collective-permute-start | bytes 393224 | tf_op jit(solution)/shard_map/ppermute | solution.py:33
  24.9 1.3 %collective-permute-start.10 = (f32[64,128]{1,0:T(8,128)S(1)}, f32[64,128]{1,0:T(8,128)S(1)}, u32[]{:S(2)}, u32[]{:S(2)}) collective-permute-start(f32[64,128]{1,0:T(8,128)S(1)} %get-tuple-element.26), channel_id=1, source_target_pairs={{0,1},{1,0},{2,3},{3,2},{4,5},{5,4},{6,7},{7,6},{8,9},{9,8},{10,11... | collective-permute-start | bytes 98312 | tf_op jit(solution)/shard_map/ppermute | solution.py:33
  26.2 4.2 %collective-permute-start.11 = (f32[64,128]{1,0:T(8,128)S(1)}, f32[64,128]{1,0:T(8,128)S(1)}, u32[]{:S(2)}, u32[]{:S(2)}) collective-permute-start(f32[64,128]{1,0:T(8,128)S(1)} %add.19), channel_id=1, source_target_pairs={{0,17},{1,16},{2,19},{3,18},{4,21},{5,20},{6,23},{7,22},{8,25},{9,... | collective-permute-start | bytes 98312 | tf_op jit(solution)/shard_map/ppermute | solution.py:33
  30.5 4.1 %collective-permute-start.13 = (f32[64,128]{1,0:T(8,128)S(1)}, f32[64,128]{1,0:T(8,128)S(1)}, u32[]{:S(2)}, u32[]{:S(2)}) collective-permute-start(f32[64,128]{1,0:T(8,128)S(1)} %add.20), channel_id=1, source_target_pairs={{0,5},{1,4},{2,7},{3,6},{4,1},{5,0},{6,3},{7,2},{8,13},{9,12},{10,... | collective-permute-start | bytes 98312 | tf_op jit(solution)/shard_map/ppermute | solution.py:33
  32.8 3.5 %collective-permute-start.14 = (f32[64,128]{1,0:T(8,128)S(1)}, f32[64,128]{1,0:T(8,128)S(1)}, u32[]{:S(2)}, u32[]{:S(2)}) collective-permute-start(f32[64,128]{1,0:T(8,128)S(1)} %add.20), channel_id=1, source_target_pairs={{0,9},{1,8},{2,11},{3,10},{4,13},{5,12},{6,15},{7,14},{8,1},{9,0},... | collective-permute-start | bytes 98312 | tf_op jit(solution)/shard_map/ppermute | solution.py:33
  33.1 4.2 %collective-permute-start.12 = (f32[64,128]{1,0:T(8,128)S(1)}, f32[64,128]{1,0:T(8,128)S(1)}, u32[]{:S(2)}, u32[]{:S(2)}) collective-permute-start(f32[64,128]{1,0:T(8,128)S(1)} %add.20), channel_id=1, source_target_pairs={{0,13},{1,12},{2,15},{3,14},{4,9},{5,8},{6,11},{7,10},{8,5},{9,4},... | collective-permute-start | bytes 98312 | tf_op jit(solution)/shard_map/ppermute | solution.py:33

commit v9 on v8

--- a/solution.py
+++ b/solution.py
@@ -92,7 +92,8 @@
     last.wait()
 
 
-def multiply(groups, per_piece, odd, index_ref, panel_ref, table_ref, lhs_ref, out_ref):
+def multiply(groups, per_piece, odd, base, index_ref, panel_ref, table_ref, lhs_ref, out_ref):
+    count = out_ref.shape[0]
     height = panel_ref.shape[1]
     slots = index_ref.shape[0]
     vectors = table_ref.shape[1]
@@ -105,8 +106,8 @@
     def chunk_of(step, chunk):
         flips = odd
         for bit in bits(groups)[:-1]:
-            flips = flips ^ ((step // bit) & 1)
-        row0 = ((2 * step + flips) ^ my_col) * per_piece + chunk * pack
+            flips = flips ^ (((base + step) // bit) & 1)
+        row0 = ((2 * (base + step) + flips) ^ my_col) * per_piece + chunk * pack
         slot_of = chunk % 2
         for inner in range(pack):
             row = row0 + inner
@@ -125,7 +126,7 @@
             out_ref[step, :, at:at + wide] = jnp.where(is_low, top, low).astype(out_ref.dtype)
 
     if groups <= 4:
-        for step in range(groups // 2):
+        for step in range(count):
             for chunk in range(per_piece // pack):
                 chunk_of(step, chunk)
     else:
@@ -134,18 +135,18 @@
                 chunk_of(step, chunk)
             return carry
 
-        lax.fori_loop(0, groups // 2, body, 0)
+        lax.fori_loop(0, count, body, 0)
 
 
 def send_kernel(groups, per_piece, orders, index_ref, panel_ref, table_in, *refs):
     table_ref, send_ref, lhs_ref = refs[len(orders):]
     for order, ref in zip(orders, refs):
         fill_table(table_ref, per_piece, panel_ref.shape[1], order, [ref.at[at] for at in range(len(order))])
-    multiply(groups, per_piece, 1, index_ref, panel_ref, table_ref, lhs_ref, send_ref)
-
-
-def keep_kernel(groups, per_piece, index_ref, panel_ref, table_ref, keep_ref, lhs_ref):
-    multiply(groups, per_piece, 0, index_ref, panel_ref, table_ref, lhs_ref, keep_ref)
+    multiply(groups, per_piece, 1, 0, index_ref, panel_ref, table_ref, lhs_ref, send_ref)
+
+
+def keep_kernel(groups, per_piece, odd, base, index_ref, panel_ref, table_ref, keep_ref, lhs_ref):
+    multiply(groups, per_piece, odd, base, index_ref, panel_ref, table_ref, lhs_ref, keep_ref)
 
 
 def gram_kernel(last, mine_ref, theirs_ref, sums_ref, got_ref, split_ref, gram_ref, stack_ref):
@@ -297,7 +298,7 @@
         lambda *refs: send_kernel(groups, per_piece, late, *refs),
         out_shape=[
             jax.ShapeDtypeStruct(table_shape, BF16),
-            jax.ShapeDtypeStruct((many, vectors, owned), BF16),
+            jax.ShapeDtypeStruct((many // 2, vectors, owned), BF16),
         ],
         in_specs=[smem()] + [vmem()] * (2 + len(far)),
         out_specs=[vmem(), vmem()],
@@ -307,8 +308,17 @@
         name="send",
     )(index, panel, table, *far)
     send, other_share = lax.optimization_barrier((send, other_share))
+    more = pl.pallas_call(
+        lambda *refs: keep_kernel(groups, per_piece, 1, many // 2, *refs),
+        out_shape=jax.ShapeDtypeStruct((many // 2, vectors, owned), BF16),
+        in_specs=[smem(), vmem(), vmem()],
+        out_specs=vmem(),
+        scratch_shapes=[lhs],
+        compiler_params=limit(8),
+        name="more",
+    )(index, panel, table)
     keep = pl.pallas_call(
-        lambda *refs: keep_kernel(groups, per_piece, *refs),
+        lambda *refs: keep_kernel(groups, per_piece, 0, 0, *refs),
         out_shape=jax.ShapeDtypeStruct((many, vectors, owned), F32),
         in_specs=[smem(), vmem(), vmem()],
         out_specs=vmem(),
@@ -319,7 +329,11 @@
     col_bits = bits(groups)
     last = col_bits.pop()
     for bit in col_bits:
-        summed = keep + swap(send, 0, bit | 1).astype(F32)
+        if bit == col_bits[0]:
+            got = jnp.concatenate([swap(send, 0, bit | 1), swap(more, 0, bit | 1)], axis=0)
+        else:
+            got = swap(send, 0, bit | 1)
+        summed = keep + got.astype(F32)
         if bit != col_bits[-1]:
             pairs = summed.reshape((-1, 2) + summed.shape[1:])
             keep, send = pairs[:, 0], pairs[:, 1].astype(BF16)

time: 40.2 us -> 40.1 us (level)
  waiting for transfers between devices: 14.5 us -> 13.6 us
  starting transfers between devices: 17.4 us -> 18.2 us
    ppermute x15 -> x16, waiting for transfers between devices: 14.5 us -> 13.6 us  [swap(): return lax.ppermute(value, ('row', 'col'), pairs)]
    ppermute x15 -> x16, starting transfers between devices: 17.4 us -> 18.2 us  [swap(): return lax.ppermute(value, ('row', 'col'), pairs)]
    pallas_call x1 -> x2, Pallas kernels: 0.72 us -> 1.09 us  [the longest x1 0.72 us: on_device(): pl.pallas_call(lambda *refs: keep_kernel(groups, per_piece, 0, 0, *refs),...]
  transfers between devices with their start and end apart: 15 -> 16, of which waited for: 12 -> 12; matrix products, arithmetic and copies ran while one was open for 0% -> 0% of each run, Pallas kernels for 6% -> 7%
where the time goes in v9:
time: 40.1 us; the launch traced here: 39.9 us
  starting transfers between devices  18.2 us (45%)
  waiting for transfers between devices  13.6 us (34%)
  Pallas kernels  7.3 us (18%)
  between operations  0.72 us (2%)
    ppermute x16, starting transfers between devices, swap(): return lax.ppermute(value, ('row', 'col'), pairs)  18.2 us
    ppermute x16, waiting for transfers between devices, swap(): return lax.ppermute(value, ('row', 'col'), pairs)  13.6 us
    pallas_call x1, Pallas kernels, on_device(): pl.pallas_call(lambda *refs: finish_kernel(total_rows, *refs), out_shape=...  2.64 us
    pallas_call x1, Pallas kernels, on_device(): pl.pallas_call(lambda *refs: load_kernel(per_piece, sources * per_piece,...  1.72 us
    pallas_call x1, Pallas kernels, on_device(): pl.pallas_call(scale_kernel, out_shape=[jax.ShapeDtypeStruct((vectors, ow...  0.86 us
  transfers between devices with their start and end apart: 16, of which 12 were waited for; matrix products, arithmetic and copies ran while one was open for 0% of the time, Pallas kernels for 7%

profile of v9, /device:TPU:0, one launch (start us, length us, event | category | flops | bytes accessed | tf_op | source)
XLA Modules:
  0.0 39.9 jit_solution(2563702797940244365)
XLA Ops:
  0.6 0.9 %scale.1 = (bf16[64,512]{1,0:T(8,128)(2,1)S(1)}, bf16[80,512]{1,0:T(8,128)(2,1)S(1)}) custom-call(bf16[64,512]{1,0:T(8,128)(2,1)} %basis_ref.1, s32[1,512]{1,0:T(1,128)} %bitcast.27), custom_call_target="tpu_custom_call" | custom-call | tf_op jit(solution)/shard_map/scale/pallas_call | solution.py:241
  1.5 4.1 %collective-permute-start = (bf16[64,512]{1,0:T(8,128)(2,1)S(1)}, bf16[64,512]{1,0:T(8,128)(2,1)S(1)}, u32[]{:S(2)}, u32[]{:S(2)}) collective-permute-start(bf16[64,512]{1,0:T(8,128)(2,1)S(1)} %get-tuple-element.15), channel_id=1, source_target_pairs={{0,16},{1,17},{2,18},{3,19},{4,20},{5,21},{6,22},{7,23},{8,24},{9,... | collective-permute-start | bytes 196616 | tf_op jit(solution)/shard_map/ppermute | solution.py:33
  5.6 1.6 %collective-permute-start.2 = (bf16[64,512]{1,0:T(8,128)(2,1)S(1)}, bf16[64,512]{1,0:T(8,128)(2,1)S(1)}, u32[]{:S(2)}, u32[]{:S(2)}) collective-permute-start(bf16[64,512]{1,0:T(8,128)(2,1)S(1)} %get-tuple-element.15), channel_id=1, source_target_pairs={{0,8},{1,9},{2,10},{3,11},{4,12},{5,13},{6,14},{7,15},{8,0},{9,1},... | collective-permute-start | bytes 196616 | tf_op jit(solution)/shard_map/ppermute | solution.py:33
  7.2 1.5 %collective-permute-start.1 = (bf16[64,512]{1,0:T(8,128)(2,1)S(1)}, bf16[64,512]{1,0:T(8,128)(2,1)S(1)}, u32[]{:S(2)}, u32[]{:S(2)}) collective-permute-start(bf16[64,512]{1,0:T(8,128)(2,1)S(1)} %get-tuple-element.15), channel_id=1, source_target_pairs={{0,4},{1,5},{2,6},{3,7},{4,0},{5,1},{6,2},{7,3},{8,12},{9,13},{10,... | collective-permute-start | bytes 196616 | tf_op jit(solution)/shard_map/ppermute | solution.py:33
  8.7 0.4 %collective-permute-start.3 = (bf16[64,512]{1,0:T(8,128)(2,1)S(1)}, bf16[64,512]{1,0:T(8,128)(2,1)S(1)}, u32[]{:S(2)}, u32[]{:S(2)}) collective-permute-start(bf16[64,512]{1,0:T(8,128)(2,1)S(1)} %get-tuple-element.15), channel_id=1, source_target_pairs={{0,12},{1,13},{2,14},{3,15},{4,8},{5,9},{6,10},{7,11},{8,4},{9,5},... | collective-permute-start | bytes 196616 | tf_op jit(solution)/shard_map/ppermute | solution.py:33
  9.1 0.0 collective-permute-done
  9.1 2.5 %collective-permute-start.4 = (bf16[64,512]{1,0:T(8,128)(2,1)S(1)}, bf16[64,512]{1,0:T(8,128)(2,1)S(1)}, u32[]{:S(2)}, u32[]{:S(2)}) collective-permute-start(bf16[64,512]{1,0:T(8,128)(2,1)S(1)} %collective-permute-done), channel_id=1, source_target_pairs={{0,12},{1,13},{2,14},{3,15},{4,8},{5,9},{6,10},{7,11},{8,4},{9,5},... | collective-permute-start | bytes 196616 | tf_op jit(solution)/shard_map/ppermute | solution.py:33
  11.6 0.4 %collective-permute-start.5 = (bf16[64,512]{1,0:T(8,128)(2,1)S(1)}, bf16[64,512]{1,0:T(8,128)(2,1)S(1)}, u32[]{:S(2)}, u32[]{:S(2)}) collective-permute-start(bf16[64,512]{1,0:T(8,128)(2,1)S(1)} %collective-permute-done), channel_id=1, source_target_pairs={{0,8},{1,9},{2,10},{3,11},{4,12},{5,13},{6,14},{7,15},{8,0},{9,1},... | collective-permute-start | bytes 196616 | tf_op jit(solution)/shard_map/ppermute | solution.py:33
  12.0 0.0 collective-permute-done.2
  12.0 0.5 %collective-permute-start.6 = (bf16[64,512]{1,0:T(8,128)(2,1)S(1)}, bf16[64,512]{1,0:T(8,128)(2,1)S(1)}, u32[]{:S(2)}, u32[]{:S(2)}) collective-permute-start(bf16[64,512]{1,0:T(8,128)(2,1)S(1)} %collective-permute-done), channel_id=1, source_target_pairs={{0,4},{1,5},{2,6},{3,7},{4,0},{5,1},{6,2},{7,3},{8,12},{9,13},{10,... | collective-permute-start | bytes 196616 | tf_op jit(solution)/shard_map/ppermute | solution.py:33
  12.6 0.3 collective-permute-done.1
  12.8 0.0 collective-permute-start.7
  12.9 1.7 %load.1 = (s32[8,32]{1,0:T(8,128)S(4)}, bf16[32,64,512]{2,1,0:T(8,128)(2,1)S(1)}, bf16[65,64,128]{2,1,0:T(8,128)(2,1)S(1)}) custom-call(s32[8,32]{1,0:T(8,128)} %bitcast.25, s32[8,32]{1,0:T(8,128)} %bitcast.26, bf16[32,64,512]{2,1,0:T(8,128)(2,1)} %bitcast.21, bf16[4,64,512]{2,1,0:T(8,128)(2,1)S(1)} %pad_maximum_fusion.refs_3_), custom_call_target="tpu_custom_call" | custom-call | tf_op jit(solution)/shard_map/load/pallas_call | solution.py:277
  14.6 0.0 collective-permute-done.3
  14.6 0.2 collective-permute-done.4
  14.8 1.0 %collective-permute-done.5 = bf16[64,512]{1,0:T(8,128)(2,1)S(1)} collective-permute-done((bf16[64,512]{1,0:T(8,128)(2,1)S(1)}, bf16[64,512]{1,0:T(8,128)(2,1)S(1)}, u32[]{:S(2)}, u32[]{:S(2)}) %collective-permute-start.5) | collective-permute-done | bytes 65568 | tf_op jit(solution)/shard_map/ppermute | solution.py:33
  15.9 0.5 %collective-permute-done.6 = bf16[64,512]{1,0:T(8,128)(2,1)S(1)} collective-permute-done((bf16[64,512]{1,0:T(8,128)(2,1)S(1)}, bf16[64,512]{1,0:T(8,128)(2,1)S(1)}, u32[]{:S(2)}, u32[]{:S(2)}) %collective-permute-start.6) | collective-permute-done | bytes 65568 | tf_op jit(solution)/shard_map/ppermute | solution.py:33
  16.3 0.5 %send.1 = (bf16[65,64,128]{2,1,0:T(8,128)(2,1)S(1)}, bf16[1,64,512]{2,1,0:T(8,128)(2,1)S(1)}) custom-call(s32[8,32]{1,0:T(8,128)S(4)} %get-tuple-element.19.refs_0_, bf16[32,64,512]{2,1,0:T(8,128)(2,1)S(1)} %get-tuple-element.20.refs_1_, bf16[65,64,128]{2,1,0:T(8,128)(2,1)S(1)} %get-tuple-element.21.refs_2_, ...), custom_call_target="tpu_custom_call", output_to_operand_aliasing={{0}: (2, {})} | custom-call | tf_op jit(solution)/shard_map/send/pallas_call | solution.py:297
  16.8 0.4 more.1
  17.2 0.1 collective-permute-start.9
  17.3 0.2 collective-permute-done.7.refs_1_
  17.5 0.3 collective-permute-start.8
  17.8 0.7 %keep.1 = f32[2,64,512]{2,1,0:T(8,128)S(1)} custom-call(s32[8,32]{1,0:T(8,128)S(4)} %get-tuple-element.19.refs_0_, bf16[32,64,512]{2,1,0:T(8,128)(2,1)S(1)} %get-tuple-element.20.refs_1_, bf16[65,64,128]{2,1,0:T(8,128)(2,1)S(1)} %get-tuple-element.24.refs_2_), custom_call_target="tpu_custom_call" | custom-call | tf_op jit(solution)/shard_map/keep/pallas_call | solution.py:320
  18.5 0.0 collective-permute-done.9
  18.5 0.3 collective-permute-done.8
  18.8 1.5 %collective-permute-start.10 = (bf16[2,64,512]{2,1,0:T(8,128)(2,1)S(1)}, bf16[2,64,512]{2,1,0:T(8,128)(2,1)S(1)}, u32[]{:S(2)}, u32[]{:S(2)}) collective-permute-start(bf16[2,64,512]{2,1,0:T(8,128)(2,1)S(1)} %add_convert_fusion.refs_2_), channel_id=1, source_target_pairs={{0,3},{1,2},{2,1},{3,0},{4,7},{5,6},{6,5},{7,4},{8,11},{9,10},{10,... | collective-permute-start | bytes 393224 | tf_op jit(solution)/shard_map/ppermute | solution.py:33
  20.2 4.0 %collective-permute-done.10.refs_3_ = bf16[2,64,512]{2,1,0:T(8,128)(2,1)S(1)} collective-permute-done((bf16[2,64,512]{2,1,0:T(8,128)(2,1)S(1)}, bf16[2,64,512]{2,1,0:T(8,128)(2,1)S(1)}, u32[]{:S(2)}, u32[]{:S(2)}) %collective-permute-start.10) | collective-permute-done | bytes 131104 | tf_op jit(solution)/shard_map/ppermute | solution.py:33
  24.3 0.5 %gram.1 = (bf16[192,512]{1,0:T(8,128)(2,1)S(1)}, f32[64,128]{1,0:T(8,128)S(1)}) custom-call(bf16[80,512]{1,0:T(8,128)(2,1)S(1)} %get-tuple-element.17.refs_0_, bf16[80,512]{1,0:T(8,128)(2,1)S(1)} %collective-permute-done.7.refs_1_, bf16[2,64,512]{2,1,0:T(8,128)(2,1)S(1)} %add_convert_fusion.refs_2_, bf16[2,64,512]{2,1,0:T(8,128)(2,1)S(1)} %collective-permute-done.10.refs_3_), custom_call_target="tpu_custom_call" | custom-call | tf_op jit(solution)/shard_map/gram/pallas_call | solution.py:342
  24.8 0.2 collective-permute-start.11
  25.1 1.0 %collective-permute-done.11 = f32[64,128]{1,0:T(8,128)S(1)} collective-permute-done((f32[64,128]{1,0:T(8,128)S(1)}, f32[64,128]{1,0:T(8,128)S(1)}, u32[]{:S(2)}, u32[]{:S(2)}) %collective-permute-start.11) | collective-permute-done | bytes 32800 | tf_op jit(solution)/shard_map/ppermute | solution.py:33
  26.1 1.9 %collective-permute-start.12 = (f32[64,128]{1,0:T(8,128)S(1)}, f32[64,128]{1,0:T(8,128)S(1)}, u32[]{:S(2)}, u32[]{:S(2)}) collective-permute-start(f32[64,128]{1,0:T(8,128)S(1)} %add.19), channel_id=1, source_target_pairs={{0,17},{1,16},{2,19},{3,18},{4,21},{5,20},{6,23},{7,22},{8,25},{9,... | collective-permute-start | bytes 98312 | tf_op jit(solution)/shard_map/ppermute | solution.py:33
  28.0 2.3 %collective-permute-done.12 = f32[64,128]{1,0:T(8,128)S(1)} collective-permute-done((f32[64,128]{1,0:T(8,128)S(1)}, f32[64,128]{1,0:T(8,128)S(1)}, u32[]{:S(2)}, u32[]{:S(2)}) %collective-permute-start.12) | collective-permute-done | bytes 32800 | tf_op jit(solution)/shard_map/ppermute | solution.py:33
  30.3 2.4 %collective-permute-start.14 = (f32[64,128]{1,0:T(8,128)S(1)}, f32[64,128]{1,0:T(8,128)S(1)}, u32[]{:S(2)}, u32[]{:S(2)}) collective-permute-start(f32[64,128]{1,0:T(8,128)S(1)} %add.20), channel_id=1, source_target_pairs={{0,5},{1,4},{2,7},{3,6},{4,1},{5,0},{6,3},{7,2},{8,13},{9,12},{10,... | collective-permute-start | bytes 98312 | tf_op jit(solution)/shard_map/ppermute | solution.py:33
  32.7 0.3 collective-permute-start.15
  33.0 0.5 %collective-permute-start.13 = (f32[64,128]{1,0:T(8,128)S(1)}, f32[64,128]{1,0:T(8,128)S(1)}, u32[]{:S(2)}, u32[]{:S(2)}) collective-permute-start(f32[64,128]{1,0:T(8,128)S(1)} %add.20), channel_id=1, source_target_pairs={{0,13},{1,12},{2,15},{3,14},{4,9},{5,8},{6,11},{7,10},{8,5},{9,4},... | collective-permute-start | bytes 98312 | tf_op jit(solution)/shard_map/ppermute | solution.py:33
  33.5 1.0 %collective-permute-done.14 = f32[64,128]{1,0:T(8,128)S(1)} collective-permute-done((f32[64,128]{1,0:T(8,128)S(1)}, f32[64,128]{1,0:T(8,128)S(1)}, u32[]{:S(2)}, u32[]{:S(2)}) %collective-permute-start.14) | collective-permute-done | bytes 32800 | tf_op jit(solution)/shard_map/ppermute | solution.py:33
  34.5 1.7 %collective-permute-done.15 = f32[64,128]{1,0:T(8,128)S(1)} collective-permute-done((f32[64,128]{1,0:T(8,128)S(1)}, f32[64,128]{1,0:T(8,128)S(1)}, u32[]{:S(2)}, u32[]{:S(2)}) %collective-permute-start.15) | collective-permute-done | bytes 32800 | tf_op jit(solution)/shard_map/ppermute | solution.py:33
  36.2 1.0 %collective-permute-done.13 = f32[64,128]{1,0:T(8,128)S(1)} collective-permute-done((f32[64,128]{1,0:T(8,128)S(1)}, f32[64,128]{1,0:T(8,128)S(1)}, u32[]{:S(2)}, u32[]{:S(2)}) %collective-permute-start.13) | collective-permute-done | bytes 32800 | tf_op jit(solution)/shard_map/ppermute | solution.py:33
  37.2 2.6 %finish.1 = (f32[64,512]{1,0:T(8,128)}, f32[64,64]{1,0:T(8,128)}) custom-call(f32[64,128]{1,0:T(8,128)S(1)} %add_add_fusion.refs_0_, bf16[192,512]{1,0:T(8,128)(2,1)S(1)} %get-tuple-element.27.refs_1_), custom_call_target="tpu_custom_call" | custom-call | tf_op jit(solution)/shard_map/finish/pallas_call | solution.py:362
  (5 shorter events, 0.1 us)
Async XLA Ops:
  1.5 7.6 %collective-permute-start = (bf16[64,512]{1,0:T(8,128)(2,1)S(1)}, bf16[64,512]{1,0:T(8,128)(2,1)S(1)}, u32[]{:S(2)}, u32[]{:S(2)}) collective-permute-start(bf16[64,512]{1,0:T(8,128)(2,1)S(1)} %get-tuple-element.15), channel_id=1, source_target_pairs={{0,16},{1,17},{2,18},{3,19},{4,20},{5,21},{6,22},{7,23},{8,24},{9,... | collective-permute-start | bytes 196616 | tf_op jit(solution)/shard_map/ppermute | solution.py:33
  5.6 6.5 %collective-permute-start.2 = (bf16[64,512]{1,0:T(8,128)(2,1)S(1)}, bf16[64,512]{1,0:T(8,128)(2,1)S(1)}, u32[]{:S(2)}, u32[]{:S(2)}) collective-permute-start(bf16[64,512]{1,0:T(8,128)(2,1)S(1)} %get-tuple-element.15), channel_id=1, source_target_pairs={{0,8},{1,9},{2,10},{3,11},{4,12},{5,13},{6,14},{7,15},{8,0},{9,1},... | collective-permute-start | bytes 196616 | tf_op jit(solution)/shard_map/ppermute | solution.py:33
  7.2 5.7 %collective-permute-start.1 = (bf16[64,512]{1,0:T(8,128)(2,1)S(1)}, bf16[64,512]{1,0:T(8,128)(2,1)S(1)}, u32[]{:S(2)}, u32[]{:S(2)}) collective-permute-start(bf16[64,512]{1,0:T(8,128)(2,1)S(1)} %get-tuple-element.15), channel_id=1, source_target_pairs={{0,4},{1,5},{2,6},{3,7},{4,0},{5,1},{6,2},{7,3},{8,12},{9,13},{10,... | collective-permute-start | bytes 196616 | tf_op jit(solution)/shard_map/ppermute | solution.py:33
  8.7 6.0 %collective-permute-start.3 = (bf16[64,512]{1,0:T(8,128)(2,1)S(1)}, bf16[64,512]{1,0:T(8,128)(2,1)S(1)}, u32[]{:S(2)}, u32[]{:S(2)}) collective-permute-start(bf16[64,512]{1,0:T(8,128)(2,1)S(1)} %get-tuple-element.15), channel_id=1, source_target_pairs={{0,12},{1,13},{2,14},{3,15},{4,8},{5,9},{6,10},{7,11},{8,4},{9,5},... | collective-permute-start | bytes 196616 | tf_op jit(solution)/shard_map/ppermute | solution.py:33
  9.1 5.7 %collective-permute-start.4 = (bf16[64,512]{1,0:T(8,128)(2,1)S(1)}, bf16[64,512]{1,0:T(8,128)(2,1)S(1)}, u32[]{:S(2)}, u32[]{:S(2)}) collective-permute-start(bf16[64,512]{1,0:T(8,128)(2,1)S(1)} %collective-permute-done), channel_id=1, source_target_pairs={{0,12},{1,13},{2,14},{3,15},{4,8},{5,9},{6,10},{7,11},{8,4},{9,5},... | collective-permute-start | bytes 196616 | tf_op jit(solution)/shard_map/ppermute | solution.py:33
  11.6 4.3 %collective-permute-start.5 = (bf16[64,512]{1,0:T(8,128)(2,1)S(1)}, bf16[64,512]{1,0:T(8,128)(2,1)S(1)}, u32[]{:S(2)}, u32[]{:S(2)}) collective-permute-start(bf16[64,512]{1,0:T(8,128)(2,1)S(1)} %collective-permute-done), channel_id=1, source_target_pairs={{0,8},{1,9},{2,10},{3,11},{4,12},{5,13},{6,14},{7,15},{8,0},{9,1},... | collective-permute-start | bytes 196616 | tf_op jit(solution)/shard_map/ppermute | solution.py:33
  12.0 4.3 %collective-permute-start.6 = (bf16[64,512]{1,0:T(8,128)(2,1)S(1)}, bf16[64,512]{1,0:T(8,128)(2,1)S(1)}, u32[]{:S(2)}, u32[]{:S(2)}) collective-permute-start(bf16[64,512]{1,0:T(8,128)(2,1)S(1)} %collective-permute-done), channel_id=1, source_target_pairs={{0,4},{1,5},{2,6},{3,7},{4,0},{5,1},{6,2},{7,3},{8,12},{9,13},{10,... | collective-permute-start | bytes 196616 | tf_op jit(solution)/shard_map/ppermute | solution.py:33
  12.8 4.7 %collective-permute-start.7 = (bf16[80,512]{1,0:T(8,128)(2,1)S(1)}, bf16[80,512]{1,0:T(8,128)(2,1)S(1)}, u32[]{:S(2)}, u32[]{:S(2)}) collective-permute-start(bf16[80,512]{1,0:T(8,128)(2,1)S(1)} %get-tuple-element.17.refs_0_), channel_id=1, source_target_pairs={{0,3},{1,2},{2,1},{3,0},{4,7},{5,6},{6,5},{7,4},{8,11},{9,10},{10,... | collective-permute-start | bytes 245768 | tf_op jit(solution)/shard_map/ppermute | solution.py:33
  17.2 1.3 %collective-permute-start.9 = (bf16[1,64,512]{2,1,0:T(8,128)(2,1)S(1)}, bf16[1,64,512]{2,1,0:T(8,128)(2,1)S(1)}, u32[]{:S(2)}, u32[]{:S(2)}) collective-permute-start(bf16[1,64,512]{2,1,0:T(8,128)(2,1)S(1)} %more.1), channel_id=1, source_target_pairs={{0,1},{1,0},{2,3},{3,2},{4,5},{5,4},{6,7},{7,6},{8,9},{9,8},{10,11... | collective-permute-start | bytes 196616 | tf_op jit(solution)/shard_map/ppermute | solution.py:33
  17.5 1.3 %collective-permute-start.8 = (bf16[1,64,512]{2,1,0:T(8,128)(2,1)S(1)}, bf16[1,64,512]{2,1,0:T(8,128)(2,1)S(1)}, u32[]{:S(2)}, u32[]{:S(2)}) collective-permute-start(bf16[1,64,512]{2,1,0:T(8,128)(2,1)S(1)} %get-tuple-element.25), channel_id=1, source_target_pairs={{0,1},{1,0},{2,3},{3,2},{4,5},{5,4},{6,7},{7,6},{8,9},{9,8},{10,11... | collective-permute-start | bytes 196616 | tf_op jit(solution)/shard_map/ppermute | solution.py:33
  18.8 5.5 %collective-permute-start.10 = (bf16[2,64,512]{2,1,0:T(8,128)(2,1)S(1)}, bf16[2,64,512]{2,1,0:T(8,128)(2,1)S(1)}, u32[]{:S(2)}, u32[]{:S(2)}) collective-permute-start(bf16[2,64,512]{2,1,0:T(8,128)(2,1)S(1)} %add_convert_fusion.refs_2_), channel_id=1, source_target_pairs={{0,3},{1,2},{2,1},{3,0},{4,7},{5,6},{6,5},{7,4},{8,11},{9,10},{10,... | collective-permute-start | bytes 393224 | tf_op jit(solution)/shard_map/ppermute | solution.py:33
  24.8 1.3 %collective-permute-start.11 = (f32[64,128]{1,0:T(8,128)S(1)}, f32[64,128]{1,0:T(8,128)S(1)}, u32[]{:S(2)}, u32[]{:S(2)}) collective-permute-start(f32[64,128]{1,0:T(8,128)S(1)} %get-tuple-element.26), channel_id=1, source_target_pairs={{0,1},{1,0},{2,3},{3,2},{4,5},{5,4},{6,7},{7,6},{8,9},{9,8},{10,11... | collective-permute-start | bytes 98312 | tf_op jit(solution)/shard_map/ppermute | solution.py:33
  26.1 4.2 %collective-permute-start.12 = (f32[64,128]{1,0:T(8,128)S(1)}, f32[64,128]{1,0:T(8,128)S(1)}, u32[]{:S(2)}, u32[]{:S(2)}) collective-permute-start(f32[64,128]{1,0:T(8,128)S(1)} %add.19), channel_id=1, source_target_pairs={{0,17},{1,16},{2,19},{3,18},{4,21},{5,20},{6,23},{7,22},{8,25},{9,... | collective-permute-start | bytes 98312 | tf_op jit(solution)/shard_map/ppermute | solution.py:33
  30.3 4.2 %collective-permute-start.14 = (f32[64,128]{1,0:T(8,128)S(1)}, f32[64,128]{1,0:T(8,128)S(1)}, u32[]{:S(2)}, u32[]{:S(2)}) collective-permute-start(f32[64,128]{1,0:T(8,128)S(1)} %add.20), channel_id=1, source_target_pairs={{0,5},{1,4},{2,7},{3,6},{4,1},{5,0},{6,3},{7,2},{8,13},{9,12},{10,... | collective-permute-start | bytes 98312 | tf_op jit(solution)/shard_map/ppermute | solution.py:33
  32.7 3.5 %collective-permute-start.15 = (f32[64,128]{1,0:T(8,128)S(1)}, f32[64,128]{1,0:T(8,128)S(1)}, u32[]{:S(2)}, u32[]{:S(2)}) collective-permute-start(f32[64,128]{1,0:T(8,128)S(1)} %add.20), channel_id=1, source_target_pairs={{0,9},{1,8},{2,11},{3,10},{4,13},{5,12},{6,15},{7,14},{8,1},{9,0},... | collective-permute-start | bytes 98312 | tf_op jit(solution)/shard_map/ppermute | solution.py:33
  33.0 4.2 %collective-permute-start.13 = (f32[64,128]{1,0:T(8,128)S(1)}, f32[64,128]{1,0:T(8,128)S(1)}, u32[]{:S(2)}, u32[]{:S(2)}) collective-permute-start(f32[64,128]{1,0:T(8,128)S(1)} %add.20), channel_id=1, source_target_pairs={{0,13},{1,12},{2,15},{3,14},{4,9},{5,8},{6,11},{7,10},{8,5},{9,4},... | collective-permute-start | bytes 98312 | tf_op jit(solution)/shard_map/ppermute | solution.py:33

commit v10 on v8

--- a/solution.py
+++ b/solution.py
@@ -260,7 +260,7 @@
         blocks = blocks + [(at ^ bit, stack[place]) for place, (at, _) in enumerate(blocks)]
     base = [at for at, _ in blocks]
     named = dict(blocks)
-    direct = [mask for mask in (low[0], low[1], diag)]
+    direct = [mask for mask in (diag, low[1], low[0])]
     relayed = [(mask, at) for at in base[1:] for mask in (diag, low[1], low[0]) if (mask ^ at) not in direct]
     pieces = [(mask, swap(scaled, mask, 0)) for mask in direct]
     early = blocks + pieces[:2]

time: 40.2 us -> 40.1 us (level)
  starting transfers between devices: 17.4 us -> 16.7 us
  waiting for transfers between devices: 14.5 us -> 15.1 us
    ppermute x15, starting transfers between devices: 17.4 us -> 16.7 us  [swap(): return lax.ppermute(value, ('row', 'col'), pairs)]
    ppermute x15, waiting for transfers between devices: 14.5 us -> 15.1 us  [swap(): return lax.ppermute(value, ('row', 'col'), pairs)]
  transfers between devices with their start and end apart: 15 -> 15, of which waited for: 12 -> 11; matrix products, arithmetic and copies ran while one was open for 0% -> 0% of each run, Pallas kernels for 6% -> 6%
where the time goes in v10:
time: 40.1 us; the launch traced here: 39.9 us
  starting transfers between devices  16.7 us (42%)
  waiting for transfers between devices  15.1 us (38%)
  Pallas kernels  7.31 us (18%)
  between operations  0.7 us (2%)
    ppermute x15, starting transfers between devices, swap(): return lax.ppermute(value, ('row', 'col'), pairs)  16.7 us
    ppermute x15, waiting for transfers between devices, swap(): return lax.ppermute(value, ('row', 'col'), pairs)  15.1 us
    pallas_call x1, Pallas kernels, on_device(): pl.pallas_call(lambda *refs: finish_kernel(total_rows, *refs), out_shape=...  2.64 us
    pallas_call x1, Pallas kernels, on_device(): pl.pallas_call(lambda *refs: load_kernel(per_piece, sources * per_piece,...  1.72 us
    pallas_call x1, Pallas kernels, on_device(): pl.pallas_call(lambda *refs: send_kernel(groups, per_piece, late, *refs),...  0.87 us
    pallas_call x1, Pallas kernels, on_device(): pl.pallas_call(scale_kernel, out_shape=[jax.ShapeDtypeStruct((vectors, ow...  0.86 us
  transfers between devices with their start and end apart: 15, of which 11 were waited for; matrix products, arithmetic and copies ran while one was open for 0% of the time, Pallas kernels for 6%

profile of v10, /device:TPU:0, one launch (start us, length us, event | category | flops | bytes accessed | tf_op | source)
XLA Modules:
  0.0 39.9 jit_solution(13639481813791096721)
XLA Ops:
  0.6 0.9 %scale.1 = (bf16[64,512]{1,0:T(8,128)(2,1)S(1)}, bf16[80,512]{1,0:T(8,128)(2,1)S(1)}) custom-call(bf16[64,512]{1,0:T(8,128)(2,1)} %basis_ref.1, s32[1,512]{1,0:T(1,128)} %bitcast.27), custom_call_target="tpu_custom_call" | custom-call | tf_op jit(solution)/shard_map/scale/pallas_call | solution.py:240
  1.5 4.1 %collective-permute-start = (bf16[64,512]{1,0:T(8,128)(2,1)S(1)}, bf16[64,512]{1,0:T(8,128)(2,1)S(1)}, u32[]{:S(2)}, u32[]{:S(2)}) collective-permute-start(bf16[64,512]{1,0:T(8,128)(2,1)S(1)} %get-tuple-element.15), channel_id=1, source_target_pairs={{0,16},{1,17},{2,18},{3,19},{4,20},{5,21},{6,22},{7,23},{8,24},{9,... | collective-permute-start | bytes 196616 | tf_op jit(solution)/shard_map/ppermute | solution.py:33
  5.6 1.6 %collective-permute-start.2 = (bf16[64,512]{1,0:T(8,128)(2,1)S(1)}, bf16[64,512]{1,0:T(8,128)(2,1)S(1)}, u32[]{:S(2)}, u32[]{:S(2)}) collective-permute-start(bf16[64,512]{1,0:T(8,128)(2,1)S(1)} %get-tuple-element.15), channel_id=1, source_target_pairs={{0,8},{1,9},{2,10},{3,11},{4,12},{5,13},{6,14},{7,15},{8,0},{9,1},... | collective-permute-start | bytes 196616 | tf_op jit(solution)/shard_map/ppermute | solution.py:33
  7.2 1.4 %collective-permute-start.1 = (bf16[64,512]{1,0:T(8,128)(2,1)S(1)}, bf16[64,512]{1,0:T(8,128)(2,1)S(1)}, u32[]{:S(2)}, u32[]{:S(2)}) collective-permute-start(bf16[64,512]{1,0:T(8,128)(2,1)S(1)} %get-tuple-element.15), channel_id=1, source_target_pairs={{0,12},{1,13},{2,14},{3,15},{4,8},{5,9},{6,10},{7,11},{8,4},{9,5},... | collective-permute-start | bytes 196616 | tf_op jit(solution)/shard_map/ppermute | solution.py:33
  8.5 0.5 %collective-permute-start.3 = (bf16[64,512]{1,0:T(8,128)(2,1)S(1)}, bf16[64,512]{1,0:T(8,128)(2,1)S(1)}, u32[]{:S(2)}, u32[]{:S(2)}) collective-permute-start(bf16[64,512]{1,0:T(8,128)(2,1)S(1)} %get-tuple-element.15), channel_id=1, source_target_pairs={{0,4},{1,5},{2,6},{3,7},{4,0},{5,1},{6,2},{7,3},{8,12},{9,13},{10,... | collective-permute-start | bytes 196616 | tf_op jit(solution)/shard_map/ppermute | solution.py:33
  9.1 0.0 collective-permute-done
  9.1 2.5 %collective-permute-start.4 = (bf16[64,512]{1,0:T(8,128)(2,1)S(1)}, bf16[64,512]{1,0:T(8,128)(2,1)S(1)}, u32[]{:S(2)}, u32[]{:S(2)}) collective-permute-start(bf16[64,512]{1,0:T(8,128)(2,1)S(1)} %collective-permute-done), channel_id=1, source_target_pairs={{0,12},{1,13},{2,14},{3,15},{4,8},{5,9},{6,10},{7,11},{8,4},{9,5},... | collective-permute-start | bytes 196616 | tf_op jit(solution)/shard_map/ppermute | solution.py:33
  11.6 0.4 %collective-permute-start.5 = (bf16[64,512]{1,0:T(8,128)(2,1)S(1)}, bf16[64,512]{1,0:T(8,128)(2,1)S(1)}, u32[]{:S(2)}, u32[]{:S(2)}) collective-permute-start(bf16[64,512]{1,0:T(8,128)(2,1)S(1)} %collective-permute-done), channel_id=1, source_target_pairs={{0,8},{1,9},{2,10},{3,11},{4,12},{5,13},{6,14},{7,15},{8,0},{9,1},... | collective-permute-start | bytes 196616 | tf_op jit(solution)/shard_map/ppermute | solution.py:33
  12.0 0.0 collective-permute-done.2
  12.0 0.5 %collective-permute-start.6 = (bf16[64,512]{1,0:T(8,128)(2,1)S(1)}, bf16[64,512]{1,0:T(8,128)(2,1)S(1)}, u32[]{:S(2)}, u32[]{:S(2)}) collective-permute-start(bf16[64,512]{1,0:T(8,128)(2,1)S(1)} %collective-permute-done), channel_id=1, source_target_pairs={{0,4},{1,5},{2,6},{3,7},{4,0},{5,1},{6,2},{7,3},{8,12},{9,13},{10,... | collective-permute-start | bytes 196616 | tf_op jit(solution)/shard_map/ppermute | solution.py:33
  12.6 0.5 %collective-permute-done.1 = bf16[64,512]{1,0:T(8,128)(2,1)S(1)} collective-permute-done((bf16[64,512]{1,0:T(8,128)(2,1)S(1)}, bf16[64,512]{1,0:T(8,128)(2,1)S(1)}, u32[]{:S(2)}, u32[]{:S(2)}) %collective-permute-start.1) | collective-permute-done | bytes 65568 | tf_op jit(solution)/shard_map/ppermute | solution.py:33
  13.1 0.0 collective-permute-start.7
  13.1 1.7 %load.1 = (s32[8,32]{1,0:T(8,128)S(4)}, bf16[32,64,512]{2,1,0:T(8,128)(2,1)S(1)}, bf16[65,64,128]{2,1,0:T(8,128)(2,1)S(1)}) custom-call(s32[8,32]{1,0:T(8,128)} %bitcast.25, s32[8,32]{1,0:T(8,128)} %bitcast.26, bf16[32,64,512]{2,1,0:T(8,128)(2,1)} %bitcast.21, bf16[4,64,512]{2,1,0:T(8,128)(2,1)S(1)} %pad_maximum_fusion.refs_3_), custom_call_target="tpu_custom_call" | custom-call | tf_op jit(solution)/shard_map/load/pallas_call | solution.py:276
  14.9 0.0 collective-permute-done.3
  14.9 0.0 collective-permute-done.4
  14.9 1.0 %collective-permute-done.5 = bf16[64,512]{1,0:T(8,128)(2,1)S(1)} collective-permute-done((bf16[64,512]{1,0:T(8,128)(2,1)S(1)}, bf16[64,512]{1,0:T(8,128)(2,1)S(1)}, u32[]{:S(2)}, u32[]{:S(2)}) %collective-permute-start.5) | collective-permute-done | bytes 65568 | tf_op jit(solution)/shard_map/ppermute | solution.py:33
  15.9 0.5 %collective-permute-done.6 = bf16[64,512]{1,0:T(8,128)(2,1)S(1)} collective-permute-done((bf16[64,512]{1,0:T(8,128)(2,1)S(1)}, bf16[64,512]{1,0:T(8,128)(2,1)S(1)}, u32[]{:S(2)}, u32[]{:S(2)}) %collective-permute-start.6) | collective-permute-done | bytes 65568 | tf_op jit(solution)/shard_map/ppermute | solution.py:33
  16.3 0.9 %send.1 = (bf16[65,64,128]{2,1,0:T(8,128)(2,1)S(1)}, bf16[2,64,512]{2,1,0:T(8,128)(2,1)S(1)}) custom-call(s32[8,32]{1,0:T(8,128)S(4)} %get-tuple-element.19.refs_0_, bf16[32,64,512]{2,1,0:T(8,128)(2,1)S(1)} %get-tuple-element.20.refs_1_, bf16[65,64,128]{2,1,0:T(8,128)(2,1)S(1)} %get-tuple-element.21.refs_2_, ...), custom_call_target="tpu_custom_call", output_to_operand_aliasing={{0}: (2, {})} | custom-call | tf_op jit(solution)/shard_map/send/pallas_call | solution.py:296
  17.2 0.6 %collective-permute-done.7.refs_1_ = bf16[80,512]{1,0:T(8,128)(2,1)S(1)} collective-permute-done((bf16[80,512]{1,0:T(8,128)(2,1)S(1)}, bf16[80,512]{1,0:T(8,128)(2,1)S(1)}, u32[]{:S(2)}, u32[]{:S(2)}) %collective-permute-start.7) | collective-permute-done | bytes 81952 | tf_op jit(solution)/shard_map/ppermute | solution.py:33
  17.8 0.1 collective-permute-start.8
  17.9 0.7 %keep.1 = f32[2,64,512]{2,1,0:T(8,128)S(1)} custom-call(s32[8,32]{1,0:T(8,128)S(4)} %get-tuple-element.19.refs_0_, bf16[32,64,512]{2,1,0:T(8,128)(2,1)S(1)} %get-tuple-element.20.refs_1_, bf16[65,64,128]{2,1,0:T(8,128)(2,1)S(1)} %get-tuple-element.24.refs_2_), custom_call_target="tpu_custom_call" | custom-call | tf_op jit(solution)/shard_map/keep/pallas_call | solution.py:310
  18.6 0.5 %collective-permute-done.8 = bf16[2,64,512]{2,1,0:T(8,128)(2,1)S(1)} collective-permute-done((bf16[2,64,512]{2,1,0:T(8,128)(2,1)S(1)}, bf16[2,64,512]{2,1,0:T(8,128)(2,1)S(1)}, u32[]{:S(2)}, u32[]{:S(2)}) %collective-permute-start.8) | collective-permute-done | bytes 131104 | tf_op jit(solution)/shard_map/ppermute | solution.py:33
  19.2 0.8 %collective-permute-start.9 = (bf16[2,64,512]{2,1,0:T(8,128)(2,1)S(1)}, bf16[2,64,512]{2,1,0:T(8,128)(2,1)S(1)}, u32[]{:S(2)}, u32[]{:S(2)}) collective-permute-start(bf16[2,64,512]{2,1,0:T(8,128)(2,1)S(1)} %add_convert_fusion.refs_2_), channel_id=1, source_target_pairs={{0,3},{1,2},{2,1},{3,0},{4,7},{5,6},{6,5},{7,4},{8,11},{9,10},{10,... | collective-permute-start | bytes 393224 | tf_op jit(solution)/shard_map/ppermute | solution.py:33
  20.0 4.7 %collective-permute-done.9.refs_3_ = bf16[2,64,512]{2,1,0:T(8,128)(2,1)S(1)} collective-permute-done((bf16[2,64,512]{2,1,0:T(8,128)(2,1)S(1)}, bf16[2,64,512]{2,1,0:T(8,128)(2,1)S(1)}, u32[]{:S(2)}, u32[]{:S(2)}) %collective-permute-start.9) | collective-permute-done | bytes 131104 | tf_op jit(solution)/shard_map/ppermute | solution.py:33
  24.7 0.5 %gram.1 = (bf16[192,512]{1,0:T(8,128)(2,1)S(1)}, f32[64,128]{1,0:T(8,128)S(1)}) custom-call(bf16[80,512]{1,0:T(8,128)(2,1)S(1)} %get-tuple-element.17.refs_0_, bf16[80,512]{1,0:T(8,128)(2,1)S(1)} %collective-permute-done.7.refs_1_, bf16[2,64,512]{2,1,0:T(8,128)(2,1)S(1)} %add_convert_fusion.refs_2_, bf16[2,64,512]{2,1,0:T(8,128)(2,1)S(1)} %collective-permute-done.9.refs_3_), custom_call_target="tpu_custom_call" | custom-call | tf_op jit(solution)/shard_map/gram/pallas_call | solution.py:328
  25.2 0.2 collective-permute-start.10
  25.4 1.1 %collective-permute-done.10 = f32[64,128]{1,0:T(8,128)S(1)} collective-permute-done((f32[64,128]{1,0:T(8,128)S(1)}, f32[64,128]{1,0:T(8,128)S(1)}, u32[]{:S(2)}, u32[]{:S(2)}) %collective-permute-start.10) | collective-permute-done | bytes 32800 | tf_op jit(solution)/shard_map/ppermute | solution.py:33
  26.5 1.5 %collective-permute-start.11 = (f32[64,128]{1,0:T(8,128)S(1)}, f32[64,128]{1,0:T(8,128)S(1)}, u32[]{:S(2)}, u32[]{:S(2)}) collective-permute-start(f32[64,128]{1,0:T(8,128)S(1)} %add.19), channel_id=1, source_target_pairs={{0,17},{1,16},{2,19},{3,18},{4,21},{5,20},{6,23},{7,22},{8,25},{9,... | collective-permute-start | bytes 98312 | tf_op jit(solution)/shard_map/ppermute | solution.py:33
  27.9 2.8 %collective-permute-done.11 = f32[64,128]{1,0:T(8,128)S(1)} collective-permute-done((f32[64,128]{1,0:T(8,128)S(1)}, f32[64,128]{1,0:T(8,128)S(1)}, u32[]{:S(2)}, u32[]{:S(2)}) %collective-permute-start.11) | collective-permute-done | bytes 32800 | tf_op jit(solution)/shard_map/ppermute | solution.py:33
  30.7 1.1 %collective-permute-start.13 = (f32[64,128]{1,0:T(8,128)S(1)}, f32[64,128]{1,0:T(8,128)S(1)}, u32[]{:S(2)}, u32[]{:S(2)}) collective-permute-start(f32[64,128]{1,0:T(8,128)S(1)} %add.20), channel_id=1, source_target_pairs={{0,5},{1,4},{2,7},{3,6},{4,1},{5,0},{6,3},{7,2},{8,13},{9,12},{10,... | collective-permute-start | bytes 98312 | tf_op jit(solution)/shard_map/ppermute | solution.py:33
  31.8 1.2 %collective-permute-start.14 = (f32[64,128]{1,0:T(8,128)S(1)}, f32[64,128]{1,0:T(8,128)S(1)}, u32[]{:S(2)}, u32[]{:S(2)}) collective-permute-start(f32[64,128]{1,0:T(8,128)S(1)} %add.20), channel_id=1, source_target_pairs={{0,9},{1,8},{2,11},{3,10},{4,13},{5,12},{6,15},{7,14},{8,1},{9,0},... | collective-permute-start | bytes 98312 | tf_op jit(solution)/shard_map/ppermute | solution.py:33
  33.0 0.7 %collective-permute-start.12 = (f32[64,128]{1,0:T(8,128)S(1)}, f32[64,128]{1,0:T(8,128)S(1)}, u32[]{:S(2)}, u32[]{:S(2)}) collective-permute-start(f32[64,128]{1,0:T(8,128)S(1)} %add.20), channel_id=1, source_target_pairs={{0,13},{1,12},{2,15},{3,14},{4,9},{5,8},{6,11},{7,10},{8,5},{9,4},... | collective-permute-start | bytes 98312 | tf_op jit(solution)/shard_map/ppermute | solution.py:33
  33.7 0.3 collective-permute-done.13
  34.1 1.1 %collective-permute-done.14 = f32[64,128]{1,0:T(8,128)S(1)} collective-permute-done((f32[64,128]{1,0:T(8,128)S(1)}, f32[64,128]{1,0:T(8,128)S(1)}, u32[]{:S(2)}, u32[]{:S(2)}) %collective-permute-start.14) | collective-permute-done | bytes 32800 | tf_op jit(solution)/shard_map/ppermute | solution.py:33
  35.1 2.1 %collective-permute-done.12 = f32[64,128]{1,0:T(8,128)S(1)} collective-permute-done((f32[64,128]{1,0:T(8,128)S(1)}, f32[64,128]{1,0:T(8,128)S(1)}, u32[]{:S(2)}, u32[]{:S(2)}) %collective-permute-start.12) | collective-permute-done | bytes 32800 | tf_op jit(solution)/shard_map/ppermute | solution.py:33
  37.3 2.6 %finish.1 = (f32[64,512]{1,0:T(8,128)}, f32[64,64]{1,0:T(8,128)}) custom-call(f32[64,128]{1,0:T(8,128)S(1)} %add_add_fusion.refs_0_, bf16[192,512]{1,0:T(8,128)(2,1)S(1)} %get-tuple-element.27.refs_1_), custom_call_target="tpu_custom_call" | custom-call | tf_op jit(solution)/shard_map/finish/pallas_call | solution.py:348
  (5 shorter events, 0.1 us)
Async XLA Ops:
  1.5 7.6 %collective-permute-start = (bf16[64,512]{1,0:T(8,128)(2,1)S(1)}, bf16[64,512]{1,0:T(8,128)(2,1)S(1)}, u32[]{:S(2)}, u32[]{:S(2)}) collective-permute-start(bf16[64,512]{1,0:T(8,128)(2,1)S(1)} %get-tuple-element.15), channel_id=1, source_target_pairs={{0,16},{1,17},{2,18},{3,19},{4,20},{5,21},{6,22},{7,23},{8,24},{9,... | collective-permute-start | bytes 196616 | tf_op jit(solution)/shard_map/ppermute | solution.py:33
  5.6 6.5 %collective-permute-start.2 = (bf16[64,512]{1,0:T(8,128)(2,1)S(1)}, bf16[64,512]{1,0:T(8,128)(2,1)S(1)}, u32[]{:S(2)}, u32[]{:S(2)}) collective-permute-start(bf16[64,512]{1,0:T(8,128)(2,1)S(1)} %get-tuple-element.15), channel_id=1, source_target_pairs={{0,8},{1,9},{2,10},{3,11},{4,12},{5,13},{6,14},{7,15},{8,0},{9,1},... | collective-permute-start | bytes 196616 | tf_op jit(solution)/shard_map/ppermute | solution.py:33
  7.2 5.9 %collective-permute-start.1 = (bf16[64,512]{1,0:T(8,128)(2,1)S(1)}, bf16[64,512]{1,0:T(8,128)(2,1)S(1)}, u32[]{:S(2)}, u32[]{:S(2)}) collective-permute-start(bf16[64,512]{1,0:T(8,128)(2,1)S(1)} %get-tuple-element.15), channel_id=1, source_target_pairs={{0,12},{1,13},{2,14},{3,15},{4,8},{5,9},{6,10},{7,11},{8,4},{9,5},... | collective-permute-start | bytes 196616 | tf_op jit(solution)/shard_map/ppermute | solution.py:33
  8.5 6.3 %collective-permute-start.3 = (bf16[64,512]{1,0:T(8,128)(2,1)S(1)}, bf16[64,512]{1,0:T(8,128)(2,1)S(1)}, u32[]{:S(2)}, u32[]{:S(2)}) collective-permute-start(bf16[64,512]{1,0:T(8,128)(2,1)S(1)} %get-tuple-element.15), channel_id=1, source_target_pairs={{0,4},{1,5},{2,6},{3,7},{4,0},{5,1},{6,2},{7,3},{8,12},{9,13},{10,... | collective-permute-start | bytes 196616 | tf_op jit(solution)/shard_map/ppermute | solution.py:33
  9.1 5.8 %collective-permute-start.4 = (bf16[64,512]{1,0:T(8,128)(2,1)S(1)}, bf16[64,512]{1,0:T(8,128)(2,1)S(1)}, u32[]{:S(2)}, u32[]{:S(2)}) collective-permute-start(bf16[64,512]{1,0:T(8,128)(2,1)S(1)} %collective-permute-done), channel_id=1, source_target_pairs={{0,12},{1,13},{2,14},{3,15},{4,8},{5,9},{6,10},{7,11},{8,4},{9,5},... | collective-permute-start | bytes 196616 | tf_op jit(solution)/shard_map/ppermute | solution.py:33
  11.6 4.3 %collective-permute-start.5 = (bf16[64,512]{1,0:T(8,128)(2,1)S(1)}, bf16[64,512]{1,0:T(8,128)(2,1)S(1)}, u32[]{:S(2)}, u32[]{:S(2)}) collective-permute-start(bf16[64,512]{1,0:T(8,128)(2,1)S(1)} %collective-permute-done), channel_id=1, source_target_pairs={{0,8},{1,9},{2,10},{3,11},{4,12},{5,13},{6,14},{7,15},{8,0},{9,1},... | collective-permute-start | bytes 196616 | tf_op jit(solution)/shard_map/ppermute | solution.py:33
  12.0 4.3 %collective-permute-start.6 = (bf16[64,512]{1,0:T(8,128)(2,1)S(1)}, bf16[64,512]{1,0:T(8,128)(2,1)S(1)}, u32[]{:S(2)}, u32[]{:S(2)}) collective-permute-start(bf16[64,512]{1,0:T(8,128)(2,1)S(1)} %collective-permute-done), channel_id=1, source_target_pairs={{0,4},{1,5},{2,6},{3,7},{4,0},{5,1},{6,2},{7,3},{8,12},{9,13},{10,... | collective-permute-start | bytes 196616 | tf_op jit(solution)/shard_map/ppermute | solution.py:33
  13.1 4.7 %collective-permute-start.7 = (bf16[80,512]{1,0:T(8,128)(2,1)S(1)}, bf16[80,512]{1,0:T(8,128)(2,1)S(1)}, u32[]{:S(2)}, u32[]{:S(2)}) collective-permute-start(bf16[80,512]{1,0:T(8,128)(2,1)S(1)} %get-tuple-element.17.refs_0_), channel_id=1, source_target_pairs={{0,3},{1,2},{2,1},{3,0},{4,7},{5,6},{6,5},{7,4},{8,11},{9,10},{10,... | collective-permute-start | bytes 245768 | tf_op jit(solution)/shard_map/ppermute | solution.py:33
  17.8 1.3 %collective-permute-start.8 = (bf16[2,64,512]{2,1,0:T(8,128)(2,1)S(1)}, bf16[2,64,512]{2,1,0:T(8,128)(2,1)S(1)}, u32[]{:S(2)}, u32[]{:S(2)}) collective-permute-start(bf16[2,64,512]{2,1,0:T(8,128)(2,1)S(1)} %get-tuple-element.25), channel_id=1, source_target_pairs={{0,1},{1,0},{2,3},{3,2},{4,5},{5,4},{6,7},{7,6},{8,9},{9,8},{10,11... | collective-permute-start | bytes 393224 | tf_op jit(solution)/shard_map/ppermute | solution.py:33
  19.2 5.5 %collective-permute-start.9 = (bf16[2,64,512]{2,1,0:T(8,128)(2,1)S(1)}, bf16[2,64,512]{2,1,0:T(8,128)(2,1)S(1)}, u32[]{:S(2)}, u32[]{:S(2)}) collective-permute-start(bf16[2,64,512]{2,1,0:T(8,128)(2,1)S(1)} %add_convert_fusion.refs_2_), channel_id=1, source_target_pairs={{0,3},{1,2},{2,1},{3,0},{4,7},{5,6},{6,5},{7,4},{8,11},{9,10},{10,... | collective-permute-start | bytes 393224 | tf_op jit(solution)/shard_map/ppermute | solution.py:33
  25.2 1.3 %collective-permute-start.10 = (f32[64,128]{1,0:T(8,128)S(1)}, f32[64,128]{1,0:T(8,128)S(1)}, u32[]{:S(2)}, u32[]{:S(2)}) collective-permute-start(f32[64,128]{1,0:T(8,128)S(1)} %get-tuple-element.26), channel_id=1, source_target_pairs={{0,1},{1,0},{2,3},{3,2},{4,5},{5,4},{6,7},{7,6},{8,9},{9,8},{10,11... | collective-permute-start | bytes 98312 | tf_op jit(solution)/shard_map/ppermute | solution.py:33
  26.5 4.2 %collective-permute-start.11 = (f32[64,128]{1,0:T(8,128)S(1)}, f32[64,128]{1,0:T(8,128)S(1)}, u32[]{:S(2)}, u32[]{:S(2)}) collective-permute-start(f32[64,128]{1,0:T(8,128)S(1)} %add.19), channel_id=1, source_target_pairs={{0,17},{1,16},{2,19},{3,18},{4,21},{5,20},{6,23},{7,22},{8,25},{9,... | collective-permute-start | bytes 98312 | tf_op jit(solution)/shard_map/ppermute | solution.py:33
  30.7 3.3 %collective-permute-start.13 = (f32[64,128]{1,0:T(8,128)S(1)}, f32[64,128]{1,0:T(8,128)S(1)}, u32[]{:S(2)}, u32[]{:S(2)}) collective-permute-start(f32[64,128]{1,0:T(8,128)S(1)} %add.20), channel_id=1, source_target_pairs={{0,5},{1,4},{2,7},{3,6},{4,1},{5,0},{6,3},{7,2},{8,13},{9,12},{10,... | collective-permute-start | bytes 98312 | tf_op jit(solution)/shard_map/ppermute | solution.py:33
  31.8 3.3 %collective-permute-start.14 = (f32[64,128]{1,0:T(8,128)S(1)}, f32[64,128]{1,0:T(8,128)S(1)}, u32[]{:S(2)}, u32[]{:S(2)}) collective-permute-start(f32[64,128]{1,0:T(8,128)S(1)} %add.20), channel_id=1, source_target_pairs={{0,9},{1,8},{2,11},{3,10},{4,13},{5,12},{6,15},{7,14},{8,1},{9,0},... | collective-permute-start | bytes 98312 | tf_op jit(solution)/shard_map/ppermute | solution.py:33
  33.0 4.2 %collective-permute-start.12 = (f32[64,128]{1,0:T(8,128)S(1)}, f32[64,128]{1,0:T(8,128)S(1)}, u32[]{:S(2)}, u32[]{:S(2)}) collective-permute-start(f32[64,128]{1,0:T(8,128)S(1)} %add.20), channel_id=1, source_target_pairs={{0,13},{1,12},{2,15},{3,14},{4,9},{5,8},{6,11},{7,10},{8,5},{9,4},... | collective-permute-start | bytes 98312 | tf_op jit(solution)/shard_map/ppermute | solution.py:33
